TPU v7x, 256 devices: a whole 4x4x8 slice. The times are simulated.
256 devices in a mesh: section: 16 (over z_hi, x, core), dp: 16 (over z_lo, y).
Axes of the slice: x: 4, y: 4, z: 8 (z_hi: 2, z_lo: 4; z = z_hi * 4 + z_lo), core: 2. Of those that a mesh axis runs over, the one named last changes fastest.
Arguments:
- examples: bfloat16 [2, 2048, 2048], P(None, 'dp'), may hold values from -6 to 6
- arriving: float32 [16, 2048, 2048], P('section', 'dp'), may hold values from -6 to 6
- returning: float32 [16, 2048, 2048], P('section', 'dp'), may hold values from -6 to 6
- stash: bfloat16 [16, 2, 2048, 2048], P('section', None, 'dp'), may hold values from -6 to 6
- plan: int32 [16, 2], P('section'), may hold values from 0 to 1, each once within a row
- forward_expert_routes: int32 [16, 2, 2048, 8], P('section', None, 'dp'), may hold values from 0 to 127, as said below
- backward_expert_routes: int32 [16, 2, 2048, 8], P('section', None, 'dp'), may hold values from 0 to 127, as said below
- input_norm_gain: float32 [16, 2048], P('section'), may hold values from 0.1 to 1.9
- router: bfloat16 [16, 2048, 128], P('section'), may hold values from -0.125 to 0.125
- frozen_gate_weight: bfloat16 [16, 2048, 384], P('section'), may hold values from -0.125 to 0.125
- frozen_up_weight: bfloat16 [16, 2048, 384], P('section'), may hold values from -0.125 to 0.125
- frozen_down_weight: bfloat16 [16, 384, 2048], P('section'), may hold values from -0.3125 to 0.3125
- down_factors: bfloat16 [16, 2048, 64], P('section'), may hold values from -0.125 to 0.125
- up_factors: bfloat16 [16, 2, 32, 384], P('section'), may hold values from -0.5 to 0.5
Outputs:
- next_acts: float32 [16, 2048, 2048], P('section', 'dp')
- next_grads: float32 [16, 2048, 2048], P('section', 'dp')
- grad_a: float32 [16, 2048, 64], P('section', 'dp')
- grad_b: float32 [16, 2, 32, 384], P('section', None, None, 'dp')
Inputs may be any that keep to these rules, and one draw needn't show every extreme that they name: forward_expert_routes[..., 0] is 0 for every token: each section holds expert 0 of its layer. The other 7 entries of a token are distinct numbers from 1 to 127. `backward_expert_routes`: as forward_expert_routes: entry 0 is 0, the rest distinct from 1 to 127. `plan`: each section's row is a permutation of 0 to 1.
All inputs are finite; a program needn't handle non-finite values.
Results may differ from a plain program's by a relative error of at most 0.015.
Values sent between devices are 32-bit elements; how exact they have to be, the bound alone decides.
No kernel may reach another device: no remote copies, remote signals or barrier semaphores. Data moves between devices by JAX's collectives and lax.ppermute only.
A program may use at most 64 MiB of HBM per device.

v0:
```python
import jax
import jax.numpy as jnp
from jax import lax
from jax.sharding import PartitionSpec as P

adapter_scale = 2.0


def shifted(value, axis, steps):
    count = lax.axis_size(axis)
    initial, last = (max(0, -steps), min(count, count - steps))
    return lax.ppermute(value, axis, [(source, source + steps) for source in range(initial, last)])


def cut_along(array, dim, size):
    dims = array.shape
    pieces = array.reshape(*dims[:dim], size, dims[dim] // size, *dims[dim + 1 :])
    return jnp.moveaxis(pieces, dim, 0)


def sent_and_summed(array, axis, dim):
    pieces = cut_along(array, dim, lax.axis_size(axis))
    arrived = lax.all_to_all(pieces, axis, split_axis=0, concat_axis=0, tiled=True)
    return arrived.sum(axis=0)


def apply_layer(inputs, routes, frozen, adapter_down, adapter_up):
    gain_vec, router_w, gate_matrix, up_matrix, down_w = frozen
    mean_square = jnp.mean(inputs * inputs, axis=-1, keepdims=True)
    normalized_input = (inputs * lax.rsqrt(mean_square + 1e-06) * gain_vec).astype(jnp.bfloat16)
    logits = jnp.dot(normalized_input, router_w, preferred_element_type=jnp.float32)
    one_hot = (
        routes[:, :, None] == jnp.arange(router_w.shape[1], dtype=jnp.int32)[None, None, :]
    ).astype(jnp.float32)
    picked = jnp.einsum("tke,te->tk", one_hot, logits)
    scores = jnp.exp(picked)
    weight = scores[:, 0] / jnp.sum(scores, axis=-1)
    factor_rank = adapter_down.shape[1] // 2
    reduced_rank_output = jnp.dot(
        normalized_input, adapter_down.astype(jnp.bfloat16), preferred_element_type=jnp.float32
    ).astype(jnp.bfloat16)
    up_factor_matrix = adapter_up.astype(jnp.bfloat16)
    gate_preactivation = jnp.dot(
        normalized_input, gate_matrix, preferred_element_type=jnp.float32
    ) + adapter_scale * jnp.dot(
        reduced_rank_output[:, :factor_rank],
        up_factor_matrix[0],
        preferred_element_type=jnp.float32,
    )
    up_preactivation = jnp.dot(
        normalized_input, up_matrix, preferred_element_type=jnp.float32
    ) + adapter_scale * jnp.dot(
        reduced_rank_output[:, factor_rank:],
        up_factor_matrix[1],
        preferred_element_type=jnp.float32,
    )
    hidden = (jax.nn.silu(gate_preactivation) * up_preactivation).astype(jnp.bfloat16)
    branch = jnp.dot(hidden, down_w, preferred_element_type=jnp.float32)
    return inputs + weight[:, None] * branch


def normalizer(grad_a, grad_b):
    entries = grad_a.size + grad_b.size
    mean_square = (jnp.sum(grad_a * grad_a) + jnp.sum(grad_b * grad_b)) / entries
    return lax.rsqrt(mean_square + 1e-06)


def example_step(inputs, routes, cotangent, frozen, adapter_down, adapter_up):

    def closed(values, first_a, first_b):
        return apply_layer(values, routes, frozen, first_a, first_b)

    result, pullback = jax.vjp(closed, inputs, adapter_down, adapter_up)
    d_input, grad_a, grad_b = pullback(cotangent)
    factor = normalizer(grad_a, grad_b)
    return (d_input, factor * grad_a, factor * grad_b)


def shards(
    examples,
    arriving,
    returning,
    stash,
    plan,
    forward_expert_routes,
    backward_expert_routes,
    input_norm_gain,
    router,
    frozen_gate_weight,
    frozen_up_weight,
    frozen_down_weight,
    down_factors,
    up_factors,
):
    section_index = lax.axis_index("section")
    section_count = lax.axis_size("section")
    replicas = lax.axis_size("dp")
    is_first = section_index == 0
    is_last = section_index == section_count - 1
    frozen = (
        input_norm_gain[0],
        router[0],
        frozen_gate_weight[0],
        frozen_up_weight[0],
        frozen_down_weight[0],
    )
    adapter_down = down_factors[0].astype(jnp.float32)
    adapter_up = up_factors[0].astype(jnp.float32)
    tick_count = examples.shape[0]
    mean_scale = 1.0 / (tick_count * replicas)
    forward_in = arriving[0]
    backward_in = returning[0]
    total_a = jnp.zeros(adapter_down.shape, jnp.float32)
    total_b = jnp.zeros(adapter_up.shape, jnp.float32)
    share_a = None
    share_b = None
    for tick_index in range(tick_count):
        target = examples[tick_index].astype(jnp.float32)
        source = jnp.where(is_first, target, forward_in)
        routes_now = forward_expert_routes[0, tick_index]
        output = apply_layer(source, routes_now, frozen, adapter_down, adapter_up)
        slot_index = plan[0, tick_index]
        stashed = lax.dynamic_index_in_dim(stash[0], slot_index, 0, keepdims=False).astype(
            jnp.float32
        )
        stashed_routes = lax.dynamic_index_in_dim(
            backward_expert_routes[0], slot_index, 0, keepdims=False
        )
        primal_in = jnp.where(is_last, source, stashed)
        primal_routes = jnp.where(is_last, routes_now, stashed_routes)
        loss_grad = output - target
        incoming = jnp.where(is_last, loss_grad, backward_in)
        d_input, grad_a, grad_b = example_step(
            primal_in, primal_routes, incoming, frozen, adapter_down, adapter_up
        )
        total_a = total_a + grad_a
        total_b = total_b + grad_b
        forward_in = shifted(output, "section", 1)
        backward_in = shifted(d_input, "section", -1)
    share_a, share_b = (
        sent_and_summed(total_a * mean_scale, "dp", 0),
        sent_and_summed(total_b * mean_scale, "dp", 2),
    )
    return (forward_in[None], backward_in[None], share_a[None], share_b[None])


def solution(mesh):
    in_specs = (
        P(None, "dp", None),
        P("section", "dp", None),
        P("section", "dp", None),
        P("section", None, "dp", None),
        P("section", None),
        P("section", None, "dp", None),
        P("section", None, "dp", None),
        P("section", None),
        P("section", None, None),
        P("section", None, None),
        P("section", None, None),
        P("section", None, None),
        P("section", None, None),
        P("section", None, None, None),
    )
    out_specs = (
        P("section", "dp", None),
        P("section", "dp", None),
        P("section", "dp", None),
        P("section", None, None, "dp"),
    )
    return jax.shard_map(shards, mesh=mesh, in_specs=in_specs, out_specs=out_specs, check_vma=False)
```

profile of v0, /device:TPU:39, one launch (start us, length us, event | category | flops | bytes accessed | tf_op | source)
XLA Modules:
  0.0 171.8 jit_solution(1858389020322567810)
XLA Ops:
  0.7 1.4 fusion.245
  3.3 0.7 slice_bitcast_fusion
  4.0 0.7 copy.26
  5.5 2.9 %multiply_reduce_fusion.3 = (f32[128]{0:T(128)S(1)}, f32[128,2048]{1,0:T(8,128)}, f32[128]{0:T(128)S(1)}) fusion(bf16[1,2,128,2048]{3,2,1,0:T(8,128)(2,1)} %param.17, s32[]{:T(128)S(6)} %select_n.88, f32[1,128,2048]{2,1,0:T(8,128)} %param.15, bf16[2,128,2048]{2,1,0:T(8,128)(2,1)} %param.14, pred[]{:T(512)S(6)} %eq.62, pred[]{:T(512)S(6)} %eq.71), kind=kLoop, calls=%fused_computation.123 | loop fusion | flops 2096896 | bytes 3146758 | tf_op jit(solution)/shard_map/jvp()/reduce_sum | solution.py:29
  8.4 1.2 fusion.98
  10.5 1.0 fusion.117
  11.4 0.9 copy.35
  12.4 2.2 %fusion.30 = f32[128,384]{1,0:T(8,128)} fusion(bf16[128,2048]{1,0:T(8,128)(2,1)} %copy-done.22, bf16[1,2048,384]{2,1,0:T(8,128)(2,1)S(1)} %copy-done), kind=kOutput, calls=%fused_computation.44 | convolution fusion | flops 201326592 | bytes 2293760 | tf_op jit(solution)/shard_map/dot_general | solution.py:50
  15.4 0.9 fusion.56
  16.3 3.6 %fusion.1 = f32[128,2048]{1,0:T(8,128)} fusion(bf16[1,384,2048]{2,1,0:T(8,128)(2,1)} %param.25, f32[128,384]{1,0:T(8,128)} %fusion.30, f32[128]{0:T(128)S(1)} %fusion.215, f32[1,128,2048]{2,1,0:T(8,128)} %param.15, pred[]{:T(512)S(6)} %eq.62, bf16[2,128,2048]{2,1,0:T(8,128)(2,1)} %param.14, f32[128,384]{1,0:T(8,128)} %fusion.56, ...), kind=kOutput, calls=%fused_computation.5 | convolution fusion | flops 205914112 | bytes 4620801 | tf_op jit(solution)/shard_map/dot_general | solution.py:58
  19.8 8.5 %collective-permute-start = (f32[128,2048]{1,0:T(8,128)}, f32[128,2048]{1,0:T(8,128)}, u32[]{:S(2)}, u32[]{:S(2)}) collective-permute-start(f32[128,2048]{1,0:T(8,128)} %fusion.1), channel_id=1, source_target_pairs={{0,16},{16,32},{32,48},{48,64},{64,80},{80,96},{96,112},{112,128},... | collective-permute-start | bytes 3145736 | tf_op jit(solution)/shard_map/ppermute | solution.py:12
  29.7 1.3 convolution_convert_fusion.15
  31.0 2.1 %fusion.103 = f32[128,128]{1,0:T(8,128)} fusion(bf16[128,2048]{1,0:T(8,128)(2,1)} %get-tuple-element.12, bf16[1,2048,128]{2,1,0:T(8,128)(2,1)} %param.22), kind=kOutput, calls=%fused_computation.135 | convolution fusion | flops 67108864 | bytes 1114112 | tf_op jit(solution)/shard_map/jvp()/dot_general | solution.py:31
  33.8 0.7 copy.28
  34.5 1.8 %fusion.115 = f32[128,1,8]{2,1,0:T(1,128)} fusion(f32[128,128,1]{1,2,0:T(1,128)} %bitcast.342, s32[128,8]{1,0:T(8,128)} %copy.28), kind=kOutput, calls=%fused_computation.152 | convolution fusion | flops 393216 | bytes 73728 | tf_op jit(solution)/shard_map/jvp(tke,te->tk)/dot_general | solution.py:35
  36.4 0.9 copy.39
  37.3 0.7 copy.29
  38.0 0.7 copy.27
  38.7 1.5 fusion.36
  41.2 10.4 %collective-permute-done = f32[128,2048]{1,0:T(8,128)} collective-permute-done((f32[128,2048]{1,0:T(8,128)}, f32[128,2048]{1,0:T(8,128)}, u32[]{:S(2)}, u32[]{:S(2)}) %collective-permute-start) | collective-permute-done | bytes 1048608 | tf_op jit(solution)/shard_map/ppermute | solution.py:12
  51.7 1.6 fusion.88
  55.0 1.5 convolution_convert_fusion.6
  56.5 1.6 multiply_reduce_fusion.1
  58.5 0.9 fusion.105
  59.4 0.9 convolution_multiply_fusion.8
  60.3 0.9 convolution_multiply_fusion.9
  61.7 0.9 fusion.100
  62.7 0.7 copy.40
  63.4 1.2 fusion.114
  64.6 1.8 %fusion.10 = bf16[128,2048]{1,0:T(8,128)(2,1)S(1)} fusion(bf16[128,2048]{1,0:T(8,128)(2,1)} %convolution_convert_fusion.6, f32[128,384]{1,0:T(8,128)} %copy-done.29, bf16[1,2048,384]{2,1,0:T(8,128)(2,1)S(1)} %copy-done), kind=kOutput, calls=%fused_computation.22 | convolution fusion | flops 201588736 | bytes 2818048 | tf_op jit(solution)/shard_map/transpose(jvp())/dot_general | solution.py:50
  66.8 1.7 multiply_reduce_fusion.7
  69.0 0.8 copy-done.16
  69.8 1.2 add_add_fusion.1
  71.0 1.9 %collective-permute-start.2 = (f32[128,2048]{1,0:T(8,128)}, f32[128,2048]{1,0:T(8,128)}, u32[]{:S(2)}, u32[]{:S(2)}) collective-permute-start(f32[128,2048]{1,0:T(8,128)} %add_add_fusion.1), channel_id=1, source_target_pairs={{16,0},{32,16},{48,32},{64,48},{80,64},{96,80},{112,96},{128,112},... | collective-permute-start | bytes 3145736 | tf_op jit(solution)/shard_map/ppermute | solution.py:12
  73.0 1.0 fusion.118
  73.9 0.9 copy.37
  74.9 2.3 %fusion.57 = f32[128,384]{1,0:T(8,128)} fusion(f32[128,384]{1,0:T(8,128)} %convolution_multiply_fusion.9, bf16[128,2048]{1,0:T(8,128)(2,1)} %copy-done.20, bf16[1,2048,384]{2,1,0:T(8,128)(2,1)S(1)} %copy-done.1), kind=kOutput, calls=%fused_computation.83 | convolution fusion | flops 201375744 | bytes 2490368 | tf_op jit(solution)/shard_map/dot_general | solution.py:43
  77.1 1.0 fusion.111
  78.1 0.9 copy.43
  79.6 4.0 %fusion = f32[128,2048]{1,0:T(8,128)} fusion(bf16[1,384,2048]{2,1,0:T(8,128)(2,1)} %param.25, f32[128,384]{1,0:T(8,128)} %convolution_multiply_fusion.8, bf16[128,2048]{1,0:T(8,128)(2,1)} %copy-done.20, bf16[1,2048,384]{2,1,0:T(8,128)(2,1)S(1)} %copy-done, f32[128]{0:T(128)S(1)} %fusion.216, f32[128,384]{1,0:T(8,128)} %fusion.57, ...), kind=kOutput, calls=%fused_computation.3 | convolution fusion | flops 404045824 | bytes 6685185 | tf_op jit(solution)/shard_map/dot_general | solution.py:58
  83.6 1.1 fusion.85
  86.6 10.6 %collective-permute-start.1 = (f32[128,2048]{1,0:T(8,128)}, f32[128,2048]{1,0:T(8,128)}, u32[]{:S(2)}, u32[]{:S(2)}) collective-permute-start(f32[128,2048]{1,0:T(8,128)} %fusion), channel_id=1, source_target_pairs={{0,16},{16,32},{32,48},{48,64},{64,80},{80,96},{96,112},{112,128},... | collective-permute-start | bytes 3145736 | tf_op jit(solution)/shard_map/ppermute | solution.py:12
  97.2 1.5 fusion.22
  100.2 1.4 fusion.94
  104.6 1.4 convolution_convert_fusion.2
  106.1 1.6 multiply_reduce_fusion.6
  107.7 0.7 fusion.158
  110.0 1.8 %fusion.110 = f32[128,1,128]{2,1,0:T(1,128)} fusion(bf16[128,8,1]{1,2,0:T(2,128)(2,1)S(1)} %copy.44, s32[128,8]{1,0:T(8,128)} %copy.29), kind=kOutput, calls=%fused_computation.146 | convolution fusion | flops 393216 | bytes 71680 | tf_op jit(solution)/shard_map/transpose(jvp(tke,te->tk))/dot_general | solution.py:35
  111.8 1.5 fusion.11
  113.3 1.1 fusion.6
  114.5 1.1 reshape.262
  115.6 1.3 copy.31
  116.9 0.8 reshape.280
  117.7 5.8 %all-to-all-start.1 = ((f32[16,1,1536]{2,1,0:T(1,128)}), f32[16,1,1536]{2,1,0:T(1,128)S(1)}, u32[]{:S(2)}, u32[]{:S(2)}) async-start(f32[16,1,1536]{2,1,0:T(1,128)} %reshape.280), calls=%async_computation.1 | async-start | bytes 196608 | tf_op jit(solution)/shard_map/all_to_all | solution.py:23
  123.6 1.6 multiply_reduce_fusion
  125.3 1.3 add_add_fusion
  126.5 1.9 %collective-permute-start.3 = (f32[128,2048]{1,0:T(8,128)}, f32[128,2048]{1,0:T(8,128)}, u32[]{:S(2)}, u32[]{:S(2)}) collective-permute-start(f32[128,2048]{1,0:T(8,128)} %add_add_fusion), channel_id=1, source_target_pairs={{16,0},{32,16},{48,32},{64,48},{80,64},{96,80},{112,96},{128,112},... | collective-permute-start | bytes 3145736 | tf_op jit(solution)/shard_map/ppermute | solution.py:12
  128.5 0.9 copy_bitcast_fusion
  129.4 6.9 %all-to-all-start = ((f32[16,128,64]{1,2,0:T(8,128)}), f32[16,128,64]{1,2,0:T(8,128)S(1)}, u32[]{:S(2)}, u32[]{:S(2)}) async-start(f32[16,128,64]{1,2,0:T(8,128)} %copy_bitcast_fusion), calls=%async_computation | async-start | bytes 1048576 | tf_op jit(solution)/shard_map/all_to_all | solution.py:23
  136.8 0.9 reduce
  138.7 7.0 %all-to-all-done = f32[16,128,64]{1,2,0:T(8,128)S(1)} async-done(((f32[16,128,64]{1,2,0:T(8,128)}), f32[16,128,64]{1,2,0:T(8,128)S(1)}, u32[]{:S(2)}, u32[]{:S(2)}) %all-to-all-start) | async-done | bytes 524320 | tf_op jit(solution)/shard_map/all_to_all | solution.py:23
  146.3 20.9 %collective-permute-done.3 = f32[128,2048]{1,0:T(8,128)} collective-permute-done((f32[128,2048]{1,0:T(8,128)}, f32[128,2048]{1,0:T(8,128)}, u32[]{:S(2)}, u32[]{:S(2)}) %collective-permute-start.3) | collective-permute-done | bytes 1048608 | tf_op jit(solution)/shard_map/ppermute | solution.py:12
  167.2 2.3 %copy.51 = f32[1,128,2048]{2,1,0:T(8,128)} copy(f32[1,128,2048]{2,1,0:T(8,128)} %bitcast.24) | data formatting | bytes 2097152
  169.5 2.3 %copy.52 = f32[1,128,2048]{2,1,0:T(8,128)} copy(f32[1,128,2048]{2,1,0:T(8,128)} %bitcast.55) | data formatting | bytes 2097152
  (166 shorter events, 14.1 us)
Async XLA Ops:
  0.6 11.7 %copy-start = (bf16[1,2048,384]{2,1,0:T(8,128)(2,1)S(1)}, bf16[1,2048,384]{2,1,0:T(8,128)(2,1)}, u32[]{:S(2)}) copy-start(bf16[1,2048,384]{2,1,0:T(8,128)(2,1)} %param.24) | copy-start | bytes 4718596
  5.4 3.0 %copy-start.17 = (bf16[2,128,2048]{2,1,0:T(8,128)(2,1)S(1)}, bf16[2,128,2048]{2,1,0:T(8,128)(2,1)}, u32[]{:S(2)}) copy-start(bf16[2,128,2048]{2,1,0:T(8,128)(2,1)} %param.14) | copy-start | bytes 3145732
  5.4 3.0 %copy-start.24 = (f32[1,128,2048]{2,1,0:T(8,128)S(1)}, f32[1,128,2048]{2,1,0:T(8,128)}, u32[]{:S(2)}) copy-start(f32[1,128,2048]{2,1,0:T(8,128)} %param.15) | copy-start | bytes 3145732
  5.4 3.0 %copy-start.31 = (bf16[1,2,128,2048]{3,2,1,0:T(8,128)(2,1)S(1)}, bf16[1,2,128,2048]{3,2,1,0:T(8,128)(2,1)}, u32[]{:S(2)}) copy-start(bf16[1,2,128,2048]{3,2,1,0:T(8,128)(2,1)} %param.17) | copy-start | bytes 3145732
  5.4 3.0 %copy-start.38 = (f32[1,2048]{1,0:T(1,128)S(1)}, f32[1,2048]{1,0:T(1,128)}, u32[]{:S(2)}) copy-start(f32[1,2048]{1,0:T(1,128)} %param.21) | copy-start | bytes 24580
  8.4 1.2 copy-start.25
  8.4 1.5 copy-start.4
  9.6 0.8 copy-start.22
  9.6 0.9 copy-start.45
  10.5 4.1 %copy-start.1 = (bf16[1,2048,384]{2,1,0:T(8,128)(2,1)S(1)}, bf16[1,2048,384]{2,1,0:T(8,128)(2,1)}, u32[]{:S(2)}) copy-start(bf16[1,2048,384]{2,1,0:T(8,128)(2,1)} %param.23) | copy-start | bytes 4718596
  12.3 2.3 %copy-start.23 = (bf16[128,2048]{1,0:T(8,128)(2,1)S(1)}, bf16[128,2048]{1,0:T(8,128)(2,1)}, u32[]{:S(2)}) copy-start(bf16[128,2048]{1,0:T(8,128)(2,1)} %copy-done.22) | copy-start | bytes 1572868
  14.6 0.8 copy-start.36
  19.8 13.9 %copy-start.48 = (s32[1,2,128,8]{2,3,1,0:T(8,128)S(1)}, s32[1,2,128,8]{2,3,1,0:T(8,128)}, u32[]{:S(2)}) copy-start(s32[1,2,128,8]{2,3,1,0:T(8,128)} %param.19) | copy-start | bytes 24580
  19.8 13.9 %copy-start.49 = (s32[1,2,128,8]{2,3,1,0:T(8,128)S(1)}, s32[1,2,128,8]{2,3,1,0:T(8,128)}, u32[]{:S(2)}) copy-start(s32[1,2,128,8]{2,3,1,0:T(8,128)} %param.20) | copy-start | bytes 24580
  19.8 31.8 %collective-permute-start = (f32[128,2048]{1,0:T(8,128)}, f32[128,2048]{1,0:T(8,128)}, u32[]{:S(2)}, u32[]{:S(2)}) collective-permute-start(f32[128,2048]{1,0:T(8,128)} %fusion.1), channel_id=1, source_target_pairs={{0,16},{16,32},{32,48},{48,64},{64,80},{80,96},{96,112},{112,128},... | collective-permute-start | bytes 3145736 | tf_op jit(solution)/shard_map/ppermute | solution.py:12
  38.7 1.8 %copy-start.21 = (bf16[128,2048]{1,0:T(8,128)(2,1)S(1)}, bf16[128,2048]{1,0:T(8,128)(2,1)}, u32[]{:S(2)}) copy-start(bf16[128,2048]{1,0:T(8,128)(2,1)} %get-tuple-element.12) | copy-start | bytes 1572868
  40.3 11.4 %copy-start.18 = (bf16[2,128,2048]{2,1,0:T(8,128)(2,1)S(1)}, bf16[2,128,2048]{2,1,0:T(8,128)(2,1)}, u32[]{:S(2)}) copy-start(bf16[2,128,2048]{2,1,0:T(8,128)(2,1)} %param.14) | copy-start | bytes 3145732
  40.3 11.3 %copy-start.26 = (f32[128,2048]{1,0:T(8,128)S(1)}, f32[128,2048]{1,0:T(8,128)}, u32[]{:S(2)}) copy-start(f32[128,2048]{1,0:T(8,128)} %fusion.1) | copy-start | bytes 3145732
  40.3 11.3 %copy-start.37 = (f32[1,128,2048]{2,1,0:T(8,128)S(1)}, f32[1,128,2048]{2,1,0:T(8,128)}, u32[]{:S(2)}) copy-start(f32[1,128,2048]{2,1,0:T(8,128)} %param.16) | copy-start | bytes 3145732
  41.2 12.1 %copy-start.2 = (bf16[1,384,2048]{2,1,0:T(8,128)(2,1)S(1)}, bf16[1,384,2048]{2,1,0:T(8,128)(2,1)}, u32[]{:S(2)}) copy-start(bf16[1,384,2048]{2,1,0:T(8,128)(2,1)} %param.25) | copy-start | bytes 4718596
  53.3 1.2 copy-start.15
  54.6 1.9 %copy-start.28 = (f32[128,384]{1,0:T(8,128)}, f32[128,384]{1,0:T(8,128)S(1)}, u32[]{:S(2)}) copy-start(f32[128,384]{1,0:T(8,128)S(1)} %get-tuple-element.21) | copy-start | bytes 589828
  54.6 1.9 %copy-start.29 = (f32[128,384]{1,0:T(8,128)}, f32[128,384]{1,0:T(8,128)S(1)}, u32[]{:S(2)}) copy-start(f32[128,384]{1,0:T(8,128)S(1)} %get-tuple-element.20) | copy-start | bytes 589828
  54.6 1.9 %copy-start.32 = (bf16[1,2,128,2048]{3,2,1,0:T(8,128)(2,1)S(1)}, bf16[1,2,128,2048]{3,2,1,0:T(8,128)(2,1)}, u32[]{:S(2)}) copy-start(bf16[1,2,128,2048]{3,2,1,0:T(8,128)(2,1)} %param.17) | copy-start | bytes 3145732
  56.5 2.0 %copy-start.5 = (bf16[1,2048,128]{2,1,0:T(8,128)(2,1)S(1)}, bf16[1,2048,128]{2,1,0:T(8,128)(2,1)}, u32[]{:S(2)}) copy-start(bf16[1,2048,128]{2,1,0:T(8,128)(2,1)} %param.22) | copy-start | bytes 1572868
  58.1 3.2 %copy-start.10 = (f32[128,2048]{1,0:T(8,128)}, f32[128,2048]{1,0:T(8,128)S(1)}, u32[]{:S(2)}) copy-start(f32[128,2048]{1,0:T(8,128)S(1)} %get-tuple-element.9) | copy-start | bytes 3145732
  58.2 3.2 %copy-start.20 = (bf16[128,2048]{1,0:T(8,128)(2,1)}, bf16[128,2048]{1,0:T(8,128)(2,1)S(1)}, u32[]{:S(2)}) copy-start(bf16[128,2048]{1,0:T(8,128)(2,1)S(1)} %get-tuple-element.15) | copy-start | bytes 1572868
  58.2 3.2 %copy-start.54 = (f32[128]{0:T(128)}, f32[128]{0:T(128)S(1)}, u32[]{:S(2)}) copy-start(f32[128]{0:T(128)S(1)} %get-tuple-element.8) | copy-start | bytes 1540
  61.2 1.4 copy-start.50
  61.4 1.2 copy-start.8
  61.7 37.7 %copy-start.39 = (bf16[128,64]{0,1:T(8,128)(2,1)}, bf16[128,64]{0,1:T(8,128)(2,1)S(1)}, u32[]{:S(2)}) copy-start(bf16[128,64]{0,1:T(8,128)(2,1)S(1)} %convolution_convert_fusion.14) | copy-start | bytes 49156
  64.6 2.2 %copy-start.12 = (f32[128,2048]{1,0:T(8,128)S(1)}, f32[128,2048]{1,0:T(8,128)}, u32[]{:S(2)}) copy-start(f32[128,2048]{1,0:T(8,128)} %get-tuple-element.11) | copy-start | bytes 3145732
  66.5 2.1 %copy-start.6 = (bf16[1,2048,128]{2,1,0:T(8,128)(2,1)S(1)}, bf16[1,2048,128]{2,1,0:T(8,128)(2,1)}, u32[]{:S(2)}) copy-start(bf16[1,2048,128]{2,1,0:T(8,128)(2,1)} %param.22) | copy-start | bytes 1572868
  68.5 1.2 copy-start.16
  69.8 3.2 %copy-start.42 = (f32[128,128]{1,0:T(8,128)S(1)}, f32[128,128]{1,0:T(8,128)}, u32[]{:S(2)}) copy-start(f32[128,128]{1,0:T(8,128)} %fusion.105) | copy-start | bytes 196612
  69.8 3.2 %copy-start.44 = (s32[128,8]{1,0:T(8,128)S(1)}, s32[128,8]{1,0:T(8,128)}, u32[]{:S(2)}) copy-start(s32[128,8]{1,0:T(8,128)} %copy.27) | copy-start | bytes 12292
  71.0 28.6 %collective-permute-start.2 = (f32[128,2048]{1,0:T(8,128)}, f32[128,2048]{1,0:T(8,128)}, u32[]{:S(2)}, u32[]{:S(2)}) collective-permute-start(f32[128,2048]{1,0:T(8,128)} %add_add_fusion.1), channel_id=1, source_target_pairs={{16,0},{32,16},{48,32},{64,48},{80,64},{96,80},{112,96},{128,112},... | collective-permute-start | bytes 3145736 | tf_op jit(solution)/shard_map/ppermute | solution.py:12
  74.8 2.3 %copy-start.41 = (f32[128,128]{1,0:T(8,128)S(1)}, f32[128,128]{1,0:T(8,128)}, u32[]{:S(2)}) copy-start(f32[128,128]{1,0:T(8,128)} %fusion.100) | copy-start | bytes 196612
  74.8 2.3 %copy-start.43 = (s32[128,8]{1,0:T(8,128)S(1)}, s32[128,8]{1,0:T(8,128)}, u32[]{:S(2)}) copy-start(s32[128,8]{1,0:T(8,128)} %copy.29) | copy-start | bytes 12292
  79.0 0.6 copy-start.46
  86.6 12.3 %copy-start.9 = (bf16[128,2048]{1,0:T(8,128)(2,1)S(1)}, bf16[128,2048]{1,0:T(8,128)(2,1)}, u32[]{:S(2)}) copy-start(bf16[128,2048]{1,0:T(8,128)(2,1)} %copy-done.8) | copy-start | bytes 1572868
  86.6 49.7 %collective-permute-start.1 = (f32[128,2048]{1,0:T(8,128)}, f32[128,2048]{1,0:T(8,128)}, u32[]{:S(2)}, u32[]{:S(2)}) collective-permute-start(f32[128,2048]{1,0:T(8,128)} %fusion), channel_id=1, source_target_pairs={{0,16},{16,32},{32,48},{48,64},{64,80},{80,96},{96,112},{112,128},... | collective-permute-start | bytes 3145736 | tf_op jit(solution)/shard_map/ppermute | solution.py:12
  98.7 1.2 copy-start.19
  98.7 1.5 copy-start.27
  99.6 2.0 %copy-start.3 = (bf16[1,384,2048]{2,1,0:T(8,128)(2,1)S(1)}, bf16[1,384,2048]{2,1,0:T(8,128)(2,1)}, u32[]{:S(2)}) copy-start(bf16[1,384,2048]{2,1,0:T(8,128)(2,1)} %param.25) | copy-start | bytes 4718596
  101.7 2.3 %copy-start.13 = (f32[128,2048]{1,0:T(8,128)}, f32[128,2048]{1,0:T(8,128)S(1)}, u32[]{:S(2)}) copy-start(f32[128,2048]{1,0:T(8,128)S(1)} %fusion.94) | copy-start | bytes 3145732
  103.4 0.8 copy-start.40
  104.0 2.1 %copy-start.30 = (f32[128,384]{1,0:T(8,128)}, f32[128,384]{1,0:T(8,128)S(1)}, u32[]{:S(2)}) copy-start(f32[128,384]{1,0:T(8,128)S(1)} %get-tuple-element.18) | copy-start | bytes 589828
  104.6 5.2 %copy-start.47 = (f32[128,1,8]{0,2,1:T(8,128)S(1)}, f32[128,1,8]{0,2,1:T(8,128)}, u32[]{:S(2)}) copy-start(f32[128,1,8]{0,2,1:T(8,128)} %copy-done.46) | copy-start | bytes 12292
  104.6 5.2 %copy-start.52 = (f32[128,1]{0,1:T(1,128)S(1)}, f32[128,1]{0,1:T(1,128)}, u32[]{:S(2)}) copy-start(f32[128,1]{0,1:T(1,128)} %get-tuple-element.34) | copy-start | bytes 1540
  104.6 5.2 %copy-start.53 = (f32[128]{0:T(128)S(1)}, f32[128]{0:T(128)}, u32[]{:S(2)}) copy-start(f32[128]{0:T(128)} %fusion.219) | copy-start | bytes 1540
  106.1 5.7 %copy-start.35 = (bf16[128,2048]{1,0:T(8,128)(2,1)S(1)}, bf16[128,2048]{1,0:T(8,128)(2,1)}, u32[]{:S(2)}) copy-start(bf16[128,2048]{1,0:T(8,128)(2,1)} %convolution_convert_fusion.2) | copy-start | bytes 1572868
  113.3 10.3 %copy-start.7 = (bf16[1,2048,128]{2,1,0:T(8,128)(2,1)S(1)}, bf16[1,2048,128]{2,1,0:T(8,128)(2,1)}, u32[]{:S(2)}) copy-start(bf16[1,2048,128]{2,1,0:T(8,128)(2,1)} %param.22) | copy-start | bytes 1572868
  113.3 10.3 %copy-start.11 = (f32[128,2048]{1,0:T(8,128)S(1)}, f32[128,2048]{1,0:T(8,128)}, u32[]{:S(2)}) copy-start(f32[128,2048]{1,0:T(8,128)} %copy-done.10) | copy-start | bytes 3145732
  117.7 11.7 %all-to-all-start.1 = ((f32[16,1,1536]{2,1,0:T(1,128)}), f32[16,1,1536]{2,1,0:T(1,128)S(1)}, u32[]{:S(2)}, u32[]{:S(2)}) async-start(f32[16,1,1536]{2,1,0:T(1,128)} %reshape.280), calls=%async_computation.1 | async-start | bytes 196608 | tf_op jit(solution)/shard_map/all_to_all | solution.py:23
  123.6 1.6 copy-start.55
  123.6 1.6 copy-start.14
  123.6 1.6 copy-start.51
  125.2 3.2 %copy-start.33 = (f32[2048,64]{0,1:T(8,128)S(1)}, f32[2048,64]{0,1:T(8,128)}, u32[]{:S(2)}) copy-start(f32[2048,64]{0,1:T(8,128)} %get-tuple-element.47) | copy-start | bytes 1572868
  125.3 3.2 %copy-start.34 = (f32[2048,64]{0,1:T(8,128)S(1)}, f32[2048,64]{0,1:T(8,128)}, u32[]{:S(2)}) copy-start(f32[2048,64]{0,1:T(8,128)} %get-tuple-element.45) | copy-start | bytes 1572868
  126.5 40.7 %collective-permute-start.3 = (f32[128,2048]{1,0:T(8,128)}, f32[128,2048]{1,0:T(8,128)}, u32[]{:S(2)}, u32[]{:S(2)}) collective-permute-start(f32[128,2048]{1,0:T(8,128)} %add_add_fusion), channel_id=1, source_target_pairs={{16,0},{32,16},{48,32},{64,48},{80,64},{96,80},{112,96},{128,112},... | collective-permute-start | bytes 3145736 | tf_op jit(solution)/shard_map/ppermute | solution.py:12
  129.4 16.2 %all-to-all-start = ((f32[16,128,64]{1,2,0:T(8,128)}), f32[16,128,64]{1,2,0:T(8,128)S(1)}, u32[]{:S(2)}, u32[]{:S(2)}) async-start(f32[16,128,64]{1,2,0:T(8,128)} %copy_bitcast_fusion), calls=%async_computation | async-start | bytes 1048576 | tf_op jit(solution)/shard_map/all_to_all | solution.py:23
where the time goes:
time: 173 us; the launch traced here: 172 us
  matrix products  51.7 us (30%)
  waiting for transfers between devices  38.4 us (22%)
  starting transfers between devices  35.6 us (21%)
  local copies, waits for them, and re-layouts  21.4 us (12%)
  other arithmetic  16.6 us (10%)
  between operations  8.07 us (5%)
    ppermute x4, waiting for transfers between devices, shifted(): lax.ppermute(value, axis, [(source, source + steps) for source in range(i...  31.3 us
    ppermute x4, starting transfers between devices, shifted(): lax.ppermute(value, axis, [(source, source + steps) for source in range(i...  22.9 us
    all_to_all x2, starting transfers between devices, sent_and_summed(): lax.all_to_all(pieces, axis, split_axis=0, concat_axis=0, tiled=True)  12.7 us
    dot_general x6, matrix products, apply_layer(): branch = jnp.dot(hidden, down_w, preferred_element_type=jnp.float32)  9.92 us
    unnamed x118, local copies, waits for them, and re-layouts  9.07 us
    dot_general x6, matrix products, apply_layer(): picked = jnp.einsum('tke,te->tk', one_hot, logits)  7.78 us
    dot_general x6, matrix products, apply_layer(): jnp.dot(normalized_input, gate_matrix, preferred_element_type=jnp.float32)  7.6 us
    dot_general x5, matrix products, apply_layer(): jnp.dot(normalized_input, up_matrix, preferred_element_type=jnp.float32)  7.53 us
  transfers between devices with their start and end apart: 6, of which 4 were waited for; matrix products, arithmetic and copies ran while one was open for 28% of the time, Pallas kernels for 0%

commit v1 on v0

v1 whole, which is shorter than its diff:
```python
import functools

import jax
import jax.numpy as jnp
from jax import lax
from jax.experimental import pallas as pl
from jax.experimental.pallas import tpu as pltpu
from jax.sharding import PartitionSpec as P

SCALE = 2.0
EPS = 1e-06
F32 = jnp.float32
BF16 = jnp.bfloat16
ANY = pl.BlockSpec(memory_space=pl.ANY)
SMEM = pl.BlockSpec(memory_space=pltpu.SMEM)
VMEM = pl.BlockSpec(memory_space=pltpu.VMEM)


def nn(a, b):
    return jnp.dot(a, b, preferred_element_type=F32)


def nt(a, b):
    return lax.dot_general(a, b, (((1,), (1,)), ((), ())), preferred_element_type=F32)


class Loads:
    def __init__(self, sems):
        self.sems = sems
        self.used = 0

    def start(self, source, target):
        copy = pltpu.make_async_copy(source, target, self.sems.at[self.used])
        self.used += 1
        copy.start()
        return copy


def primal(x, routes_t, gain, copies, router, a_t, gate, up, factors):
    rstd = lax.rsqrt(jnp.mean(x * x, axis=-1, keepdims=True) + EPS)
    normed = (x * rstd * gain).astype(BF16)
    copies["router"].wait()
    logits = nn(normed, router[...])
    experts = logits.shape[1]
    expert = lax.broadcasted_iota(jnp.int32, (experts, routes_t.shape[1]), 0)
    named = jnp.zeros(expert.shape, F32)
    for k in range(routes_t.shape[0]):
        named = jnp.where(routes_t[k : k + 1, :] == expert, 1.0, named)
    scores = jnp.where(named.T > 0.5, jnp.exp(logits), 0.0)
    share = scores / jnp.sum(scores, axis=-1, keepdims=True)
    weight = share[:, 0:1]
    copies["a"].wait()
    low = nt(normed, a_t[...]).astype(BF16)
    rank = low.shape[1] // 2
    copies["b"].wait()
    copies["gate"].wait()
    gate_pre = nn(normed, gate[...]) + SCALE * nn(low[:, :rank], factors[0])
    copies["up"].wait()
    up_pre = nn(normed, up[...]) + SCALE * nn(low[:, rank:], factors[1])
    return rstd, normed, share, weight, low, gate_pre, up_pre


def forward_kernel(
    tick,
    arriving,
    examples,
    routes_t,
    gain,
    router_h,
    a_h,
    gate_h,
    up_h,
    b_h,
    down_h,
    out,
    x_s,
    ex_s,
    r_s,
    gain_s,
    router,
    a_t,
    gate,
    up,
    factors,
    down,
    sems,
):
    first = lax.axis_index("section") == 0
    loads = Loads(sems)
    x_copy = pltpu.make_async_copy(arriving, x_s, sems.at[0])
    ex_copy = pltpu.make_async_copy(examples.at[tick], ex_s, sems.at[1])
    loads.used = 2

    @pl.when(first)
    def _():
        ex_copy.start()

    @pl.when(jnp.logical_not(first))
    def _():
        x_copy.start()

    copies = {}
    copies["gain"] = loads.start(gain, gain_s)
    copies["routes"] = loads.start(routes_t.at[tick], r_s)
    copies["router"] = loads.start(router_h, router)
    copies["a"] = loads.start(a_h, a_t)
    copies["b"] = loads.start(b_h, factors)
    copies["gate"] = loads.start(gate_h, gate)
    copies["up"] = loads.start(up_h, up)
    copies["down"] = loads.start(down_h, down)

    @pl.when(first)
    def _():
        ex_copy.wait()
        x_s[...] = ex_s[...].astype(F32)

    @pl.when(jnp.logical_not(first))
    def _():
        x_copy.wait()

    copies["gain"].wait()
    copies["routes"].wait()
    x = x_s[...]
    _, _, _, weight, _, gate_pre, up_pre = primal(
        x, r_s[...], gain_s[...], copies, router, a_t, gate, up, factors
    )
    hidden = (gate_pre * jax.nn.sigmoid(gate_pre) * up_pre).astype(BF16)
    copies["down"].wait()
    out[...] = x_s[...] + weight * nn(hidden, down[...])


def backward_kernel(
    tick,
    last_tick,
    mean_scale,
    plan,
    arriving,
    returning,
    examples,
    stash,
    fwd_routes_t,
    bwd_routes_t,
    gain,
    router_h,
    a_h,
    gate_h,
    up_h,
    b_h,
    down_h,
    *rest,
):
    if last_tick:
        ga_in, gb_in, dx, packed = rest[:4]
        rest = rest[4:]
    else:
        dx, ga_out, gb_out = rest[:3]
        rest = rest[3:]
    x_s, g_s, ex_s, st_s, r_s, gain_s, router, a_t, gate, up, factors, down, sems = rest
    last = lax.axis_index("section") == lax.axis_size("section") - 1
    other = jnp.logical_not(last)
    slot = plan[0, tick]
    loads = Loads(sems)
    loads.used = 6
    x_copy = pltpu.make_async_copy(arriving, x_s, sems.at[0])
    ex_copy = pltpu.make_async_copy(examples.at[tick], ex_s, sems.at[1])
    fr_copy = pltpu.make_async_copy(fwd_routes_t.at[tick], r_s, sems.at[2])
    st_copy = pltpu.make_async_copy(stash.at[slot], st_s, sems.at[3])
    g_copy = pltpu.make_async_copy(returning, g_s, sems.at[4])
    br_copy = pltpu.make_async_copy(bwd_routes_t.at[slot], r_s, sems.at[5])

    @pl.when(last)
    def _():
        x_copy.start()
        fr_copy.start()
        ex_copy.start()

    @pl.when(other)
    def _():
        st_copy.start()
        br_copy.start()

    copies = {}
    copies["gain"] = loads.start(gain, gain_s)
    copies["router"] = loads.start(router_h, router)
    copies["a"] = loads.start(a_h, a_t)
    copies["b"] = loads.start(b_h, factors)
    copies["gate"] = loads.start(gate_h, gate)
    copies["up"] = loads.start(up_h, up)
    copies["down"] = loads.start(down_h, down)

    @pl.when(other)
    def _():
        g_copy.start()
        st_copy.wait()
        br_copy.wait()
        x_s[...] = st_s[...].astype(F32)

    @pl.when(last)
    def _():
        x_copy.wait()
        fr_copy.wait()

    copies["gain"].wait()
    rstd, normed, share, weight, low, gate_pre, up_pre = primal(
        x_s[...], r_s[...], gain_s[...], copies, router, a_t, gate, up, factors
    )
    sig = jax.nn.sigmoid(gate_pre)
    silu = gate_pre * sig
    hidden = (silu * up_pre).astype(BF16)
    copies["down"].wait()

    @pl.when(last)
    def _():
        ex_copy.wait()
        g_s[...] = x_s[...] + weight * nn(hidden, down[...]) - ex_s[...].astype(F32)

    @pl.when(other)
    def _():
        g_copy.wait()

    back = nt(g_s[...].astype(BF16), down[...])
    d_weight = jnp.sum(hidden.astype(F32) * back, axis=-1, keepdims=True)
    lead = (lax.broadcasted_iota(jnp.int32, share.shape, 1) == 0).astype(F32)
    d_logits = ((d_weight * weight) * (lead - share)).astype(BF16)
    d_hidden = (weight * back).astype(BF16).astype(F32)
    d_gate = (d_hidden * up_pre * (sig * (1.0 + gate_pre * (1.0 - sig)))).astype(BF16)
    d_up = (d_hidden * silu).astype(BF16)
    d_low_f = SCALE * jnp.concatenate([nt(d_gate, factors[0]), nt(d_up, factors[1])], axis=1)
    d_low = d_low_f.astype(BF16)
    d_normed = (
        nt(d_logits, router[...])
        + nn(d_low, a_t[...])
        + nt(d_gate, gate[...])
        + nt(d_up, up[...])
    )
    scaled = d_normed * gain_s[...]
    x = x_s[...]
    along = jnp.mean(scaled * x, axis=-1, keepdims=True) * (rstd * rstd)
    dx[...] = g_s[...] + rstd * (scaled - x * along)

    rank = low.shape[1] // 2
    ga = nn(d_low_f.T.astype(BF16), normed)
    low_t = low.astype(F32).T.astype(BF16)
    gb = SCALE * jnp.concatenate([nn(low_t[:rank], d_gate), nn(low_t[rank:], d_up)], axis=0)
    entries = ga.size + gb.size
    square = (jnp.sum(ga * ga) + jnp.sum(gb * gb)) / entries
    factor = lax.rsqrt(square + EPS) * mean_scale
    if not last_tick:
        ga_out[...] = factor * ga
        gb_out[...] = factor * gb
        return
    ga = ga_in[...] + factor * ga
    gb_t = (gb_in[...] + factor * gb).T
    ys, zs = packed.shape[:2]
    width = ga.shape[1] // (ys * zs)
    rows = gb_t.shape[0] // (ys * zs)
    tall = ga.shape[0]
    half = rows // 2
    for y in range(ys):
        for z in range(zs):
            p = z * ys + y
            packed[y, z, :tall, :] = ga[:, p * width : (p + 1) * width]
            packed[y, z, tall : tall + half, :tall] = gb_t[p * rows : p * rows + half]
            packed[y, z, tall : tall + half, tall:] = gb_t[p * rows + half : (p + 1) * rows]
            packed[y, z, tall + half :, :] = jnp.zeros((packed.shape[2] - tall - half, width), F32)


def sum_kernel(parts, total):
    total[...] = jnp.sum(parts[...], axis=0)


def final_kernel(tall, half, parts, ga, gb):
    total = jnp.sum(parts[...], axis=0)
    ga[...] = total[:tall]
    rank = gb.shape[2]
    for side in range(2):
        for part in range(2):
            lane = part * tall + side * rank
            gb[side, part * half : (part + 1) * half, :] = total[
                tall : tall + half, lane : lane + rank
            ]


def shifted(value, axis, steps):
    count = lax.axis_size(axis)
    initial, last = (max(0, -steps), min(count, count - steps))
    return lax.ppermute(value, axis, [(source, source + steps) for source in range(initial, last)])


def shards(
    y_size,
    examples,
    arriving,
    returning,
    stash,
    plan,
    forward_expert_routes,
    backward_expert_routes,
    input_norm_gain,
    router,
    frozen_gate_weight,
    frozen_up_weight,
    frozen_down_weight,
    down_factors,
    up_factors,
):
    replicas = lax.axis_size("dp")
    z_size = replicas // y_size
    ticks, tokens, width = examples.shape
    mean_scale = 1.0 / (ticks * replicas)
    gain, router, gate, up, down = (
        input_norm_gain,
        router[0],
        frozen_gate_weight[0],
        frozen_up_weight[0],
        frozen_down_weight[0],
    )
    a_t = down_factors[0].T
    b = up_factors[0]
    stash = stash[0]
    fwd_routes_t = jnp.swapaxes(forward_expert_routes[0], 1, 2)
    bwd_routes_t = jnp.swapaxes(backward_expert_routes[0], 1, 2)
    topk = fwd_routes_t.shape[1]
    hidden_units = gate.shape[1]
    columns = a_t.shape[0]
    weights = (gain, router, a_t, gate, up, b, down)
    weight_scratch = [pltpu.VMEM(w.shape, w.dtype) for w in weights]
    activation = jax.ShapeDtypeStruct((tokens, width), F32)
    params = pltpu.CompilerParams(vmem_limit_bytes=40 << 20)
    primal_flops = 2 * tokens * width * (router.shape[1] + columns + 2 * hidden_units)
    down_flops = 2 * tokens * width * hidden_units
    weight_bytes = sum(w.size * w.dtype.itemsize for w in weights)

    def forward(tick, source):
        return pl.pallas_call(
            functools.partial(forward_kernel, tick),
            out_shape=activation,
            in_specs=[ANY] * (3 + len(weights)),
            out_specs=VMEM,
            scratch_shapes=[
                pltpu.VMEM((tokens, width), F32),
                pltpu.VMEM((tokens, width), BF16),
                pltpu.VMEM((topk, tokens), jnp.int32),
                *weight_scratch,
                pltpu.SemaphoreType.DMA((10,)),
            ],
            compiler_params=params,
            cost_estimate=pl.CostEstimate(
                flops=primal_flops + down_flops,
                bytes_accessed=weight_bytes + 8 * tokens * width,
                transcendentals=0,
            ),
            name="forward_%d" % tick,
        )(source, examples, fwd_routes_t, *weights)

    gb_rows = columns
    rows_each = hidden_units // replicas
    packed_rows = columns + -(-(rows_each // 2) // 8) * 8

    def backward(tick, source, returned, sums):
        last_tick = tick == ticks - 1
        if last_tick:
            outs = (
                activation,
                jax.ShapeDtypeStruct((y_size, z_size, packed_rows, width // replicas), F32),
            )
        else:
            outs = (
                activation,
                jax.ShapeDtypeStruct((columns, width), F32),
                jax.ShapeDtypeStruct((gb_rows, hidden_units), F32),
            )
        return pl.pallas_call(
            functools.partial(backward_kernel, tick, last_tick, mean_scale),
            out_shape=outs,
            in_specs=[SMEM] + [ANY] * (6 + len(weights)) + [VMEM] * len(sums),
            out_specs=tuple(VMEM for _ in outs),
            scratch_shapes=[
                pltpu.VMEM((tokens, width), F32),
                pltpu.VMEM((tokens, width), F32),
                pltpu.VMEM((tokens, width), BF16),
                pltpu.VMEM((tokens, width), BF16),
                pltpu.VMEM((topk, tokens), jnp.int32),
                *weight_scratch,
                pltpu.SemaphoreType.DMA((13,)),
            ],
            compiler_params=params,
            cost_estimate=pl.CostEstimate(
                flops=2 * primal_flops + down_flops,
                bytes_accessed=weight_bytes + 10 * tokens * width,
                transcendentals=0,
            ),
            name="backward_%d" % tick,
        )(plan, source, returned, examples, stash, fwd_routes_t, bwd_routes_t, *weights, *sums)

    forward_in = arriving[0]
    backward_in = returning[0]
    sums = ()
    for tick in range(ticks):
        output = forward(tick, forward_in)
        source = forward_in
        forward_in = shifted(output, "section", 1)
        d_input, *sums = backward(tick, source, backward_in, sums)
        backward_in = shifted(d_input, "section", -1)
    packed = sums[0]
    y_groups = [[z * y_size + y for y in range(y_size)] for z in range(z_size)]
    z_groups = [[z * y_size + y for z in range(z_size)] for y in range(y_size)]
    parts = lax.all_to_all(packed, "dp", 0, 0, axis_index_groups=y_groups, tiled=True)
    parts = pl.pallas_call(
        sum_kernel,
        out_shape=jax.ShapeDtypeStruct(parts.shape[1:], F32),
        in_specs=[VMEM],
        out_specs=VMEM,
        name="sum_y",
    )(parts)
    parts = lax.all_to_all(parts, "dp", 0, 0, axis_index_groups=z_groups, tiled=True)
    share_a, share_b = pl.pallas_call(
        functools.partial(final_kernel, columns, rows_each // 2),
        out_shape=(
            jax.ShapeDtypeStruct((columns, width // replicas), F32),
            jax.ShapeDtypeStruct((2, rows_each, columns // 2), F32),
        ),
        in_specs=[VMEM],
        out_specs=(VMEM, VMEM),
        name="sum_z",
    )(parts)
    return (
        forward_in[None],
        backward_in[None],
        share_a.T[None],
        jnp.swapaxes(share_b, 1, 2)[None],
    )


def solution(mesh):
    in_specs = (
        P(None, "dp", None),
        P("section", "dp", None),
        P("section", "dp", None),
        P("section", None, "dp", None),
        P("section", None),
        P("section", None, "dp", None),
        P("section", None, "dp", None),
        P("section", None),
        P("section", None, None),
        P("section", None, None),
        P("section", None, None),
        P("section", None, None),
        P("section", None, None),
        P("section", None, None, None),
    )
    out_specs = (
        P("section", "dp", None),
        P("section", "dp", None),
        P("section", "dp", None),
        P("section", None, None, "dp"),
    )
    return jax.shard_map(
        functools.partial(shards, 4),
        mesh=mesh,
        in_specs=in_specs,
        out_specs=out_specs,
        check_vma=False,
    )
```

time: 173 us -> 110 us (0.64)
  matrix products: 51.7 us -> 0 us
  Pallas kernels: 0 us -> 22.1 us
  blocking collectives: 0 us -> 19.7 us
  other arithmetic: 16.6 us -> 0 us
  waiting for transfers between devices: 38.4 us -> 23 us
  starting transfers between devices: 35.6 us -> 24.2 us
  between operations: 8.07 us -> 0.79 us
  local copies, waits for them, and re-layouts: 21.4 us -> 18 us
    dot_general x52 -> x0, matrix products: 51.7 us -> none  [the longest x6 9.92 us: apply_layer(): branch = jnp.dot(hidden, down_w, preferred_element_type=jnp.float32)]
    pallas_call x0 -> x6, Pallas kernels: none -> 22.1 us  [the longest x2 12.4 us: backward(): pl.pallas_call(functools.partial(backward_kernel, tick, last_tick, mean_s...]
    all_to_all x0 -> x2, blocking collectives: none -> 19.7 us  [the longest x1 11.7 us: shards(): lax.all_to_all(packed, 'dp', 0, 0, axis_index_groups=y_groups, tiled=True)]
    all_to_all x2 -> x0, starting transfers between devices: 12.7 us -> none  [sent_and_summed(): lax.all_to_all(pieces, axis, split_axis=0, concat_axis=0, tiled=True)]
    unnamed x118 -> x42, local copies, waits for them, and re-layouts: 9.07 us -> 18 us
    ppermute x4, waiting for transfers between devices: 31.3 us -> 23 us  [shifted(): lax.ppermute(value, axis, [(source, source + steps) for source in range(i...]
    all_to_all x2 -> x0, waiting for transfers between devices: 7.13 us -> none  [sent_and_summed(): lax.all_to_all(pieces, axis, split_axis=0, concat_axis=0, tiled=True)]
    reduce_sum x6 -> x0, other arithmetic: 6.63 us -> none  [the longest x2 4.54 us: apply_layer(): mean_square = jnp.mean(inputs * inputs, axis=-1, keepdims=True)]
  transfers between devices with their start and end apart: 6 -> 4, of which waited for: 4 -> 2; matrix products, arithmetic and copies ran while one was open for 28% -> 0% of each run, Pallas kernels for 0% -> 9%
where the time goes in v1:
time: 110 us; the launch traced here: 108 us
  starting transfers between devices  24.2 us (22%)
  waiting for transfers between devices  23 us (21%)
  Pallas kernels  22.1 us (20%)
  blocking collectives  19.7 us (18%)
  local copies, waits for them, and re-layouts  18 us (16%)
    ppermute x4, starting transfers between devices, shifted(): lax.ppermute(value, axis, [(source, source + steps) for source in range(i...  24.2 us
    ppermute x4, waiting for transfers between devices, shifted(): lax.ppermute(value, axis, [(source, source + steps) for source in range(i...  23 us
    unnamed x42, local copies, waits for them, and re-layouts  18 us
    pallas_call x2, Pallas kernels, backward(): pl.pallas_call(functools.partial(backward_kernel, tick, last_tick, mean_s...  12.4 us
    all_to_all x1, blocking collectives, shards(): lax.all_to_all(packed, 'dp', 0, 0, axis_index_groups=y_groups, tiled=True)  11.7 us
    all_to_all x1, blocking collectives, shards(): lax.all_to_all(parts, 'dp', 0, 0, axis_index_groups=z_groups, tiled=True)  7.97 us
    pallas_call x2, Pallas kernels, forward(): pl.pallas_call(functools.partial(forward_kernel, tick), out_shape=activat...  6.34 us
  transfers between devices with their start and end apart: 4, of which 2 were waited for; matrix products, arithmetic and copies ran while one was open for 0% of the time, Pallas kernels for 9%

profile of v1, /device:TPU:39, one launch (start us, length us, event | category | flops | bytes accessed | tf_op | source)
XLA Modules:
  0.0 107.7 jit_solution(697320455786867884)
XLA Ops:
  0.6 0.0 copy-start
  0.6 1.4 %copy-done = bf16[1,2048,384]{2,1,0:T(8,128)(2,1)S(1)} copy-done((bf16[1,2048,384]{2,1,0:T(8,128)(2,1)S(1)}, bf16[1,2048,384]{2,1,0:T(8,128)(2,1)}, u32[]{:S(2)}) %copy-start) | copy-done | bytes 1572888
  2.0 0.0 copy-start.2
  2.0 1.4 %copy-done.2 = bf16[1,2048,384]{2,1,0:T(8,128)(2,1)S(1)} copy-done((bf16[1,2048,384]{2,1,0:T(8,128)(2,1)S(1)}, bf16[1,2048,384]{2,1,0:T(8,128)(2,1)}, u32[]{:S(2)}) %copy-start.2) | copy-done | bytes 1572888
  3.5 0.0 copy-start.4
  3.5 1.4 %copy-done.4 = bf16[1,384,2048]{2,1,0:T(8,128)(2,1)S(1)} copy-done((bf16[1,384,2048]{2,1,0:T(8,128)(2,1)S(1)}, bf16[1,384,2048]{2,1,0:T(8,128)(2,1)}, u32[]{:S(2)}) %copy-start.4) | copy-done | bytes 1572888
  4.9 0.0 copy-start.6
  4.9 1.2 %copy-done.6 = bf16[2,128,2048]{2,1,0:T(8,128)(2,1)S(1)} copy-done((bf16[2,128,2048]{2,1,0:T(8,128)(2,1)S(1)}, bf16[2,128,2048]{2,1,0:T(8,128)(2,1)}, u32[]{:S(2)}) %copy-start.6) | copy-done | bytes 1048600
  6.1 0.0 copy-start.8
  6.1 1.0 copy-done.8
  7.1 0.0 copy-start.9
  7.1 0.9 copy-done.9
  8.1 0.0 copy-start.10
  8.1 1.2 %copy-done.10 = f32[1,128,2048]{2,1,0:T(8,128)S(1)} copy-done((f32[1,128,2048]{2,1,0:T(8,128)S(1)}, f32[1,128,2048]{2,1,0:T(8,128)}, u32[]{:S(2)}) %copy-start.10) | copy-done | bytes 1048600
  9.3 0.0 copy-start.11
  9.3 1.2 %copy-done.11 = bf16[1,2,128,2048]{3,2,1,0:T(8,128)(2,1)S(1)} copy-done((bf16[1,2,128,2048]{3,2,1,0:T(8,128)(2,1)S(1)}, bf16[1,2,128,2048]{3,2,1,0:T(8,128)(2,1)}, u32[]{:S(2)}) %copy-start.11) | copy-done | bytes 1048600
  10.5 0.0 copy-start.13
  10.5 1.2 %copy-done.13 = f32[1,128,2048]{2,1,0:T(8,128)S(1)} copy-done((f32[1,128,2048]{2,1,0:T(8,128)S(1)}, f32[1,128,2048]{2,1,0:T(8,128)}, u32[]{:S(2)}) %copy-start.13) | copy-done | bytes 1048600
  11.8 0.0 copy-start.14
  11.8 0.8 copy-done.14
  12.6 0.0 copy-start.15
  12.6 0.7 copy-done.15
  13.3 0.0 copy-start.16
  13.3 0.7 copy-done.16
  13.9 0.0 copy-start.17
  14.0 0.7 copy-done.17
  14.6 0.0 copy-start.18
  14.6 0.7 copy-done.18
  15.3 6.1 %backward_0.1 = (f32[128,2048]{1,0:T(8,128)S(1)}, f32[64,2048]{1,0:T(8,128)S(1)}, f32[64,384]{1,0:T(8,128)S(1)}) custom-call(s32[1,2]{1,0:T(1,128)S(1)} %copy-done.18, f32[128,2048]{1,0:T(8,128)S(1)} %bitcast.45, f32[128,2048]{1,0:T(8,128)S(1)} %bitcast.49, bf16[2,128,2048]{2,1,0:T(8,128)(2,1)S(1)} %copy-done.6, bf16[2,128,2048]{2,1,0:T(8,128)(2,1)S(1)} %bitcast.47, ...), custom_call_target="tpu_custom_call" | custom-call | flops 1207959552 | bytes 8183808 | tf_op jit(solution)/shard_map/backward_0/pallas_call | solution.py:373
  21.4 0.0 copy-start.1
  21.4 0.0 copy-start.3
  21.4 0.0 copy-start.5
  21.5 0.0 copy-start.7
  21.5 0.0 copy-start.12
  21.5 0.0 copy-start.19
  21.5 2.9 %collective-permute-start.2 = (f32[128,2048]{1,0:T(8,128)S(1)}, f32[128,2048]{1,0:T(8,128)S(1)}, u32[]{:S(2)}, u32[]{:S(2)}) collective-permute-start(f32[128,2048]{1,0:T(8,128)S(1)} %get-tuple-element.11), channel_id=1, source_target_pairs={{16,0},{32,16},{48,32},{64,48},{80,64},{96,80},{112,96},{128,112},... | collective-permute-start | bytes 3145736 | tf_op jit(solution)/shard_map/ppermute | solution.py:287
  24.4 3.2 %forward_0.1 = f32[128,2048]{1,0:T(8,128)S(1)} custom-call(f32[128,2048]{1,0:T(8,128)S(1)} %bitcast.46, bf16[2,128,2048]{2,1,0:T(8,128)(2,1)S(1)} %copy-done.6, s32[2,8,128]{2,1,0:T(8,128)S(1)} %bitcast.55, f32[1,2048]{1,0:T(1,128)S(1)} %copy-done.16, bf16[2048,128]{1,0:T(8,128)(2,1)S(1)} %bitcast.38, bf16[64,2048]{1,0:T(8,128)(2,1)S(1)} %bitcast.42, ...), custom_call_target="tpu_custom_call" | custom-call | flops 704643072 | bytes 7659520 | tf_op jit(solution)/shard_map/forward_0/pallas_call | solution.py:335
  27.5 9.0 %collective-permute-start = (f32[128,2048]{1,0:T(8,128)S(1)}, f32[128,2048]{1,0:T(8,128)S(1)}, u32[]{:S(2)}, u32[]{:S(2)}) collective-permute-start(f32[128,2048]{1,0:T(8,128)S(1)} %forward_0.1), channel_id=1, source_target_pairs={{0,16},{16,32},{32,48},{48,64},{64,80},{80,96},{96,112},{112,128},... | collective-permute-start | bytes 3145736 | tf_op jit(solution)/shard_map/ppermute | solution.py:287
  36.5 18.6 %collective-permute-done.2.returning = f32[128,2048]{1,0:T(8,128)S(1)} collective-permute-done((f32[128,2048]{1,0:T(8,128)S(1)}, f32[128,2048]{1,0:T(8,128)S(1)}, u32[]{:S(2)}, u32[]{:S(2)}) %collective-permute-start.2) | collective-permute-done | bytes 1048608 | tf_op jit(solution)/shard_map/ppermute | solution.py:287
  55.1 4.4 %collective-permute-done.arriving = f32[128,2048]{1,0:T(8,128)S(1)} collective-permute-done((f32[128,2048]{1,0:T(8,128)S(1)}, f32[128,2048]{1,0:T(8,128)S(1)}, u32[]{:S(2)}, u32[]{:S(2)}) %collective-permute-start) | collective-permute-done | bytes 1048608 | tf_op jit(solution)/shard_map/ppermute | solution.py:287
  59.5 0.0 copy-done.1
  59.5 0.0 copy-done.3
  59.5 0.0 copy-done.5
  59.5 0.0 copy-done.7
  59.5 0.0 copy-done.12
  59.5 0.0 copy-done.19
  59.5 6.3 %backward_1.1 = (f32[128,2048]{1,0:T(8,128)S(1)}, f32[4,4,80,128]{3,2,1,0:T(8,128)S(1)}) custom-call(s32[1,2]{1,0:T(1,128)S(1)} %copy-done.19, f32[128,2048]{1,0:T(8,128)S(1)} %collective-permute-done.arriving, f32[128,2048]{1,0:T(8,128)S(1)} %collective-permute-done.2.returning, bf16[2,128,2048]{2,1,0:T(8,128)(2,1)S(1)} %copy-done.7, ...), custom_call_target="tpu_custom_call" | custom-call | flops 1207959552 | bytes 8183808 | tf_op jit(solution)/shard_map/backward_1/pallas_call | solution.py:373
  65.8 1.9 %collective-permute-start.3 = (f32[128,2048]{1,0:T(8,128)S(1)}, f32[128,2048]{1,0:T(8,128)S(1)}, u32[]{:S(2)}, u32[]{:S(2)}) collective-permute-start(f32[128,2048]{1,0:T(8,128)S(1)} %get-tuple-element.14), channel_id=1, source_target_pairs={{16,0},{32,16},{48,32},{64,48},{80,64},{96,80},{112,96},{128,112},... | collective-permute-start | bytes 3145736 | tf_op jit(solution)/shard_map/ppermute | solution.py:287
  67.7 3.2 %forward_1.1 = f32[128,2048]{1,0:T(8,128)S(1)} custom-call(f32[128,2048]{1,0:T(8,128)S(1)} %collective-permute-done.arriving, bf16[2,128,2048]{2,1,0:T(8,128)(2,1)S(1)} %copy-done.7, s32[2,8,128]{2,1,0:T(8,128)S(1)} %bitcast.57, f32[1,2048]{1,0:T(1,128)S(1)} %copy-done.16, bf16[2048,128]{1,0:T(8,128)(2,1)S(1)} %bitcast.40, bf16[64,2048]{1,0:T(8,128)(2,1)S(1)} %bitcast.44, ...), custom_call_target="tpu_custom_call" | custom-call | flops 704643072 | bytes 7659520 | tf_op jit(solution)/shard_map/forward_1/pallas_call | solution.py:335
  70.9 10.4 %collective-permute-start.1 = (f32[128,2048]{1,0:T(8,128)S(1)}, f32[128,2048]{1,0:T(8,128)}, u32[]{:S(2)}, u32[]{:S(2)}) collective-permute-start(f32[128,2048]{1,0:T(8,128)S(1)} %forward_1.1), channel_id=1, source_target_pairs={{0,16},{16,32},{32,48},{48,64},{64,80},{80,96},{96,112},{112,128},... | collective-permute-start | bytes 3145736 | tf_op jit(solution)/shard_map/ppermute | solution.py:287
  81.3 11.7 %all_to_all.10.parts = f32[4,4,80,128]{3,2,1,0:T(8,128)} all-to-all(f32[4,4,80,128]{3,2,1,0:T(8,128)S(1)} %get-tuple-element.15), channel_id=1, replica_groups={{0,1,2,3},{4,5,6,7},{8,9,10,11},{12,13,14,15},{16,17,18,19},{20,21,22,2..., dimensions={0} | all-to-all | bytes 1310720 | tf_op jit(solution)/shard_map/all_to_all | solution.py:408
  93.1 1.8 %sum_y.1 = f32[4,80,128]{2,1,0:T(8,128)} custom-call(f32[4,4,80,128]{3,2,1,0:T(8,128)} %all_to_all.10.parts), custom_call_target="tpu_custom_call" | custom-call | tf_op jit(solution)/shard_map/sum_y/pallas_call | solution.py:409
  94.8 8.0 %all_to_all.11.parts = f32[4,80,128]{2,1,0:T(8,128)} all-to-all(f32[4,80,128]{2,1,0:T(8,128)} %sum_y.1), channel_id=1, replica_groups={{0,4,8,12},{1,5,9,13},{2,6,10,14},{3,7,11,15},{16,20,24,28},{17,21,25,2..., dimensions={0} | all-to-all | bytes 327680 | tf_op jit(solution)/shard_map/all_to_all | solution.py:416
  102.8 1.6 %sum_z.1 = (f32[64,128]{1,0:T(8,128)}, f32[2,24,32]{2,1,0:T(8,128)}) custom-call(f32[4,80,128]{2,1,0:T(8,128)} %all_to_all.11.parts), custom_call_target="tpu_custom_call" | custom-call | tf_op jit(solution)/shard_map/sum_z/pallas_call | solution.py:417
  104.4 0.0 collective-permute-done.3
  104.4 0.0 collective-permute-done.1
  104.4 2.3 %copy.20 = f32[1,128,2048]{2,1,0:T(8,128)} copy(f32[1,128,2048]{2,1,0:T(8,128)} %bitcast.10) | data formatting | bytes 2097152
  106.7 1.0 copy.21
Async XLA Ops:
  0.6 1.4 %copy-start = (bf16[1,2048,384]{2,1,0:T(8,128)(2,1)S(1)}, bf16[1,2048,384]{2,1,0:T(8,128)(2,1)}, u32[]{:S(2)}) copy-start(bf16[1,2048,384]{2,1,0:T(8,128)(2,1)} %param.23) | copy-start | bytes 4718596
  2.0 1.4 %copy-start.2 = (bf16[1,2048,384]{2,1,0:T(8,128)(2,1)S(1)}, bf16[1,2048,384]{2,1,0:T(8,128)(2,1)}, u32[]{:S(2)}) copy-start(bf16[1,2048,384]{2,1,0:T(8,128)(2,1)} %param.24) | copy-start | bytes 4718596
  3.5 1.4 %copy-start.4 = (bf16[1,384,2048]{2,1,0:T(8,128)(2,1)S(1)}, bf16[1,384,2048]{2,1,0:T(8,128)(2,1)}, u32[]{:S(2)}) copy-start(bf16[1,384,2048]{2,1,0:T(8,128)(2,1)} %param.25) | copy-start | bytes 4718596
  4.9 1.2 %copy-start.6 = (bf16[2,128,2048]{2,1,0:T(8,128)(2,1)S(1)}, bf16[2,128,2048]{2,1,0:T(8,128)(2,1)}, u32[]{:S(2)}) copy-start(bf16[2,128,2048]{2,1,0:T(8,128)(2,1)} %examples.7) | copy-start | bytes 3145732
  6.1 1.0 copy-start.8
  7.1 0.9 copy-start.9
  8.1 1.2 %copy-start.10 = (f32[1,128,2048]{2,1,0:T(8,128)S(1)}, f32[1,128,2048]{2,1,0:T(8,128)}, u32[]{:S(2)}) copy-start(f32[1,128,2048]{2,1,0:T(8,128)} %param.15) | copy-start | bytes 3145732
  9.3 1.2 %copy-start.11 = (bf16[1,2,128,2048]{3,2,1,0:T(8,128)(2,1)S(1)}, bf16[1,2,128,2048]{3,2,1,0:T(8,128)(2,1)}, u32[]{:S(2)}) copy-start(bf16[1,2,128,2048]{3,2,1,0:T(8,128)(2,1)} %param.17) | copy-start | bytes 3145732
  10.5 1.2 %copy-start.13 = (f32[1,128,2048]{2,1,0:T(8,128)S(1)}, f32[1,128,2048]{2,1,0:T(8,128)}, u32[]{:S(2)}) copy-start(f32[1,128,2048]{2,1,0:T(8,128)} %param.16) | copy-start | bytes 3145732
  11.8 0.8 copy-start.14
  12.6 0.7 copy-start.15
  13.3 0.7 copy-start.16
  13.9 0.7 copy-start.17
  14.6 0.7 copy-start.18
  21.4 38.1 %copy-start.1 = (bf16[1,2048,384]{2,1,0:T(8,128)(2,1)S(1)}, bf16[1,2048,384]{2,1,0:T(8,128)(2,1)}, u32[]{:S(2)}) copy-start(bf16[1,2048,384]{2,1,0:T(8,128)(2,1)} %param.23) | copy-start | bytes 4718596
  21.4 38.1 %copy-start.3 = (bf16[1,2048,384]{2,1,0:T(8,128)(2,1)S(1)}, bf16[1,2048,384]{2,1,0:T(8,128)(2,1)}, u32[]{:S(2)}) copy-start(bf16[1,2048,384]{2,1,0:T(8,128)(2,1)} %param.24) | copy-start | bytes 4718596
  21.4 38.1 %copy-start.5 = (bf16[1,384,2048]{2,1,0:T(8,128)(2,1)S(1)}, bf16[1,384,2048]{2,1,0:T(8,128)(2,1)}, u32[]{:S(2)}) copy-start(bf16[1,384,2048]{2,1,0:T(8,128)(2,1)} %param.25) | copy-start | bytes 4718596
  21.5 38.0 %copy-start.7 = (bf16[2,128,2048]{2,1,0:T(8,128)(2,1)S(1)}, bf16[2,128,2048]{2,1,0:T(8,128)(2,1)}, u32[]{:S(2)}) copy-start(bf16[2,128,2048]{2,1,0:T(8,128)(2,1)} %examples.7) | copy-start | bytes 3145732
  21.5 38.0 %copy-start.12 = (bf16[1,2,128,2048]{3,2,1,0:T(8,128)(2,1)S(1)}, bf16[1,2,128,2048]{3,2,1,0:T(8,128)(2,1)}, u32[]{:S(2)}) copy-start(bf16[1,2,128,2048]{3,2,1,0:T(8,128)(2,1)} %param.17) | copy-start | bytes 3145732
  21.5 38.0 %copy-start.19 = (s32[1,2]{1,0:T(1,128)S(1)}, s32[1,2]{1,0:T(1,128)}, u32[]{:S(2)}) copy-start(s32[1,2]{1,0:T(1,128)} %plan.3) | copy-start | bytes 28
  21.5 33.6 %collective-permute-start.2 = (f32[128,2048]{1,0:T(8,128)S(1)}, f32[128,2048]{1,0:T(8,128)S(1)}, u32[]{:S(2)}, u32[]{:S(2)}) collective-permute-start(f32[128,2048]{1,0:T(8,128)S(1)} %get-tuple-element.11), channel_id=1, source_target_pairs={{16,0},{32,16},{48,32},{64,48},{80,64},{96,80},{112,96},{128,112},... | collective-permute-start | bytes 3145736 | tf_op jit(solution)/shard_map/ppermute | solution.py:287
  27.5 32.0 %collective-permute-start = (f32[128,2048]{1,0:T(8,128)S(1)}, f32[128,2048]{1,0:T(8,128)S(1)}, u32[]{:S(2)}, u32[]{:S(2)}) collective-permute-start(f32[128,2048]{1,0:T(8,128)S(1)} %forward_0.1), channel_id=1, source_target_pairs={{0,16},{16,32},{32,48},{48,64},{64,80},{80,96},{96,112},{112,128},... | collective-permute-start | bytes 3145736 | tf_op jit(solution)/shard_map/ppermute | solution.py:287
  65.8 38.6 %collective-permute-start.3 = (f32[128,2048]{1,0:T(8,128)S(1)}, f32[128,2048]{1,0:T(8,128)S(1)}, u32[]{:S(2)}, u32[]{:S(2)}) collective-permute-start(f32[128,2048]{1,0:T(8,128)S(1)} %get-tuple-element.14), channel_id=1, source_target_pairs={{16,0},{32,16},{48,32},{64,48},{80,64},{96,80},{112,96},{128,112},... | collective-permute-start | bytes 3145736 | tf_op jit(solution)/shard_map/ppermute | solution.py:287
  70.9 33.5 %collective-permute-start.1 = (f32[128,2048]{1,0:T(8,128)S(1)}, f32[128,2048]{1,0:T(8,128)}, u32[]{:S(2)}, u32[]{:S(2)}) collective-permute-start(f32[128,2048]{1,0:T(8,128)S(1)} %forward_1.1), channel_id=1, source_target_pairs={{0,16},{16,32},{32,48},{48,64},{64,80},{80,96},{96,112},{112,128},... | collective-permute-start | bytes 3145736 | tf_op jit(solution)/shard_map/ppermute | solution.py:287

commit v2 on v0

v2 whole, which is shorter than its diff:
```python
import functools

import jax
import jax.numpy as jnp
from jax import lax
from jax.experimental import pallas as pl
from jax.experimental.pallas import tpu as pltpu
from jax.sharding import PartitionSpec as P


SCALE = 2.0
EPS = 1e-06
F32 = jnp.float32
BF16 = jnp.bfloat16
ANY = pl.BlockSpec(memory_space=pl.ANY)
SMEM = pl.BlockSpec(memory_space=pltpu.SMEM)
VMEM = pl.BlockSpec(memory_space=pltpu.VMEM)


def nn(a, b):
    return jnp.dot(a, b, preferred_element_type=F32)


def nt(a, b):
    return lax.dot_general(a, b, (((1,), (1,)), ((), ())), preferred_element_type=F32)


def primal(x, routes_t, gain, copies, router, a_t, gate, up, factors):
    rstd = lax.rsqrt(jnp.mean(x * x, axis=-1, keepdims=True) + EPS)
    normed = (x * rstd * gain).astype(BF16)
    copies["router"].wait()
    logits = nn(normed, router[...])
    experts = logits.shape[1]
    expert = lax.broadcasted_iota(jnp.int32, (experts, routes_t.shape[1]), 0)
    named = jnp.zeros(expert.shape, F32)
    for k in range(routes_t.shape[0]):
        named = jnp.where(routes_t[k : k + 1, :] == expert, 1.0, named)
    scores = jnp.where(named.T > 0.5, jnp.exp(logits), 0.0)
    share = scores / jnp.sum(scores, axis=-1, keepdims=True)
    weight = share[:, 0:1]
    copies["a"].wait()
    low = nt(normed, a_t[...]).astype(BF16)
    rank = low.shape[1] // 2
    copies["b"].wait()
    copies["gate"].wait()
    gate_pre = nn(normed, gate[...]) + SCALE * nn(low[:, :rank], factors[0])
    copies["up"].wait()
    up_pre = nn(normed, up[...]) + SCALE * nn(low[:, rank:], factors[1])
    return rstd, normed, share, weight, low, gate_pre, up_pre


def when_all(*predicates):
    both = predicates[0]
    for predicate in predicates[1:]:
        both = jnp.logical_and(both, predicate)
    return pl.when(both)


def position():
    section = lax.axis_index("section")
    odd = lax.rem(section, 2) == 1
    return (
        odd,
        jnp.logical_not(odd),
        section == 0,
        section == lax.axis_size("section") - 1,
    )


def fetch(cases, x_s, b_s, r_s, sems):
    moves = []
    for predicates, source, routes in cases:
        narrow = source.dtype == BF16
        x_copy = pltpu.make_async_copy(source, b_s if narrow else x_s, sems.at[0])
        r_copy = pltpu.make_async_copy(routes, r_s, sems.at[1])
        moves.append((predicates, narrow, x_copy, r_copy))

        @when_all(*predicates)
        def _(x_copy=x_copy, r_copy=r_copy):
            x_copy.start()
            r_copy.start()

    def wait():
        for predicates, narrow, x_copy, r_copy in moves:

            @when_all(*predicates)
            def _(narrow=narrow, x_copy=x_copy, r_copy=r_copy):
                x_copy.wait()
                r_copy.wait()
                if narrow:
                    x_s[...] = b_s[...].astype(F32)

    return wait


def fetch_cotangent(cases, g_s, e_s, sems):
    moves = []
    for predicates, source, target in cases:
        g_copy = pltpu.make_async_copy(source, g_s, sems.at[2])
        t_copy = None if target is None else pltpu.make_async_copy(target, e_s, sems.at[3])
        moves.append((predicates, g_copy, t_copy))

        @when_all(*predicates)
        def _(g_copy=g_copy, t_copy=t_copy):
            g_copy.start()
            if t_copy is not None:
                t_copy.start()

    def wait():
        for predicates, g_copy, t_copy in moves:

            @when_all(*predicates)
            def _(g_copy=g_copy, t_copy=t_copy):
                g_copy.wait()
                if t_copy is not None:
                    t_copy.wait()
                    g_s[...] = g_s[...] - e_s[...].astype(F32)

    return wait


NAMES = ("gain", "router", "a", "gate", "up", "b", "down")


def fetch_weights(hbm, weights, order, sems):
    copies = {}
    for name in order:
        i = NAMES.index(name)
        copies[name] = pltpu.make_async_copy(hbm[i], weights[i], sems.at[4 + i])
        copies[name].start()
    return copies


def primal_of(x, routes, copies, weights):
    gain_s, router, a_t, gate, up, factors = weights[:6]
    copies["gain"].wait()
    return primal(x, routes, gain_s[...], copies, router, a_t, gate, up, factors)


def output_of(x_s, values, down):
    _, _, _, weight, _, gate_pre, up_pre = values
    hidden = (gate_pre * jax.nn.sigmoid(gate_pre) * up_pre).astype(BF16)
    return x_s[...] + weight * nn(hidden, down[...])


def gradients(x_s, g_s, saved, weights):
    gain_s, router, a_t, gate, up, factors, down = weights
    rstd, normed, share, weight, low, gate_pre, up_pre = saved
    sig = jax.nn.sigmoid(gate_pre)
    silu = gate_pre * sig
    hidden = (silu * up_pre).astype(BF16)
    back = nt(g_s[...].astype(BF16), down[...])
    d_weight = jnp.sum(hidden.astype(F32) * back, axis=-1, keepdims=True)
    lead = (lax.broadcasted_iota(jnp.int32, share.shape, 1) == 0).astype(F32)
    d_logits = ((d_weight * weight) * (lead - share)).astype(BF16)
    d_hidden = (weight * back).astype(BF16).astype(F32)
    d_gate = (d_hidden * up_pre * (sig * (1.0 + gate_pre * (1.0 - sig)))).astype(BF16)
    d_up = (d_hidden * silu).astype(BF16)
    d_low_f = SCALE * jnp.concatenate([nt(d_gate, factors[0]), nt(d_up, factors[1])], axis=1)
    d_normed = (
        nt(d_gate, gate[...])
        + nt(d_up, up[...])
        + nt(d_logits, router[...])
        + nn(d_low_f.astype(BF16), a_t[...])
    )
    scaled = d_normed * gain_s[...]
    x = x_s[...]
    along = jnp.mean(scaled * x, axis=-1, keepdims=True) * (rstd * rstd)
    dx = g_s[...] + rstd * (scaled - x * along)
    rank = low.shape[1] // 2
    ga = nn(d_low_f.T.astype(BF16), normed)
    low_t = low.astype(F32).T.astype(BF16)
    gb = SCALE * jnp.concatenate([nn(low_t[:rank], d_gate), nn(low_t[rank:], d_up)], axis=0)
    return dx, ga, gb


def normalizer(ga, gb, mean_scale):
    square = (jnp.sum(ga * ga) + jnp.sum(gb * gb)) / (ga.size + gb.size)
    return lax.rsqrt(square + EPS) * mean_scale


def pack(packed, ga, gb):
    gb_t = gb.T
    ys = packed.shape[0]
    width = packed.shape[2]
    zs = ga.shape[1] // (ys * width)
    size = packed.shape[1] // zs
    rows = gb_t.shape[0] // (ys * zs)
    tall = ga.shape[0]
    half = rows // 2
    for y in range(ys):
        for z in range(zs):
            p = z * ys + y
            at = z * size
            packed[y, at : at + tall, :] = ga[:, p * width : (p + 1) * width]
            packed[y, at + tall : at + tall + half, :tall] = gb_t[p * rows : p * rows + half]
            packed[y, at + tall : at + tall + half, tall:] = gb_t[p * rows + half : (p + 1) * rows]
            packed[y, at + tall + half : at + size, :] = jnp.zeros((size - tall - half, width), F32)


FIRST_ORDER = ("gain", "router", "a", "b", "gate", "up", "down")


def step_kernel(
    tick,
    odd_forward,
    mean_scale,
    plan,
    act_in,
    grad_in,
    output,
    examples,
    stash,
    fwd_routes_t,
    bwd_routes_t,
    *rest,
):
    hbm, rest = rest[:7], rest[7:]
    if tick:
        ga_in, gb_in, sent, packed, *rest = rest
    else:
        sent, ga_out, gb_out, *rest = rest
    x_s, g_s, b_s, e_s, r_s, *weights, sems = rest
    odd, even, first, last = position()
    slot = plan[0, tick]
    stored = (stash.at[slot], bwd_routes_t.at[slot])
    mine = fwd_routes_t.at[tick]
    if odd_forward:
        ahead, behind = odd, even
        cases = [((odd,), act_in, mine), ((even,), *stored)]
        g_cases = [((even,), grad_in, None)]
    else:
        ahead, behind = even, odd
        cases = [
            ((first,), examples.at[tick], mine),
            ((even, jnp.logical_not(first)), act_in, mine),
            ((last,), act_in, mine),
            ((odd, jnp.logical_not(last)), *stored),
        ]
        g_cases = [
            ((last,), output, examples.at[tick]),
            ((odd, jnp.logical_not(last)), grad_in, None),
        ]
    x_wait = fetch(cases, x_s, b_s, r_s, sems)
    copies = fetch_weights(hbm, weights, FIRST_ORDER, sems)
    g_wait = fetch_cotangent(g_cases, g_s, e_s, sems)
    x_wait()
    values = primal_of(x_s[...], r_s[...], copies, weights)
    copies["down"].wait()

    @pl.when(ahead)
    def _():
        sent[...] = output_of(x_s, values, weights[6])

    @pl.when(behind)
    def _():
        g_wait()
        dx, ga, gb = gradients(x_s, g_s, values, weights)
        sent[...] = dx
        factor = normalizer(ga, gb, mean_scale)
        if tick:
            pack(packed, ga_in[...] + factor * ga, gb_in[...] + factor * gb)
        else:
            ga_out[...] = factor * ga
            gb_out[...] = factor * gb


def recompute_kernel(tick, plan, act_in, after, examples, stash, fwd_routes_t, bwd_routes_t, *rest):
    hbm, outs, (b_s, r_s, *weights, sems) = rest[:6], rest[6:13], rest[13:]
    x_o, rstd_o, normed_o, share_o, low_o, gate_o, up_o = outs
    odd, _, _, last = position()

    @pl.when(odd)
    def _():
        slot = plan[0, tick]
        cases = [
            ((last,), act_in, fwd_routes_t.at[tick]),
            ((jnp.logical_not(last),), stash.at[slot], bwd_routes_t.at[slot]),
        ]
        x_wait = fetch(cases, x_o, b_s, r_s, sems)
        copies = fetch_weights(hbm, weights, FIRST_ORDER[:6], sems)
        x_wait()
        values = primal_of(x_o[...], r_s[...], copies, weights)
        rstd, normed, share, _, low, gate_pre, up_pre = values
        rstd_o[...] = jnp.broadcast_to(rstd, rstd_o.shape)
        normed_o[...] = normed
        share_o[...] = share
        low_o[...] = low
        gate_o[...] = gate_pre
        up_o[...] = up_pre


def last_kernel(
    tick,
    mean_scale,
    arrived,
    output,
    examples,
    fwd_routes_t,
    packed_in,
    ga_in,
    gb_in,
    *rest,
):
    saved, rest = rest[:7], rest[7:]
    hbm, (sent, packed, x_s, g_s, b_s, e_s, r_s, *weights, sems) = rest[:7], rest[7:]
    x_o, rstd_o, normed_o, share_o, low_o, gate_o, up_o = saved
    odd, even, first, last = position()

    @pl.when(even)
    def _():
        keep = pltpu.make_async_copy(packed_in, packed, sems.at[2])
        keep.start()
        mine = fwd_routes_t.at[tick]
        cases = [
            ((first,), examples.at[tick], mine),
            ((jnp.logical_not(first),), arrived, mine),
        ]
        x_wait = fetch(cases, x_s, b_s, r_s, sems)
        copies = fetch_weights(hbm, weights, FIRST_ORDER, sems)
        x_wait()
        values = primal_of(x_s[...], r_s[...], copies, weights)
        copies["down"].wait()
        sent[...] = output_of(x_s, values, weights[6])
        keep.wait()

    @pl.when(odd)
    def _():
        g_cases = [
            ((last,), output, examples.at[tick]),
            ((jnp.logical_not(last),), arrived, None),
        ]
        g_wait = fetch_cotangent(g_cases, g_s, e_s, sems)
        copies = fetch_weights(hbm, weights, ("down", "b", "gate", "up", "router", "a", "gain"), sems)
        share = share_o[...]
        values = (
            rstd_o[:, 0:1],
            normed_o[...],
            share,
            share[:, 0:1],
            low_o[...],
            gate_o[...],
            up_o[...],
        )
        for name in NAMES:
            copies[name].wait()
        g_wait()
        dx, ga, gb = gradients(x_o, g_s, values, weights)
        sent[...] = dx
        factor = normalizer(ga, gb, mean_scale)
        pack(packed, ga_in[...] + factor * ga, gb_in[...] + factor * gb)


def sum_kernel(parts, total):
    total[...] = jnp.sum(parts[...], axis=0).reshape(total.shape)


def final_kernel(tall, half, pieces, parts, slow, fast, ga, gb, acts_o, grads_o, slow_s, fast_s, sems):
    odd, even, _, _ = position()
    rows = slow.shape[0] // pieces
    moves = []
    for source, stage, low, high in (
        (slow, slow_s, acts_o, grads_o),
        (fast, fast_s, grads_o, acts_o),
    ):
        for i in range(pieces):
            at = pl.ds(i * rows, rows)
            k = 2 * len(moves)
            move_in = pltpu.make_async_copy(source.at[at], stage.at[at], sems.at[k])
            move_even = pltpu.make_async_copy(stage.at[at], low.at[at], sems.at[k + 1])
            move_odd = pltpu.make_async_copy(stage.at[at], high.at[at], sems.at[k + 1])
            moves.append((move_in, move_even, move_odd))
    for move_in, _, _ in moves:
        move_in.start()
    for move_in, move_even, move_odd in moves:
        move_in.wait()
        pl.when(even)(move_even.start)
        pl.when(odd)(move_odd.start)
    total = jnp.sum(parts[...], axis=0)
    ga[...] = total[:tall]
    rank = gb.shape[2]
    for side in range(2):
        for part in range(2):
            lane = part * tall + side * rank
            gb[side, part * half : (part + 1) * half, :] = total[
                tall : tall + half, lane : lane + rank
            ]
    for _, move_even, move_odd in moves:
        pl.when(even)(move_even.wait)
        pl.when(odd)(move_odd.wait)


def swaps(first, count):
    pairs = []
    for s in range(first, count - 1, 2):
        pairs += [(s, s + 1), (s + 1, s)]
    return pairs


def shards(
    y_size,
    examples,
    arriving,
    returning,
    stash,
    plan,
    forward_expert_routes,
    backward_expert_routes,
    input_norm_gain,
    router,
    frozen_gate_weight,
    frozen_up_weight,
    frozen_down_weight,
    down_factors,
    up_factors,
):
    replicas = lax.axis_size("dp")
    z_size = replicas // y_size
    ticks, tokens, width = examples.shape
    mean_scale = 1.0 / (ticks * replicas)
    gain, router, gate, up, down = (
        input_norm_gain,
        router[0],
        frozen_gate_weight[0],
        frozen_up_weight[0],
        frozen_down_weight[0],
    )
    a_t = down_factors[0].T
    b = up_factors[0]
    stash = stash[0]
    fwd_routes_t = jnp.swapaxes(forward_expert_routes[0], 1, 2)
    bwd_routes_t = jnp.swapaxes(backward_expert_routes[0], 1, 2)
    topk = fwd_routes_t.shape[1]
    hidden_units = gate.shape[1]
    columns = a_t.shape[0]
    weights = (gain, router, a_t, gate, up, b, down)
    scratch = [pltpu.VMEM(w.shape, w.dtype) for w in weights]
    x_scratch = pltpu.VMEM((tokens, width), F32)
    b_scratch = pltpu.VMEM((tokens, width), BF16)
    r_scratch = pltpu.VMEM((topk, tokens), jnp.int32)
    semaphores = pltpu.SemaphoreType.DMA((12,))
    activation = jax.ShapeDtypeStruct((tokens, width), F32)
    adapter_a = jax.ShapeDtypeStruct((columns, width), F32)
    adapter_b = jax.ShapeDtypeStruct((columns, hidden_units), F32)
    whole = pltpu.CompilerParams()
    some = pltpu.CompilerParams(vmem_limit_bytes=24 << 20)
    few = pltpu.CompilerParams(vmem_limit_bytes=8 << 20)
    primal_flops = 2 * tokens * width * (router.shape[1] + columns + 2 * hidden_units)
    down_flops = 2 * tokens * width * hidden_units
    weight_bytes = sum(w.size * w.dtype.itemsize for w in weights)

    def cost(flops):
        return pl.CostEstimate(
            flops=flops, bytes_accessed=weight_bytes + 8 * tokens * width, transcendentals=0
        )

    sections = lax.axis_size("section")
    near = swaps(0, sections)
    far = swaps(1, sections)
    rows_each = hidden_units // replicas
    size = columns + -(-(rows_each // 2) // 8) * 8
    share_width = width // replicas
    packed_shape = jax.ShapeDtypeStruct((y_size, z_size * size, share_width), F32)
    work = [x_scratch, x_scratch, b_scratch, b_scratch, r_scratch, *scratch, semaphores]

    def step(tick, odd_forward, acts, grads, output, sums, params):
        outs = (activation, packed_shape) if tick else (activation, adapter_a, adapter_b)
        return pl.pallas_call(
            functools.partial(step_kernel, tick, odd_forward, mean_scale),
            out_shape=outs,
            in_specs=[SMEM] + [ANY] * (7 + len(weights)) + [VMEM] * len(sums),
            out_specs=(VMEM,) * len(outs),
            scratch_shapes=work,
            compiler_params=params,
            cost_estimate=cost(2 * primal_flops + down_flops),
        )(plan, acts, grads, output, examples, stash, fwd_routes_t, bwd_routes_t, *weights, *sums)

    start = arriving[0]
    back = returning[0]
    sent, *even_sums = step(0, True, start, back, start, (), whole)
    slow_0 = lax.ppermute(sent, "section", far)
    sent, *odd_sums = step(0, False, start, back, sent, (), whole)
    fast_0 = lax.ppermute(sent, "section", near)
    ahead, packed = step(1, True, fast_0, fast_0, fast_0, even_sums, whole)
    slow_1 = lax.ppermute(ahead, "section", far)
    saved = pl.pallas_call(
        functools.partial(recompute_kernel, 1),
        out_shape=(
            activation,
            jax.ShapeDtypeStruct((tokens, 128), F32),
            jax.ShapeDtypeStruct((tokens, width), BF16),
            jax.ShapeDtypeStruct((tokens, router.shape[1]), F32),
            jax.ShapeDtypeStruct((tokens, columns), BF16),
            jax.ShapeDtypeStruct((tokens, hidden_units), F32),
            jax.ShapeDtypeStruct((tokens, hidden_units), F32),
        ),
        in_specs=[SMEM] + [ANY] * (6 + len(weights) - 1),
        out_specs=(VMEM,) * 7,
        scratch_shapes=[b_scratch, r_scratch, *scratch[:-1], semaphores],
        compiler_params=some,
        cost_estimate=cost(primal_flops),
        name="recompute_1",
    )(plan, fast_0, ahead, examples, stash, fwd_routes_t, bwd_routes_t, *weights[:-1])
    sent, packed = pl.pallas_call(
        functools.partial(last_kernel, 1, mean_scale),
        out_shape=(activation, packed_shape),
        in_specs=[ANY] * 5 + [VMEM] * 2 + [VMEM] * len(saved) + [ANY] * len(weights),
        out_specs=(VMEM,) * 2,
        scratch_shapes=work,
        compiler_params=some,
        cost_estimate=cost(primal_flops + down_flops),
        name="step_1b",
    )(slow_0, ahead, examples, fwd_routes_t, packed, *odd_sums, *saved, *weights)
    fast_1 = lax.ppermute(sent, "section", near)
    y_groups = [[z * y_size + y for y in range(y_size)] for z in range(z_size)]
    z_groups = [[z * y_size + y for z in range(z_size)] for y in range(y_size)]
    parts = lax.all_to_all(packed, "dp", 0, 0, axis_index_groups=y_groups, tiled=True)
    parts = pl.pallas_call(
        sum_kernel,
        out_shape=jax.ShapeDtypeStruct((z_size, size, share_width), F32),
        in_specs=[VMEM],
        out_specs=VMEM,
        compiler_params=few,
        name="sum_y",
    )(parts)
    parts = lax.all_to_all(parts, "dp", 0, 0, axis_index_groups=z_groups, tiled=True)
    pieces = 4
    share_a, share_b, next_acts, next_grads = pl.pallas_call(
        functools.partial(final_kernel, columns, rows_each // 2, pieces),
        out_shape=(
            jax.ShapeDtypeStruct((columns, share_width), F32),
            jax.ShapeDtypeStruct((2, rows_each, columns // 2), F32),
            activation,
            activation,
        ),
        in_specs=[VMEM, ANY, ANY],
        out_specs=(VMEM, VMEM, ANY, ANY),
        scratch_shapes=[x_scratch, x_scratch, pltpu.SemaphoreType.DMA((4 * pieces,))],
        compiler_params=few,
        name="sum_z",
    )(parts, slow_1, fast_1)
    return (
        next_acts[None],
        next_grads[None],
        share_a.T[None],
        jnp.swapaxes(share_b, 1, 2)[None],
    )


def solution(mesh):
    in_specs = (
        P(None, "dp", None),
        P("section", "dp", None),
        P("section", "dp", None),
        P("section", None, "dp", None),
        P("section", None),
        P("section", None, "dp", None),
        P("section", None, "dp", None),
        P("section", None),
        P("section", None, None),
        P("section", None, None),
        P("section", None, None),
        P("section", None, None),
        P("section", None, None),
        P("section", None, None, None),
    )
    out_specs = (
        P("section", "dp", None),
        P("section", "dp", None),
        P("section", "dp", None),
        P("section", None, None, "dp"),
    )

    def body(*args):
        return shards(4, *args)

    return jax.shard_map(
        body, mesh=mesh, in_specs=in_specs, out_specs=out_specs, check_vma=False
    )
```

time: 173 us -> 84 us (0.49)
  matrix products: 51.7 us -> 0 us
  Pallas kernels: 0 us -> 29.8 us
  waiting for transfers between devices: 38.4 us -> 8.93 us
  blocking collectives: 0 us -> 19.2 us
  starting transfers between devices: 35.6 us -> 16.5 us
  other arithmetic: 16.6 us -> 0 us
  local copies, waits for them, and re-layouts: 21.4 us -> 6.96 us
  between operations: 8.07 us -> 1.04 us
    dot_general x52 -> x0, matrix products: 51.7 us -> none  [the longest x6 9.92 us: apply_layer(): branch = jnp.dot(hidden, down_w, preferred_element_type=jnp.float32)]
    pallas_call x0 -> x7, Pallas kernels: none -> 29.8 us  [the longest x3 20.1 us: step(): pl.pallas_call(functools.partial(step_kernel, tick, odd_forward, mean_sca...]
    ppermute x4, waiting for transfers between devices: 31.3 us -> 8.93 us  [the longest x1 8.93 us: shards(): slow_0 = lax.ppermute(sent, 'section', far)]
    all_to_all x0 -> x2, blocking collectives: none -> 19.2 us  [the longest x1 11.6 us: shards(): lax.all_to_all(packed, 'dp', 0, 0, axis_index_groups=y_groups, tiled=True)]
    all_to_all x2 -> x0, starting transfers between devices: 12.7 us -> none  [sent_and_summed(): lax.all_to_all(pieces, axis, split_axis=0, concat_axis=0, tiled=True)]
    all_to_all x2 -> x0, waiting for transfers between devices: 7.13 us -> none  [sent_and_summed(): lax.all_to_all(pieces, axis, split_axis=0, concat_axis=0, tiled=True)]
    reduce_sum x6 -> x0, other arithmetic: 6.63 us -> none  [the longest x2 4.54 us: apply_layer(): mean_square = jnp.mean(inputs * inputs, axis=-1, keepdims=True)]
    ppermute x4, starting transfers between devices: 22.9 us -> 16.5 us  [the longest x1 7.88 us: shards(): slow_1 = lax.ppermute(ahead, 'section', far)]
  transfers between devices with their start and end apart: 6 -> 4, of which waited for: 4 -> 1; matrix products, arithmetic and copies ran while one was open for 28% -> 0% of each run, Pallas kernels for 0% -> 12%
where the time goes in v2:
time: 84 us; the launch traced here: 82.3 us
  Pallas kernels  29.8 us (35%)
  blocking collectives  19.2 us (23%)
  starting transfers between devices  16.5 us (20%)
  waiting for transfers between devices  8.93 us (11%)
  local copies, waits for them, and re-layouts  6.96 us (8%)
  between operations  1.04 us (1%)
    pallas_call x3, Pallas kernels, step(): pl.pallas_call(functools.partial(step_kernel, tick, odd_forward, mean_sca...  20.1 us
    all_to_all x1, blocking collectives, shards(): lax.all_to_all(packed, 'dp', 0, 0, axis_index_groups=y_groups, tiled=True)  11.6 us
    ppermute x1, waiting for transfers between devices, shards(): slow_0 = lax.ppermute(sent, 'section', far)  8.93 us
    ppermute x1, starting transfers between devices, shards(): slow_1 = lax.ppermute(ahead, 'section', far)  7.88 us
    ppermute x1, starting transfers between devices, shards(): slow_0 = lax.ppermute(sent, 'section', far)  7.73 us
    all_to_all x1, blocking collectives, shards(): lax.all_to_all(parts, 'dp', 0, 0, axis_index_groups=z_groups, tiled=True)  7.53 us
    unnamed x40, local copies, waits for them, and re-layouts  6.96 us
    pallas_call x1, Pallas kernels, shards(): pl.pallas_call(functools.partial(last_kernel, 1, mean_scale), out_shape=(...  4.08 us
  transfers between devices with their start and end apart: 4, of which 1 were waited for; matrix products, arithmetic and copies ran while one was open for 0% of the time, Pallas kernels for 12%

profile of v2, /device:TPU:39, one launch (start us, length us, event | category | flops | bytes accessed | tf_op | source)
XLA Modules:
  0.0 82.3 jit_solution(17135696384880396303)
XLA Ops:
  0.6 5.8 %shard_map.165 = (f32[128,2048]{1,0:T(8,128)}, f32[64,2048]{1,0:T(8,128)}, f32[64,384]{1,0:T(8,128)}) custom-call(s32[1,2]{1,0:T(1,128)} %plan.7, f32[128,2048]{1,0:T(8,128)} %bitcast.67, f32[128,2048]{1,0:T(8,128)} %bitcast.70, f32[128,2048]{1,0:T(8,128)} %bitcast.68, bf16[2,128,2048]{2,1,0:T(8,128)(2,1)} %examples.9, bf16[2,128,2048]{2,1,0:T(8,128)(2,1)} %bitcast.39, ...), custom_call_target="tpu_custom_call" | custom-call | flops 1207959552 | bytes 7659520 | tf_op jit(solution)/shard_map/pallas_call | solution.py:468
  6.4 7.8 %shard_map.166 = (f32[128,2048]{1,0:T(8,128)}, f32[64,2048]{1,0:T(8,128)}, f32[64,384]{1,0:T(8,128)}) custom-call(s32[1,2]{1,0:T(1,128)} %plan.7, f32[128,2048]{1,0:T(8,128)} %bitcast.69, f32[128,2048]{1,0:T(8,128)} %bitcast.71, f32[128,2048]{1,0:T(8,128)} %get-tuple-element.25.output, bf16[2,128,2048]{2,1,0:T(8,128)(2,1)} %examples.9, ...), custom_call_target="tpu_custom_call" | custom-call | flops 1207959552 | bytes 7659520 | tf_op jit(solution)/shard_map/pallas_call | solution.py:468
  14.2 0.8 collective-permute-start.1
  15.0 7.7 %collective-permute-start = (f32[128,2048]{1,0:T(8,128)}, f32[128,2048]{1,0:T(8,128)}, u32[]{:S(2)}, u32[]{:S(2)}) collective-permute-start(f32[128,2048]{1,0:T(8,128)} %get-tuple-element.25.output), channel_id=1, source_target_pairs={{16,32},{32,16},{48,64},{64,48},{80,96},{96,80},{112,128},{128,112... | collective-permute-start | bytes 3145736 | tf_op jit(solution)/shard_map/ppermute | solution.py:481
  22.7 0.0 collective-permute-done.1.act_in.grad_in.output
  22.7 0.0 copy-start.6
  22.7 1.0 %copy-done.6 = f32[128,2048]{1,0:T(8,128)} copy-done((f32[128,2048]{1,0:T(8,128)}, f32[128,2048]{1,0:T(8,128)S(1)}, u32[]{:S(2)}) %copy-start.6) | copy-done | bytes 1048600
  23.7 0.0 copy-start
  23.7 0.0 copy-start.1
  23.7 0.0 copy-start.9
  23.7 0.0 copy-start.12
  23.7 0.0 copy-start.15
  23.7 0.0 copy-start.16
  23.7 0.0 copy-start.17
  23.7 0.0 copy-start.19
  23.7 6.6 %shard_map.167 = (f32[128,2048]{1,0:T(8,128)}, f32[4,320,128]{2,1,0:T(8,128)}) custom-call(s32[1,2]{1,0:T(1,128)} %plan.7, f32[128,2048]{1,0:T(8,128)} %copy-done.6, f32[128,2048]{1,0:T(8,128)} %copy-done.6, f32[128,2048]{1,0:T(8,128)} %copy-done.6, bf16[2,128,2048]{2,1,0:T(8,128)(2,1)} %examples.9, bf16[2,128,2048]{2,1,0:T(8,128)(2,1)} %bitcast.41, ...), custom_call_target="tpu_custom_call" | custom-call | flops 1207959552 | bytes 7659520 | tf_op jit(solution)/shard_map/pallas_call | solution.py:468
  30.3 0.0 copy-done
  30.3 0.0 copy-done.1
  30.3 0.0 copy-done.9
  30.3 0.0 copy-done.12
  30.4 0.0 copy-done.15
  30.4 0.0 copy-done.16
  30.4 0.0 copy-done.17
  30.4 0.0 copy-done.19
  30.4 0.0 copy-start.2
  30.4 1.2 %copy-done.2 = bf16[2,128,2048]{2,1,0:T(8,128)(2,1)S(1)} copy-done((bf16[2,128,2048]{2,1,0:T(8,128)(2,1)S(1)}, bf16[2,128,2048]{2,1,0:T(8,128)(2,1)}, u32[]{:S(2)}) %copy-start.2) | copy-done | bytes 1048600
  31.6 0.0 copy-start.5
  31.6 1.2 %copy-done.5 = bf16[1,2,128,2048]{3,2,1,0:T(8,128)(2,1)S(1)} copy-done((bf16[1,2,128,2048]{3,2,1,0:T(8,128)(2,1)S(1)}, bf16[1,2,128,2048]{3,2,1,0:T(8,128)(2,1)}, u32[]{:S(2)}) %copy-start.5) | copy-done | bytes 1048600
  32.9 0.0 copy-start.7
  32.9 1.2 %copy-done.7 = f32[128,2048]{1,0:T(8,128)S(1)} copy-done((f32[128,2048]{1,0:T(8,128)S(1)}, f32[128,2048]{1,0:T(8,128)}, u32[]{:S(2)}) %copy-start.7) | copy-done | bytes 1048600
  34.1 0.0 copy-start.8
  34.1 1.0 %copy-done.8 = bf16[1,2048,128]{2,1,0:T(8,128)(2,1)S(1)} copy-done((bf16[1,2048,128]{2,1,0:T(8,128)(2,1)S(1)}, bf16[1,2048,128]{2,1,0:T(8,128)(2,1)}, u32[]{:S(2)}) %copy-start.8) | copy-done | bytes 524312
  35.1 0.0 copy-start.10
  35.1 1.2 %copy-done.10 = f32[128,2048]{1,0:T(8,128)S(1)} copy-done((f32[128,2048]{1,0:T(8,128)S(1)}, f32[128,2048]{1,0:T(8,128)}, u32[]{:S(2)}) %copy-start.10) | copy-done | bytes 1048600
  36.3 0.0 copy-start.3
  36.3 0.0 copy-start.4
  36.3 0.0 copy-start.11
  36.3 0.0 copy-start.13
  36.4 0.0 copy-start.14
  36.4 0.0 copy-start.18
  36.4 3.3 %recompute_1.1 = (f32[128,2048]{1,0:T(8,128)S(1)}, f32[128,128]{1,0:T(8,128)S(1)}, bf16[128,2048]{1,0:T(8,128)(2,1)S(1)}, f32[128,128]{1,0:T(8,128)S(1)}, bf16[1...) custom-call(s32[1,2]{1,0:T(1,128)S(1)} %copy-done.19, f32[128,2048]{1,0:T(8,128)S(1)} %copy-done.7, ...), custom_call_target="tpu_custom_call" | custom-call | flops 503316480 | bytes 7659520 | tf_op jit(solution)/shard_map/recompute_1/pallas_call | solution.py:486
  39.7 8.9 %collective-permute-done.arrived = f32[128,2048]{1,0:T(8,128)} collective-permute-done((f32[128,2048]{1,0:T(8,128)}, f32[128,2048]{1,0:T(8,128)}, u32[]{:S(2)}, u32[]{:S(2)}) %collective-permute-start) | collective-permute-done | bytes 1048608 | tf_op jit(solution)/shard_map/ppermute | solution.py:481
  48.6 0.0 copy-done.3
  48.6 0.0 copy-done.4
  48.6 0.0 copy-done.11
  48.6 0.0 copy-done.13
  48.7 0.0 copy-done.14
  48.7 0.0 copy-done.18
  48.7 4.1 %step_1b.1 = (f32[128,2048]{1,0:T(8,128)S(1)}, f32[4,320,128]{2,1,0:T(8,128)S(1)}) custom-call(f32[128,2048]{1,0:T(8,128)} %collective-permute-done.arrived, f32[128,2048]{1,0:T(8,128)S(1)} %copy-done.11, bf16[2,128,2048]{2,1,0:T(8,128)(2,1)S(1)} %copy-done.3, s32[2,8,128]{2,1,0:T(8,128)S(1)} %bitcast.62, f32[4,320,128]{2,1,0:T(8,128)S(1)} %copy-done.13, ...), custom_call_target="tpu_custom_call" | custom-call | flops 704643072 | bytes 7659520 | tf_op jit(solution)/shard_map/step_1b/pallas_call | solution.py:504
  52.8 0.1 collective-permute-start.3
  52.9 7.9 %collective-permute-start.2 = (f32[128,2048]{1,0:T(8,128)S(1)}, f32[128,2048]{1,0:T(8,128)S(1)}, u32[]{:S(2)}, u32[]{:S(2)}) collective-permute-start(f32[128,2048]{1,0:T(8,128)S(1)} %copy-done.11), channel_id=1, source_target_pairs={{16,32},{32,16},{48,64},{64,48},{80,96},{96,80},{112,128},{128,112... | collective-permute-start | bytes 3145736 | tf_op jit(solution)/shard_map/ppermute | solution.py:485
  60.8 11.6 %all_to_all.10.parts = f32[4,320,128]{2,1,0:T(8,128)S(1)} all-to-all(f32[4,320,128]{2,1,0:T(8,128)S(1)} %get-tuple-element.40), channel_id=1, replica_groups={{0,1,2,3},{4,5,6,7},{8,9,10,11},{12,13,14,15},{16,17,18,19},{20,21,22,2..., dimensions={0} | all-to-all | bytes 1310720 | tf_op jit(solution)/shard_map/all_to_all | solution.py:517
  72.4 7.5 %all_to_all.11.parts = f32[4,80,128]{2,1,0:T(8,128)S(1)} all-to-all(f32[4,80,128]{2,1,0:T(8,128)S(1)} %sum_y.1), channel_id=1, replica_groups={{0,4,8,12},{1,5,9,13},{2,6,10,14},{3,7,11,15},{16,20,24,28},{17,21,25,2..., dimensions={0} | all-to-all | bytes 327680 | tf_op jit(solution)/shard_map/all_to_all | solution.py:526
  80.0 0.0 collective-permute-done.3.fast
  80.0 0.0 collective-permute-done.2.slow
  80.0 2.2 %sum_z.1 = (f32[64,128]{1,0:T(8,128)}, f32[2,24,32]{2,1,0:T(8,128)}, f32[128,2048]{1,0:T(8,128)}, f32[128,2048]{1,0:T(8,128)}) custom-call(f32[4,80,128]{2,1,0:T(8,128)S(1)} %all_to_all.11.parts, f32[128,2048]{1,0:T(8,128)S(1)} %collective-permute-done.2.slow, f32[128,2048]{1,0:T(8,128)S(1)} %collective-permute-done.3.fast), custom_call_target="tpu_custom_call" | custom-call | tf_op jit(solution)/shard_map/sum_z/pallas_call | solution.py:528
  (1 shorter events, 0.0 us)
Async XLA Ops:
  14.2 8.5 %collective-permute-start.1 = (f32[128,2048]{1,0:T(8,128)}, f32[128,2048]{1,0:T(8,128)S(1)}, u32[]{:S(2)}, u32[]{:S(2)}) collective-permute-start(f32[128,2048]{1,0:T(8,128)} %get-tuple-element.26), channel_id=1, source_target_pairs={{0,16},{16,0},{32,48},{48,32},{64,80},{80,64},{96,112},{112,96},{1... | collective-permute-start | bytes 3145736 | tf_op jit(solution)/shard_map/ppermute | solution.py:483
  15.0 33.7 %collective-permute-start = (f32[128,2048]{1,0:T(8,128)}, f32[128,2048]{1,0:T(8,128)}, u32[]{:S(2)}, u32[]{:S(2)}) collective-permute-start(f32[128,2048]{1,0:T(8,128)} %get-tuple-element.25.output), channel_id=1, source_target_pairs={{16,32},{32,16},{48,64},{64,48},{80,96},{96,80},{112,128},{128,112... | collective-permute-start | bytes 3145736 | tf_op jit(solution)/shard_map/ppermute | solution.py:481
  22.7 1.0 %copy-start.6 = (f32[128,2048]{1,0:T(8,128)}, f32[128,2048]{1,0:T(8,128)S(1)}, u32[]{:S(2)}) copy-start(f32[128,2048]{1,0:T(8,128)S(1)} %collective-permute-done.1.act_in.grad_in.output) | copy-start | bytes 3145732
  23.7 6.6 %copy-start = (bf16[1,2048,384]{2,1,0:T(8,128)(2,1)S(1)}, bf16[1,2048,384]{2,1,0:T(8,128)(2,1)}, u32[]{:S(2)}) copy-start(bf16[1,2048,384]{2,1,0:T(8,128)(2,1)} %param.23) | copy-start | bytes 4718596
  23.7 6.6 %copy-start.1 = (bf16[1,2048,384]{2,1,0:T(8,128)(2,1)S(1)}, bf16[1,2048,384]{2,1,0:T(8,128)(2,1)}, u32[]{:S(2)}) copy-start(bf16[1,2048,384]{2,1,0:T(8,128)(2,1)} %param.24) | copy-start | bytes 4718596
  23.7 6.6 %copy-start.9 = (bf16[1,2048,64]{1,2,0:T(8,128)(2,1)S(1)}, bf16[1,2048,64]{1,2,0:T(8,128)(2,1)}, u32[]{:S(2)}) copy-start(bf16[1,2048,64]{1,2,0:T(8,128)(2,1)} %param.26) | copy-start | bytes 786436
  23.7 6.7 %copy-start.12 = (bf16[1,2,32,384]{3,2,1,0:T(8,128)(2,1)S(1)}, bf16[1,2,32,384]{3,2,1,0:T(8,128)(2,1)}, u32[]{:S(2)}) copy-start(bf16[1,2,32,384]{3,2,1,0:T(8,128)(2,1)} %param.27) | copy-start | bytes 147460
  23.7 6.7 %copy-start.15 = (s32[1,2,128,8]{2,3,1,0:T(8,128)S(1)}, s32[1,2,128,8]{2,3,1,0:T(8,128)}, u32[]{:S(2)}) copy-start(s32[1,2,128,8]{2,3,1,0:T(8,128)} %param.19) | copy-start | bytes 24580
  23.7 6.7 %copy-start.16 = (f32[1,2048]{1,0:T(1,128)S(1)}, f32[1,2048]{1,0:T(1,128)}, u32[]{:S(2)}) copy-start(f32[1,2048]{1,0:T(1,128)} %rest_7_.1) | copy-start | bytes 24580
  23.7 6.7 %copy-start.17 = (s32[1,2,128,8]{2,3,1,0:T(8,128)S(1)}, s32[1,2,128,8]{2,3,1,0:T(8,128)}, u32[]{:S(2)}) copy-start(s32[1,2,128,8]{2,3,1,0:T(8,128)} %param.20) | copy-start | bytes 24580
  23.7 6.7 %copy-start.19 = (s32[1,2]{1,0:T(1,128)S(1)}, s32[1,2]{1,0:T(1,128)}, u32[]{:S(2)}) copy-start(s32[1,2]{1,0:T(1,128)} %plan.7) | copy-start | bytes 28
  30.4 1.2 %copy-start.2 = (bf16[2,128,2048]{2,1,0:T(8,128)(2,1)S(1)}, bf16[2,128,2048]{2,1,0:T(8,128)(2,1)}, u32[]{:S(2)}) copy-start(bf16[2,128,2048]{2,1,0:T(8,128)(2,1)} %examples.9) | copy-start | bytes 3145732
  31.6 1.2 %copy-start.5 = (bf16[1,2,128,2048]{3,2,1,0:T(8,128)(2,1)S(1)}, bf16[1,2,128,2048]{3,2,1,0:T(8,128)(2,1)}, u32[]{:S(2)}) copy-start(bf16[1,2,128,2048]{3,2,1,0:T(8,128)(2,1)} %param.17) | copy-start | bytes 3145732
  32.9 1.2 %copy-start.7 = (f32[128,2048]{1,0:T(8,128)S(1)}, f32[128,2048]{1,0:T(8,128)}, u32[]{:S(2)}) copy-start(f32[128,2048]{1,0:T(8,128)} %copy-done.6) | copy-start | bytes 3145732
  34.1 1.0 %copy-start.8 = (bf16[1,2048,128]{2,1,0:T(8,128)(2,1)S(1)}, bf16[1,2048,128]{2,1,0:T(8,128)(2,1)}, u32[]{:S(2)}) copy-start(bf16[1,2048,128]{2,1,0:T(8,128)(2,1)} %param.22) | copy-start | bytes 1572868
  35.1 1.2 %copy-start.10 = (f32[128,2048]{1,0:T(8,128)S(1)}, f32[128,2048]{1,0:T(8,128)}, u32[]{:S(2)}) copy-start(f32[128,2048]{1,0:T(8,128)} %get-tuple-element.29.after.output) | copy-start | bytes 3145732
  36.3 12.3 %copy-start.3 = (bf16[2,128,2048]{2,1,0:T(8,128)(2,1)S(1)}, bf16[2,128,2048]{2,1,0:T(8,128)(2,1)}, u32[]{:S(2)}) copy-start(bf16[2,128,2048]{2,1,0:T(8,128)(2,1)} %examples.9) | copy-start | bytes 3145732
  36.3 12.3 %copy-start.4 = (bf16[1,384,2048]{2,1,0:T(8,128)(2,1)S(1)}, bf16[1,384,2048]{2,1,0:T(8,128)(2,1)}, u32[]{:S(2)}) copy-start(bf16[1,384,2048]{2,1,0:T(8,128)(2,1)} %param.25) | copy-start | bytes 4718596
  36.3 12.3 %copy-start.11 = (f32[128,2048]{1,0:T(8,128)S(1)}, f32[128,2048]{1,0:T(8,128)}, u32[]{:S(2)}) copy-start(f32[128,2048]{1,0:T(8,128)} %get-tuple-element.29.after.output) | copy-start | bytes 3145732
  36.3 12.3 %copy-start.13 = (f32[4,320,128]{2,1,0:T(8,128)S(1)}, f32[4,320,128]{2,1,0:T(8,128)}, u32[]{:S(2)}) copy-start(f32[4,320,128]{2,1,0:T(8,128)} %get-tuple-element.30.packed_in) | copy-start | bytes 1966084
  36.4 12.3 %copy-start.14 = (f32[64,2048]{1,0:T(8,128)S(1)}, f32[64,2048]{1,0:T(8,128)}, u32[]{:S(2)}) copy-start(f32[64,2048]{1,0:T(8,128)} %get-tuple-element.31.ga_in) | copy-start | bytes 1572868
  36.4 12.3 %copy-start.18 = (f32[64,384]{1,0:T(8,128)S(1)}, f32[64,384]{1,0:T(8,128)}, u32[]{:S(2)}) copy-start(f32[64,384]{1,0:T(8,128)} %get-tuple-element.32.gb_in) | copy-start | bytes 294916
  52.8 27.2 %collective-permute-start.3 = (f32[128,2048]{1,0:T(8,128)S(1)}, f32[128,2048]{1,0:T(8,128)S(1)}, u32[]{:S(2)}, u32[]{:S(2)}) collective-permute-start(f32[128,2048]{1,0:T(8,128)S(1)} %get-tuple-element.41), channel_id=1, source_target_pairs={{0,16},{16,0},{32,48},{48,32},{64,80},{80,64},{96,112},{112,96},{1... | collective-permute-start | bytes 3145736 | tf_op jit(solution)/shard_map/ppermute | solution.py:514
  52.9 27.1 %collective-permute-start.2 = (f32[128,2048]{1,0:T(8,128)S(1)}, f32[128,2048]{1,0:T(8,128)S(1)}, u32[]{:S(2)}, u32[]{:S(2)}) collective-permute-start(f32[128,2048]{1,0:T(8,128)S(1)} %copy-done.11), channel_id=1, source_target_pairs={{16,32},{32,16},{48,64},{64,48},{80,96},{96,80},{112,128},{128,112... | collective-permute-start | bytes 3145736 | tf_op jit(solution)/shard_map/ppermute | solution.py:485

commit v3 on v2

v3 whole, which is shorter than its diff:
```python
import functools

import jax
import jax.numpy as jnp
from jax import lax
from jax.experimental import pallas as pl
from jax.experimental.pallas import tpu as pltpu
from jax.sharding import PartitionSpec as P


SCALE = 2.0
EPS = 1e-06
F32 = jnp.float32
BF16 = jnp.bfloat16
ANY = pl.BlockSpec(memory_space=pl.ANY)
SMEM = pl.BlockSpec(memory_space=pltpu.SMEM)
VMEM = pl.BlockSpec(memory_space=pltpu.VMEM)


def nn(a, b):
    return jnp.dot(a, b, preferred_element_type=F32)


def nt(a, b):
    return lax.dot_general(a, b, (((1,), (1,)), ((), ())), preferred_element_type=F32)


def primal(x, routes_t, gain, copies, router, a_t, gate, up, factors):
    def ready(name):
        if copies is not None:
            copies[name].wait()

    rstd = lax.rsqrt(jnp.mean(x * x, axis=-1, keepdims=True) + EPS)
    normed = (x * rstd * gain).astype(BF16)
    ready("router")
    logits = nn(normed, router[...])
    experts = logits.shape[1]
    expert = lax.broadcasted_iota(jnp.int32, (experts, routes_t.shape[1]), 0)
    named = jnp.zeros(expert.shape, F32)
    for k in range(routes_t.shape[0]):
        named = jnp.where(routes_t[k : k + 1, :] == expert, 1.0, named)
    scores = jnp.where(named.T > 0.5, jnp.exp(logits), 0.0)
    share = scores / jnp.sum(scores, axis=-1, keepdims=True)
    weight = share[:, 0:1]
    ready("a")
    low = nt(normed, a_t[...]).astype(BF16)
    rank = low.shape[1] // 2
    ready("b")
    ready("gate")
    gate_pre = nn(normed, gate[...]) + SCALE * nn(low[:, :rank], factors[0])
    ready("up")
    up_pre = nn(normed, up[...]) + SCALE * nn(low[:, rank:], factors[1])
    return rstd, normed, share, weight, low, gate_pre, up_pre


def when_all(*predicates):
    both = predicates[0]
    for predicate in predicates[1:]:
        both = jnp.logical_and(both, predicate)
    return pl.when(both)


def position():
    section = lax.axis_index("section")
    odd = lax.rem(section, 2) == 1
    return (
        odd,
        jnp.logical_not(odd),
        section == 0,
        section == lax.axis_size("section") - 1,
    )


def fetch(cases, x_s, b_s, r_s, sems):
    moves = []
    for predicates, source, routes in cases:
        narrow = source.dtype == BF16
        mine = [pltpu.make_async_copy(source, b_s if narrow else x_s, sems.at[0])]
        if routes is not None:
            mine.append(pltpu.make_async_copy(routes, r_s, sems.at[1]))
        moves.append((predicates, narrow, mine))

        @when_all(*predicates)
        def _(mine=mine):
            for copy in mine:
                copy.start()

    def wait():
        for predicates, narrow, mine in moves:

            @when_all(*predicates)
            def _(narrow=narrow, mine=mine):
                for copy in mine:
                    copy.wait()
                if narrow:
                    x_s[...] = b_s[...].astype(F32)

    return wait


NAMES = ("gain", "router", "a", "gate", "up", "b", "down")


def fetch_weights(hbm, weights, order, sems):
    copies = {}
    for name in order:
        i = NAMES.index(name)
        copies[name] = pltpu.make_async_copy(hbm[i], weights[i], sems.at[i])
        copies[name].start()
    return copies


def primal_of(x, routes, copies, weights):
    gain_s, router, a_t, gate, up, factors = weights[:6]
    if copies is not None:
        copies["gain"].wait()
    return primal(x, routes, gain_s[...], copies, router, a_t, gate, up, factors)


def output_of(x_s, values, down):
    _, _, _, weight, _, gate_pre, up_pre = values
    hidden = (gate_pre * jax.nn.sigmoid(gate_pre) * up_pre).astype(BF16)
    return x_s[...] + weight * nn(hidden, down[...])


def gradients(x_s, g_s, saved, weights, copies=None, x_wait=None):
    def ready(*names):
        if copies is not None:
            for name in names:
                copies[name].wait()

    gain_s, router, a_t, gate, up, factors, down = weights
    rstd, normed, share, weight, low, gate_pre, up_pre = saved
    sig = jax.nn.sigmoid(gate_pre)
    silu = gate_pre * sig
    hidden = (silu * up_pre).astype(BF16)
    ready("down")
    back = nt(g_s[...].astype(BF16), down[...])
    d_weight = jnp.sum(hidden.astype(F32) * back, axis=-1, keepdims=True)
    lead = (lax.broadcasted_iota(jnp.int32, share.shape, 1) == 0).astype(F32)
    d_logits = ((d_weight * weight) * (lead - share)).astype(BF16)
    d_hidden = (weight * back).astype(BF16).astype(F32)
    d_gate = (d_hidden * up_pre * (sig * (1.0 + gate_pre * (1.0 - sig)))).astype(BF16)
    d_up = (d_hidden * silu).astype(BF16)
    ready("b", "gate", "up", "router", "a", "gain")
    if x_wait is not None:
        x_wait()
    d_low_f = SCALE * jnp.concatenate([nt(d_gate, factors[0]), nt(d_up, factors[1])], axis=1)
    d_normed = (
        nt(d_gate, gate[...])
        + nt(d_up, up[...])
        + nt(d_logits, router[...])
        + nn(d_low_f.astype(BF16), a_t[...])
    )
    scaled = d_normed * gain_s[...]
    x = x_s[...]
    along = jnp.mean(scaled * x, axis=-1, keepdims=True) * (rstd * rstd)
    dx = g_s[...] + rstd * (scaled - x * along)
    rank = low.shape[1] // 2
    ga = nn(d_low_f.T.astype(BF16), normed)
    low_t = low.astype(F32).T.astype(BF16)
    gb = SCALE * jnp.concatenate([nn(low_t[:rank], d_gate), nn(low_t[rank:], d_up)], axis=0)
    return dx, ga, gb


def normalizer(ga, gb, mean_scale):
    square = (jnp.sum(ga * ga) + jnp.sum(gb * gb)) / (ga.size + gb.size)
    return lax.rsqrt(square + EPS) * mean_scale


def pack(packed, ga, gb):
    gb_t = gb.T
    parts, size, width = packed.shape
    rows = gb_t.shape[0] // parts
    tall = ga.shape[0]
    half = rows // 2
    for p in range(parts):
        packed[p, :tall, :] = ga[:, p * width : (p + 1) * width]
        packed[p, tall : tall + half, :tall] = gb_t[p * rows : p * rows + half]
        packed[p, tall : tall + half, tall:] = gb_t[p * rows + half : (p + 1) * rows]
        packed[p, tall + half :, :] = jnp.zeros((size - tall - half, width), F32)


FIRST_ORDER = ("gain", "router", "a", "b", "gate", "up", "down")
X1, X2, G, W, OUT = (pl.ds(0, 2), pl.ds(2, 2), pl.ds(4, 2), pl.ds(6, 7), pl.ds(13, 7))


def first_kernel(
    mean_scale, plan, arriving, returning, examples, stash, fwd_routes_t, bwd_routes_t, *rest
):
    hbm, (slow_o, fast_o, ga_o, gb_o), rest = rest[:7], rest[7:11], rest[11:]
    x_s, x2_s, g_s, y_s, d_s, b_s, b2_s, e_s, r_s, r2_s, ga_s, gb_s, *weights, sems = rest
    odd, even, first, last = position()
    slot = plan[0, 0]
    mine = fwd_routes_t.at[0]
    x_wait = fetch(
        [
            ((first,), examples.at[0], mine),
            ((jnp.logical_not(first),), arriving, mine),
        ],
        x_s,
        b_s,
        r_s,
        sems.at[X1],
    )
    copies = fetch_weights(hbm, weights, FIRST_ORDER, sems.at[W])
    x2_wait = fetch(
        [
            ((last,), arriving, mine),
            ((jnp.logical_not(last),), stash.at[slot], bwd_routes_t.at[slot]),
        ],
        x2_s,
        b2_s,
        r2_s,
        sems.at[X2],
    )
    g_copy = pltpu.make_async_copy(returning, g_s, sems.at[4])
    t_copy = pltpu.make_async_copy(examples.at[0], e_s, sems.at[5])
    pl.when(jnp.logical_not(last))(g_copy.start)
    pl.when(last)(t_copy.start)
    x_wait()
    values = primal_of(x_s[...], r_s[...], copies, weights)
    copies["down"].wait()
    y_s[...] = output_of(x_s, values, weights[6])
    outs = sems.at[OUT]
    y_slow = pltpu.make_async_copy(y_s, slow_o, outs.at[0])
    y_fast = pltpu.make_async_copy(y_s, fast_o, outs.at[0])
    d_slow = pltpu.make_async_copy(d_s, slow_o, outs.at[1])
    d_fast = pltpu.make_async_copy(d_s, fast_o, outs.at[1])
    pl.when(odd)(y_slow.start)
    pl.when(even)(y_fast.start)
    x2_wait()

    @pl.when(last)
    def _():
        t_copy.wait()
        g_s[...] = y_s[...] - e_s[...].astype(F32)

    values = primal_of(x2_s[...], r2_s[...], None, weights)
    pl.when(jnp.logical_not(last))(g_copy.wait)
    dx, ga, gb = gradients(x2_s, g_s, values, weights)
    d_s[...] = dx
    pl.when(odd)(d_fast.start)
    pl.when(even)(d_slow.start)
    factor = normalizer(ga, gb, mean_scale)
    ga_s[...] = factor * ga
    gb_s[...] = factor * gb
    tail = [
        pltpu.make_async_copy(ga_s, ga_o, outs.at[2]),
        pltpu.make_async_copy(gb_s, gb_o, outs.at[3]),
    ]
    for copy in tail:
        copy.start()
    for copy in tail:
        copy.wait()

    @pl.when(odd)
    def _():
        y_slow.wait()
        d_fast.wait()

    @pl.when(even)
    def _():
        y_fast.wait()
        d_slow.wait()


def second_kernel(
    tick, mean_scale, plan, arrived, stash, fwd_routes_t, bwd_routes_t, ga_in, gb_in, *rest
):
    hbm, (sent, packed, *saved_o), rest = rest[:7], rest[7:15], rest[15:]
    x_s, x2_s, y_s, b_s, b2_s, r_s, r2_s, ga_s, gb_s, packed_s, *rest = rest
    saved, weights, sems = rest[:6], rest[6:13], rest[13]
    odd, even, _, last = position()
    slot = plan[0, tick]
    mine = fwd_routes_t.at[tick]
    stored = (stash.at[slot], bwd_routes_t.at[slot])
    inner = jnp.logical_and(odd, jnp.logical_not(last))
    x_wait = fetch([((odd,), arrived, mine), ((even,), *stored)], x_s, b_s, r_s, sems.at[X1])
    copies = fetch_weights(hbm, weights, FIRST_ORDER, sems.at[W])
    x2_wait = fetch(
        [((last,), arrived, mine), ((inner,), *stored)], x2_s, b2_s, r2_s, sems.at[X2]
    )
    g_copies = [
        pltpu.make_async_copy(arrived, x2_s, sems.at[4]),
        pltpu.make_async_copy(ga_in, ga_s, sems.at[5]),
        pltpu.make_async_copy(gb_in, gb_s, sems.at[20]),
    ]

    @pl.when(even)
    def _():
        for copy in g_copies:
            copy.start()

    x_wait()
    values = primal_of(x_s[...], r_s[...], copies, weights)
    copies["down"].wait()
    outs = sems.at[OUT]
    y_copy = pltpu.make_async_copy(y_s, sent, outs.at[0])

    @pl.when(odd)
    def _():
        y_s[...] = output_of(x_s, values, weights[6])
        y_copy.start()
        x2_wait()
        rstd, normed, share, _, low, gate_pre, up_pre = primal_of(
            x2_s[...], r2_s[...], None, weights
        )
        kept = (jnp.broadcast_to(rstd, saved[0].shape), normed, share, low, gate_pre, up_pre)
        moves = []
        for i, value in enumerate(kept):
            saved[i][...] = value
            moves.append(pltpu.make_async_copy(saved[i], saved_o[i], outs.at[1 + i]))
            moves[-1].start()
        for move in moves:
            move.wait()

    @pl.when(even)
    def _():
        for copy in g_copies:
            copy.wait()
        dx, ga, gb = gradients(x_s, x2_s, values, weights)
        y_s[...] = dx
        y_copy.start()
        factor = normalizer(ga, gb, mean_scale)
        pack(packed_s, ga_s[...] + factor * ga, gb_s[...] + factor * gb)
        move = pltpu.make_async_copy(packed_s, packed, outs.at[1])
        move.start()
        move.wait()

    y_copy.wait()


def third_kernel(
    tick,
    mean_scale,
    plan,
    arrived,
    near,
    output,
    examples,
    stash,
    fwd_routes_t,
    packed_in,
    ga_in,
    gb_in,
    *rest,
):
    saved_in, rest = rest[:6], rest[6:]
    hbm, (sent, packed), rest = rest[:7], rest[7:9], rest[9:]
    x_s, g_s, y_s, b_s, e_s, r_s, ga_s, gb_s, packed_s, *rest = rest
    saved, weights, sems = rest[:6], rest[6:13], rest[13]
    odd, even, first, last = position()
    inner = jnp.logical_and(odd, jnp.logical_not(last))
    outs = sems.at[OUT]
    y_copy = pltpu.make_async_copy(y_s, sent, outs.at[0])
    p_copy = pltpu.make_async_copy(packed_s, packed, outs.at[1])

    @pl.when(even)
    def _():
        mine = fwd_routes_t.at[tick]
        x_wait = fetch(
            [
                ((first,), examples.at[tick], mine),
                ((jnp.logical_not(first),), arrived, mine),
            ],
            x_s,
            b_s,
            r_s,
            sems.at[X1],
        )
        copies = fetch_weights(hbm, weights, FIRST_ORDER, sems.at[W])
        keep = pltpu.make_async_copy(packed_in, packed_s, sems.at[4])
        keep.start()
        x_wait()
        values = primal_of(x_s[...], r_s[...], copies, weights)
        copies["down"].wait()
        keep.wait()
        p_copy.start()
        y_s[...] = output_of(x_s, values, weights[6])
        y_copy.start()

    @pl.when(odd)
    def _():
        g_copy = pltpu.make_async_copy(arrived, g_s, sems.at[4])
        o_copy = pltpu.make_async_copy(output, g_s, sems.at[4])
        t_copy = pltpu.make_async_copy(examples.at[tick], e_s, sems.at[5])
        pl.when(inner)(g_copy.start)

        @pl.when(last)
        def _():
            o_copy.start()
            t_copy.start()

        moves = [pltpu.make_async_copy(saved_in[i], saved[i], outs.at[1 + i]) for i in range(6)]
        for i in (2, 4, 5):
            moves[i].start()
        copies = fetch_weights(hbm, weights, ("down", "b", "gate", "up"), sems.at[W])
        for i in (0, 1, 3):
            moves[i].start()
        x_wait = fetch(
            [((last,), near, None), ((inner,), stash.at[plan[0, tick]], None)],
            x_s,
            b_s,
            None,
            sems.at[X1],
        )
        copies.update(fetch_weights(hbm, weights, ("router", "a", "gain"), sems.at[W]))
        sums = [
            pltpu.make_async_copy(ga_in, ga_s, sems.at[2]),
            pltpu.make_async_copy(gb_in, gb_s, sems.at[3]),
        ]
        for copy in sums:
            copy.start()
        for move in moves:
            move.wait()
        pl.when(inner)(g_copy.wait)

        @pl.when(last)
        def _():
            o_copy.wait()
            t_copy.wait()
            g_s[...] = g_s[...] - e_s[...].astype(F32)

        rstd, normed, share, low, gate_pre, up_pre = (ref[...] for ref in saved)
        values = (rstd[:, 0:1], normed, share, share[:, 0:1], low, gate_pre, up_pre)
        dx, ga, gb = gradients(x_s, g_s, values, weights, copies, x_wait)
        y_s[...] = dx
        y_copy.start()
        factor = normalizer(ga, gb, mean_scale)
        for copy in sums:
            copy.wait()
        pack(packed_s, ga_s[...] + factor * ga, gb_s[...] + factor * gb)
        p_copy.start()

    y_copy.wait()
    p_copy.wait()


def final_kernel(tall, half, pieces, parts, slow, fast, ga, gb, acts_o, grads_o, slow_s, fast_s, sems):
    odd, even, _, _ = position()
    rows = slow.shape[0] // pieces
    moves = []
    for source, stage, low, high in (
        (slow, slow_s, acts_o, grads_o),
        (fast, fast_s, grads_o, acts_o),
    ):
        for i in range(pieces):
            at = pl.ds(i * rows, rows)
            k = 2 * len(moves)
            move_in = pltpu.make_async_copy(source.at[at], stage.at[at], sems.at[k])
            move_even = pltpu.make_async_copy(stage.at[at], low.at[at], sems.at[k + 1])
            move_odd = pltpu.make_async_copy(stage.at[at], high.at[at], sems.at[k + 1])
            moves.append((move_in, move_even, move_odd))
    for move_in, _, _ in moves:
        move_in.start()
    for move_in, move_even, move_odd in moves:
        move_in.wait()
        pl.when(even)(move_even.start)
        pl.when(odd)(move_odd.start)
    total = jnp.sum(parts[...], axis=0)
    ga[...] = total[:tall]
    rank = gb.shape[2]
    for side in range(2):
        for part in range(2):
            lane = part * tall + side * rank
            gb[side, part * half : (part + 1) * half, :] = total[
                tall : tall + half, lane : lane + rank
            ]
    for _, move_even, move_odd in moves:
        pl.when(even)(move_even.wait)
        pl.when(odd)(move_odd.wait)


def swaps(first, count):
    pairs = []
    for s in range(first, count - 1, 2):
        pairs += [(s, s + 1), (s + 1, s)]
    return pairs


def shards(
    examples,
    arriving,
    returning,
    stash,
    plan,
    forward_expert_routes,
    backward_expert_routes,
    input_norm_gain,
    router,
    frozen_gate_weight,
    frozen_up_weight,
    frozen_down_weight,
    down_factors,
    up_factors,
):
    replicas = lax.axis_size("dp")
    ticks, tokens, width = examples.shape
    mean_scale = 1.0 / (ticks * replicas)
    gain, router, gate, up, down = (
        input_norm_gain,
        router[0],
        frozen_gate_weight[0],
        frozen_up_weight[0],
        frozen_down_weight[0],
    )
    a_t = down_factors[0].T
    b = up_factors[0]
    stash = stash[0]
    fwd_routes_t = jnp.swapaxes(forward_expert_routes[0], 1, 2)
    bwd_routes_t = jnp.swapaxes(backward_expert_routes[0], 1, 2)
    topk = fwd_routes_t.shape[1]
    hidden_units = gate.shape[1]
    columns = a_t.shape[0]
    weights = (gain, router, a_t, gate, up, b, down)
    scratch = [pltpu.VMEM(w.shape, w.dtype) for w in weights]
    x_scratch = pltpu.VMEM((tokens, width), F32)
    b_scratch = pltpu.VMEM((tokens, width), BF16)
    r_scratch = pltpu.VMEM((topk, tokens), jnp.int32)
    semaphores = pltpu.SemaphoreType.DMA((21,))
    sections = lax.axis_size("section")
    near = swaps(0, sections)
    far = swaps(1, sections)
    rows_each = hidden_units // replicas
    size = columns + -(-(rows_each // 2) // 8) * 8
    share_width = width // replicas
    activation = jax.ShapeDtypeStruct((tokens, width), F32)
    sums_shape = (
        jax.ShapeDtypeStruct((columns, width), F32),
        jax.ShapeDtypeStruct((columns, hidden_units), F32),
    )
    packed_shape = jax.ShapeDtypeStruct((replicas, size, share_width), F32)
    saved_shape = (
        jax.ShapeDtypeStruct((tokens, 128), F32),
        jax.ShapeDtypeStruct((tokens, width), BF16),
        jax.ShapeDtypeStruct((tokens, router.shape[1]), F32),
        jax.ShapeDtypeStruct((tokens, columns), BF16),
        jax.ShapeDtypeStruct((tokens, hidden_units), F32),
        jax.ShapeDtypeStruct((tokens, hidden_units), F32),
    )

    def rooms(shapes):
        return [pltpu.VMEM(shape.shape, shape.dtype) for shape in shapes]

    primal_flops = 2 * tokens * width * (router.shape[1] + columns + 2 * hidden_units)
    down_flops = 2 * tokens * width * hidden_units
    weight_bytes = sum(w.size * w.dtype.itemsize for w in weights)

    def kernel(body, flops, outs, rooms, operands):
        return pl.pallas_call(
            body,
            out_shape=outs,
            in_specs=[SMEM] + [ANY] * (len(operands) - 1),
            out_specs=(ANY,) * len(outs),
            scratch_shapes=[*rooms, *scratch, semaphores],
            cost_estimate=pl.CostEstimate(
                flops=flops, bytes_accessed=weight_bytes + 8 * tokens * width, transcendentals=0
            ),
        )(*operands)

    slow, fast, *sums = kernel(
        functools.partial(first_kernel, mean_scale),
        3 * primal_flops + 2 * down_flops,
        (activation, activation, *sums_shape),
        [x_scratch] * 5 + [b_scratch] * 3 + [r_scratch] * 2 + rooms(sums_shape),
        (plan, arriving[0], returning[0], examples, stash, fwd_routes_t, bwd_routes_t, *weights),
    )
    slow_0 = lax.ppermute(slow, "section", far)
    fast_0 = lax.ppermute(fast, "section", near)
    ahead, packed, *saved = kernel(
        functools.partial(second_kernel, 1, mean_scale),
        2 * primal_flops + down_flops,
        (activation, packed_shape, *saved_shape),
        [x_scratch] * 3
        + [b_scratch] * 2
        + [r_scratch] * 2
        + rooms((*sums_shape, packed_shape, *saved_shape)),
        (plan, fast_0, stash, fwd_routes_t, bwd_routes_t, *sums, *weights),
    )
    slow_1 = lax.ppermute(ahead, "section", far)
    sent, packed = kernel(
        functools.partial(third_kernel, 1, mean_scale),
        primal_flops + down_flops,
        (activation, packed_shape),
        [x_scratch] * 3
        + [b_scratch] * 2
        + [r_scratch]
        + rooms((*sums_shape, packed_shape, *saved_shape)),
        (plan, slow_0, fast_0, ahead, examples, stash, fwd_routes_t, packed, *sums, *saved, *weights),
    )
    parts = lax.all_to_all(packed, "dp", 0, 0, tiled=True)
    fast_1 = lax.ppermute(sent, "section", near)
    pieces = 4
    share_a, share_b, next_acts, next_grads = pl.pallas_call(
        functools.partial(final_kernel, columns, rows_each // 2, pieces),
        out_shape=(
            jax.ShapeDtypeStruct((columns, share_width), F32),
            jax.ShapeDtypeStruct((2, rows_each, columns // 2), F32),
            activation,
            activation,
        ),
        in_specs=[VMEM, ANY, ANY],
        out_specs=(VMEM, VMEM, ANY, ANY),
        scratch_shapes=[x_scratch, x_scratch, pltpu.SemaphoreType.DMA((4 * pieces,))],
        compiler_params=pltpu.CompilerParams(vmem_limit_bytes=8 << 20),
        name="sum_dp",
    )(parts, slow_1, fast_1)
    return (
        next_acts[None],
        next_grads[None],
        share_a.T[None],
        jnp.swapaxes(share_b, 1, 2)[None],
    )


def solution(mesh):
    in_specs = (
        P(None, "dp", None),
        P("section", "dp", None),
        P("section", "dp", None),
        P("section", None, "dp", None),
        P("section", None),
        P("section", None, "dp", None),
        P("section", None, "dp", None),
        P("section", None),
        P("section", None, None),
        P("section", None, None),
        P("section", None, None),
        P("section", None, None),
        P("section", None, None),
        P("section", None, None, None),
    )
    out_specs = (
        P("section", "dp", None),
        P("section", "dp", None),
        P("section", "dp", None),
        P("section", None, None, "dp"),
    )

    return jax.shard_map(shards, mesh=mesh, in_specs=in_specs, out_specs=out_specs, check_vma=False)
```

time: 84 us -> 97 us (1.15); the launches traced: 82.3 us -> 96.6 us
  waiting for transfers between devices: 8.93 us -> 46.3 us
  blocking collectives: 19.2 us -> 0 us
  local copies, waits for them, and re-layouts: 6.96 us -> 1.93 us
  starting transfers between devices: 16.5 us -> 20.4 us
  Pallas kernels: 29.8 us -> 27.2 us
    ppermute x1, waiting for transfers between devices: 0.01 us -> 28.1 us  [shards(): slow_1 = lax.ppermute(ahead, 'section', far)]
    all_to_all x2 -> x0, blocking collectives: 19.2 us -> none  [the longest x1 11.6 us: shards(): lax.all_to_all(packed, 'dp', 0, 0, axis_index_groups=y_groups, tiled=True)]
    ppermute x2, waiting for transfers between devices: 8.93 us -> 18.1 us  [the longest x1 18.1 us: shards(): slow_0 = lax.ppermute(slow, 'section', far)]
    all_to_all x0 -> x1, starting transfers between devices: none -> 5.66 us  [shards(): parts = lax.all_to_all(packed, 'dp', 0, 0, tiled=True)]
    unnamed x40 -> x4, local copies, waits for them, and re-layouts: 6.96 us -> 1.93 us
    pallas_call x6 -> x3, Pallas kernels: 27.6 us -> 25 us  [kernel(): pl.pallas_call(body, out_shape=outs, in_specs=[SMEM] + [ANY] * (len(opera...]
    ppermute x1, starting transfers between devices: 7.88 us -> 6.19 us  [shards(): slow_1 = lax.ppermute(ahead, 'section', far)]
  transfers between devices with their start and end apart: 4 -> 5, of which waited for: 1 -> 2; matrix products, arithmetic and copies ran while one was open for 0% -> 0% of each run, Pallas kernels for 12% -> 7%
where the time goes in v3:
time: 97 us; the launch traced here: 96.6 us
  waiting for transfers between devices  46.3 us (48%)
  Pallas kernels  27.2 us (28%)
  starting transfers between devices  20.4 us (21%)
  local copies, waits for them, and re-layouts  1.93 us (2%)
    ppermute x1, waiting for transfers between devices, shards(): slow_1 = lax.ppermute(ahead, 'section', far)  28.1 us
    pallas_call x3, Pallas kernels, kernel(): pl.pallas_call(body, out_shape=outs, in_specs=[SMEM] + [ANY] * (len(opera...  25 us
    ppermute x1, waiting for transfers between devices, shards(): slow_0 = lax.ppermute(slow, 'section', far)  18.1 us
    ppermute x1, starting transfers between devices, shards(): slow_0 = lax.ppermute(slow, 'section', far)  7.75 us
    ppermute x1, starting transfers between devices, shards(): slow_1 = lax.ppermute(ahead, 'section', far)  6.19 us
    all_to_all x1, starting transfers between devices, shards(): parts = lax.all_to_all(packed, 'dp', 0, 0, tiled=True)  5.66 us
    pallas_call x1, Pallas kernels, shards(): pl.pallas_call(functools.partial(final_kernel, columns, rows_each // 2, p...  2.21 us
  transfers between devices with their start and end apart: 5, of which 2 were waited for; matrix products, arithmetic and copies ran while one was open for 0% of the time, Pallas kernels for 7%

profile of v3, /device:TPU:39, one launch (start us, length us, event | category | flops | bytes accessed | tf_op | source)
XLA Modules:
  0.0 96.6 jit_solution(919692268211507285)
XLA Ops:
  0.6 10.0 %shard_map.165 = (f32[128,2048]{1,0:T(8,128)}, f32[128,2048]{1,0:T(8,128)}, f32[64,2048]{1,0:T(8,128)}, f32[64,384]{1,0:T(8,128)}) custom-call(s32[1,2]{1,0:T(1,128)} %plan.5, f32[128,2048]{1,0:T(8,128)} %bitcast.43, f32[128,2048]{1,0:T(8,128)} %bitcast.44, bf16[2,128,2048]{2,1,0:T(8,128)(2,1)} %examples.3, bf16[2,128,2048]{2,1,0:T(8,128)(2,1)} %bitcast.34, ...), custom_call_target="tpu_custom_call" | custom-call | flops 1912602624 | bytes 7659520 | tf_op jit(solution)/shard_map/pallas_call | solution.py:551
  10.6 0.8 collective-permute-start.1
  11.4 7.7 %collective-permute-start = (f32[128,2048]{1,0:T(8,128)}, f32[128,2048]{1,0:T(8,128)S(1)}, u32[]{:S(2)}, u32[]{:S(2)}) collective-permute-start(f32[128,2048]{1,0:T(8,128)} %get-tuple-element.22), channel_id=1, source_target_pairs={{16,32},{32,16},{48,64},{64,48},{80,96},{96,80},{112,128},{128,112... | collective-permute-start | bytes 3145736 | tf_op jit(solution)/shard_map/ppermute | solution.py:569
  19.1 0.0 collective-permute-done.1.arrived.near
  19.1 0.0 copy-start
  19.1 1.0 copy-done
  20.1 7.0 %shard_map.166 = (f32[128,2048]{1,0:T(8,128)}, f32[16,80,128]{2,1,0:T(8,128)}, f32[128,128]{1,0:T(8,128)}, bf16[128,2048]{1,0:T(8,128)(2,1)}, f32[128,128]{1,0:T...) custom-call(s32[1,2]{1,0:T(1,128)} %plan.5, f32[128,2048]{1,0:T(8,128)} %copy-done, ...), custom_call_target="tpu_custom_call" | custom-call | flops 1207959552 | bytes 7659520 | tf_op jit(solution)/shard_map/pallas_call | solution.py:551
  27.1 18.1 %collective-permute-done.arrived = f32[128,2048]{1,0:T(8,128)S(1)} collective-permute-done((f32[128,2048]{1,0:T(8,128)}, f32[128,2048]{1,0:T(8,128)S(1)}, u32[]{:S(2)}, u32[]{:S(2)}) %collective-permute-start) | collective-permute-done | bytes 1048608 | tf_op jit(solution)/shard_map/ppermute | solution.py:569
  45.2 0.0 copy-start.1
  45.2 1.0 %copy-done.1 = f32[128,2048]{1,0:T(8,128)} copy-done((f32[128,2048]{1,0:T(8,128)}, f32[128,2048]{1,0:T(8,128)S(1)}, u32[]{:S(2)}) %copy-start.1) | copy-done | bytes 1048600
  46.2 8.0 %shard_map.167 = (f32[128,2048]{1,0:T(8,128)}, f32[16,80,128]{2,1,0:T(8,128)}) custom-call(s32[1,2]{1,0:T(1,128)} %plan.5, f32[128,2048]{1,0:T(8,128)} %copy-done.1, f32[128,2048]{1,0:T(8,128)} %copy-done, f32[128,2048]{1,0:T(8,128)} %get-tuple-element.26.output, bf16[2,128,2048]{2,1,0:T(8,128)(2,1)} %examples.3, bf16[2,128,2048]{2,1,0:T(8,128)(2,1)} %bitcast.36, ...), custom_call_target="tpu_custom_call" | custom-call | flops 704643072 | bytes 7659520 | tf_op jit(solution)/shard_map/pallas_call | solution.py:551
  54.2 5.7 %all-to-all-start = ((f32[16,80,128]{2,1,0:T(8,128)}), f32[16,80,128]{2,1,0:T(8,128)S(1)}, u32[]{:S(2)}, u32[]{:S(2)}) async-start(f32[16,80,128]{2,1,0:T(8,128)} %get-tuple-element.34), calls=%async_computation | async-start | bytes 1310720 | tf_op jit(solution)/shard_map/all_to_all | solution.py:592
  59.9 0.0 collective-permute-start.3
  59.9 6.2 %collective-permute-start.2 = (f32[128,2048]{1,0:T(8,128)}, f32[128,2048]{1,0:T(8,128)S(1)}, u32[]{:S(2)}, u32[]{:S(2)}) collective-permute-start(f32[128,2048]{1,0:T(8,128)} %get-tuple-element.26.output), channel_id=1, source_target_pairs={{16,32},{32,16},{48,64},{64,48},{80,96},{96,80},{112,128},{128,112... | collective-permute-start | bytes 3145736 | tf_op jit(solution)/shard_map/ppermute | solution.py:581
  66.1 0.0 collective-permute-done.3.fast
  66.1 28.1 %collective-permute-done.2.slow = f32[128,2048]{1,0:T(8,128)S(1)} collective-permute-done((f32[128,2048]{1,0:T(8,128)}, f32[128,2048]{1,0:T(8,128)S(1)}, u32[]{:S(2)}, u32[]{:S(2)}) %collective-permute-start.2) | collective-permute-done | bytes 1048608 | tf_op jit(solution)/shard_map/ppermute | solution.py:581
  94.2 0.0 all-to-all-done.parts
  94.2 2.2 %sum_dp.1 = (f32[64,128]{1,0:T(8,128)}, f32[2,24,32]{2,1,0:T(8,128)}, f32[128,2048]{1,0:T(8,128)}, f32[128,2048]{1,0:T(8,128)}) custom-call(f32[16,80,128]{2,1,0:T(8,128)S(1)} %all-to-all-done.parts, f32[128,2048]{1,0:T(8,128)S(1)} %collective-permute-done.2.slow, f32[128,2048]{1,0:T(8,128)S(1)} %collective-permute-done.3.fast), custom_call_target="tpu_custom_call" | custom-call | tf_op jit(solution)/shard_map/sum_dp/pallas_call | solution.py:595
Async XLA Ops:
  10.6 8.5 %collective-permute-start.1 = (f32[128,2048]{1,0:T(8,128)}, f32[128,2048]{1,0:T(8,128)S(1)}, u32[]{:S(2)}, u32[]{:S(2)}) collective-permute-start(f32[128,2048]{1,0:T(8,128)} %get-tuple-element.23), channel_id=1, source_target_pairs={{0,16},{16,0},{32,48},{48,32},{64,80},{80,64},{96,112},{112,96},{1... | collective-permute-start | bytes 3145736 | tf_op jit(solution)/shard_map/ppermute | solution.py:570
  11.4 33.9 %collective-permute-start = (f32[128,2048]{1,0:T(8,128)}, f32[128,2048]{1,0:T(8,128)S(1)}, u32[]{:S(2)}, u32[]{:S(2)}) collective-permute-start(f32[128,2048]{1,0:T(8,128)} %get-tuple-element.22), channel_id=1, source_target_pairs={{16,32},{32,16},{48,64},{64,48},{80,96},{96,80},{112,128},{128,112... | collective-permute-start | bytes 3145736 | tf_op jit(solution)/shard_map/ppermute | solution.py:569
  19.1 1.0 %copy-start = (f32[128,2048]{1,0:T(8,128)}, f32[128,2048]{1,0:T(8,128)S(1)}, u32[]{:S(2)}) copy-start(f32[128,2048]{1,0:T(8,128)S(1)} %collective-permute-done.1.arrived.near) | copy-start | bytes 3145732
  45.2 1.0 %copy-start.1 = (f32[128,2048]{1,0:T(8,128)}, f32[128,2048]{1,0:T(8,128)S(1)}, u32[]{:S(2)}) copy-start(f32[128,2048]{1,0:T(8,128)S(1)} %collective-permute-done.arrived) | copy-start | bytes 3145732
  54.2 40.0 %all-to-all-start = ((f32[16,80,128]{2,1,0:T(8,128)}), f32[16,80,128]{2,1,0:T(8,128)S(1)}, u32[]{:S(2)}, u32[]{:S(2)}) async-start(f32[16,80,128]{2,1,0:T(8,128)} %get-tuple-element.34), calls=%async_computation | async-start | bytes 1310720 | tf_op jit(solution)/shard_map/all_to_all | solution.py:592
  59.9 6.2 %collective-permute-start.3 = (f32[128,2048]{1,0:T(8,128)}, f32[128,2048]{1,0:T(8,128)S(1)}, u32[]{:S(2)}, u32[]{:S(2)}) collective-permute-start(f32[128,2048]{1,0:T(8,128)} %get-tuple-element.35), channel_id=1, source_target_pairs={{0,16},{16,0},{32,48},{48,32},{64,80},{80,64},{96,112},{112,96},{1... | collective-permute-start | bytes 3145736 | tf_op jit(solution)/shard_map/ppermute | solution.py:593
  59.9 34.4 %collective-permute-start.2 = (f32[128,2048]{1,0:T(8,128)}, f32[128,2048]{1,0:T(8,128)S(1)}, u32[]{:S(2)}, u32[]{:S(2)}) collective-permute-start(f32[128,2048]{1,0:T(8,128)} %get-tuple-element.26.output), channel_id=1, source_target_pairs={{16,32},{32,16},{48,64},{64,48},{80,96},{96,80},{112,128},{128,112... | collective-permute-start | bytes 3145736 | tf_op jit(solution)/shard_map/ppermute | solution.py:581

commit v4 on v3

--- a/solution.py
+++ b/solution.py
@@ -110,6 +110,10 @@
     return copies
 
 
+SOON = ("gain", "router", "a", "b", "gate")
+THEN = ("up", "down")
+
+
 def primal_of(x, routes, copies, weights):
     gain_s, router, a_t, gate, up, factors = weights[:6]
     if copies is not None:
@@ -123,14 +127,18 @@
     return x_s[...] + weight * nn(hidden, down[...])
 
 
-def gradients(x_s, g_s, saved, weights, copies=None, x_wait=None):
+def gradients(x_s, g_s, saved, weights, copies=None, late=None):
     def ready(*names):
         if copies is not None:
             for name in names:
                 copies[name].wait()
 
     gain_s, router, a_t, gate, up, factors, down = weights
-    rstd, normed, share, weight, low, gate_pre, up_pre = saved
+    if late is None:
+        rstd, normed, share, weight, low, gate_pre, up_pre = saved
+    else:
+        share, gate_pre, up_pre = (saved[i][...] for i in (2, 4, 5))
+        weight = share[:, 0:1]
     sig = jax.nn.sigmoid(gate_pre)
     silu = gate_pre * sig
     hidden = (silu * up_pre).astype(BF16)
@@ -143,8 +151,8 @@
     d_gate = (d_hidden * up_pre * (sig * (1.0 + gate_pre * (1.0 - sig)))).astype(BF16)
     d_up = (d_hidden * silu).astype(BF16)
     ready("b", "gate", "up", "router", "a", "gain")
-    if x_wait is not None:
-        x_wait()
+    if late is not None:
+        rstd, normed, low = late()
     d_low_f = SCALE * jnp.concatenate([nt(d_gate, factors[0]), nt(d_up, factors[1])], axis=1)
     d_normed = (
         nt(d_gate, gate[...])
@@ -170,18 +178,23 @@
 
 def pack(packed, ga, gb):
     gb_t = gb.T
-    parts, size, width = packed.shape
-    rows = gb_t.shape[0] // parts
+    ys, _, width = packed.shape
+    zs = ga.shape[1] // (ys * width)
+    size = packed.shape[1] // zs
+    rows = gb_t.shape[0] // (ys * zs)
     tall = ga.shape[0]
     half = rows // 2
-    for p in range(parts):
-        packed[p, :tall, :] = ga[:, p * width : (p + 1) * width]
-        packed[p, tall : tall + half, :tall] = gb_t[p * rows : p * rows + half]
-        packed[p, tall : tall + half, tall:] = gb_t[p * rows + half : (p + 1) * rows]
-        packed[p, tall + half :, :] = jnp.zeros((size - tall - half, width), F32)
-
-
-FIRST_ORDER = ("gain", "router", "a", "b", "gate", "up", "down")
+    for y in range(ys):
+        for z in range(zs):
+            p = z * ys + y
+            at = z * size
+            packed[y, at : at + tall, :] = ga[:, p * width : (p + 1) * width]
+            at += tall
+            packed[y, at : at + half, :tall] = gb_t[p * rows : p * rows + half]
+            packed[y, at : at + half, tall:] = gb_t[p * rows + half : (p + 1) * rows]
+            packed[y, at + half : (z + 1) * size, :] = jnp.zeros((size - tall - half, width), F32)
+
+
 X1, X2, G, W, OUT = (pl.ds(0, 2), pl.ds(2, 2), pl.ds(4, 2), pl.ds(6, 7), pl.ds(13, 7))
 
 
@@ -203,7 +216,9 @@
         r_s,
         sems.at[X1],
     )
-    copies = fetch_weights(hbm, weights, FIRST_ORDER, sems.at[W])
+    copies = fetch_weights(hbm, weights, SOON, sems.at[W])
+    x_wait()
+    copies.update(fetch_weights(hbm, weights, THEN, sems.at[W]))
     x2_wait = fetch(
         [
             ((last,), arriving, mine),
@@ -218,7 +233,6 @@
     t_copy = pltpu.make_async_copy(examples.at[0], e_s, sems.at[5])
     pl.when(jnp.logical_not(last))(g_copy.start)
     pl.when(last)(t_copy.start)
-    x_wait()
     values = primal_of(x_s[...], r_s[...], copies, weights)
     copies["down"].wait()
     y_s[...] = output_of(x_s, values, weights[6])
@@ -265,61 +279,152 @@
         d_slow.wait()
 
 
+def keep(values, saved, saved_o, sems):
+    rstd, normed, share, _, low, gate_pre, up_pre = values
+    kept = (jnp.broadcast_to(rstd, saved[0].shape), normed, share, low, gate_pre, up_pre)
+    moves = []
+    for i, value in enumerate(kept):
+        saved[i][...] = value
+        moves.append(pltpu.make_async_copy(saved[i], saved_o[i], sems.at[i]))
+        moves[-1].start()
+    for move in moves:
+        move.wait()
+
+
+def recompute_kernel(tick, plan, stash, bwd_routes_t, *rest):
+    hbm, saved_o, rest = rest[:7], rest[7:13], rest[13:]
+    x_s, b_s, r_s, *rest = rest
+    saved, weights, sems = rest[:6], rest[6:13], rest[13]
+    slot = plan[0, tick]
+    x_wait = fetch(
+        [((slot >= 0,), stash.at[slot], bwd_routes_t.at[slot])], x_s, b_s, r_s, sems.at[X1]
+    )
+    copies = fetch_weights(hbm, weights, SOON, sems.at[W])
+    x_wait()
+    copies.update(fetch_weights(hbm, weights, ("up",), sems.at[W]))
+    keep(primal_of(x_s[...], r_s[...], copies, weights), saved, saved_o, sems.at[OUT])
+
+
+def backward_of_saved(hbm, weights, saved_cases, saved, g_cases, x_cases, refs, sums_in, sems):
+    x_s, g_s, b_s, e_s, ga_s, gb_s = refs
+    extra = sems.at[OUT]
+    early, late = (2, 4, 5), (0, 1, 3)
+    waits = []
+
+    def load(indices):
+        for predicates, source in saved_cases:
+            moves = [
+                pltpu.make_async_copy(source[i], saved[i], extra.at[1 + i]) for i in indices
+            ]
+            waits.append((predicates, moves))
+
+            @when_all(*predicates)
+            def _(moves=moves):
+                for move in moves:
+                    move.start()
+
+    def settle():
+        while waits:
+            predicates, moves = waits.pop()
+
+            @when_all(*predicates)
+            def _(moves=moves):
+                for move in moves:
+                    move.wait()
+
+    g_moves = []
+    for predicates, source, target in g_cases:
+        mine = [pltpu.make_async_copy(source, g_s, sems.at[4])]
+        if target is not None:
+            mine.append(pltpu.make_async_copy(target, e_s, sems.at[5]))
+        g_moves.append((predicates, mine))
+
+        @when_all(*predicates)
+        def _(mine=mine):
+            for move in mine:
+                move.start()
+
+    load(early)
+    copies = fetch_weights(hbm, weights, ("down",), sems.at[W])
+    settle()
+    for predicates, mine in g_moves:
+
+        @when_all(*predicates)
+        def _(mine=mine):
+            for move in mine:
+                move.wait()
+            if len(mine) > 1:
+                g_s[...] = g_s[...] - e_s[...].astype(F32)
+
+    copies.update(fetch_weights(hbm, weights, ("b", "gate", "up", "router", "a"), sems.at[W]))
+    load(late)
+    x_wait = fetch(x_cases, x_s, b_s, None, sems.at[X1])
+    copies.update(fetch_weights(hbm, weights, ("gain",), sems.at[W]))
+    sums = [
+        pltpu.make_async_copy(sums_in[0], ga_s, sems.at[2]),
+        pltpu.make_async_copy(sums_in[1], gb_s, sems.at[3]),
+    ]
+    for copy in sums:
+        copy.start()
+
+    def values():
+        settle()
+        x_wait()
+        return saved[0][:, 0:1], saved[1][...], saved[3][...]
+
+    result = gradients(x_s, g_s, saved, weights, copies, values)
+    for copy in sums:
+        copy.wait()
+    return result
+
+
 def second_kernel(
-    tick, mean_scale, plan, arrived, stash, fwd_routes_t, bwd_routes_t, ga_in, gb_in, *rest
+    tick,
+    mean_scale,
+    plan,
+    arrived,
+    stash,
+    fwd_routes_t,
+    ga_in,
+    gb_in,
+    *rest,
 ):
+    saved_in, rest = rest[:6], rest[6:]
     hbm, (sent, packed, *saved_o), rest = rest[:7], rest[7:15], rest[15:]
-    x_s, x2_s, y_s, b_s, b2_s, r_s, r2_s, ga_s, gb_s, packed_s, *rest = rest
+    x_s, g_s, y_s, b_s, e_s, r_s, ga_s, gb_s, packed_s, *rest = rest
     saved, weights, sems = rest[:6], rest[6:13], rest[13]
     odd, even, _, last = position()
-    slot = plan[0, tick]
-    mine = fwd_routes_t.at[tick]
-    stored = (stash.at[slot], bwd_routes_t.at[slot])
-    inner = jnp.logical_and(odd, jnp.logical_not(last))
-    x_wait = fetch([((odd,), arrived, mine), ((even,), *stored)], x_s, b_s, r_s, sems.at[X1])
-    copies = fetch_weights(hbm, weights, FIRST_ORDER, sems.at[W])
-    x2_wait = fetch(
-        [((last,), arrived, mine), ((inner,), *stored)], x2_s, b2_s, r2_s, sems.at[X2]
-    )
-    g_copies = [
-        pltpu.make_async_copy(arrived, x2_s, sems.at[4]),
-        pltpu.make_async_copy(ga_in, ga_s, sems.at[5]),
-        pltpu.make_async_copy(gb_in, gb_s, sems.at[20]),
-    ]
+    outs = sems.at[OUT]
+    y_copy = pltpu.make_async_copy(y_s, sent, outs.at[0])
+
+    @pl.when(odd)
+    def _():
+        x_wait = fetch([((odd,), arrived, fwd_routes_t.at[tick])], x_s, b_s, r_s, sems.at[X1])
+        copies = fetch_weights(hbm, weights, SOON, sems.at[W])
+        x_wait()
+        copies.update(fetch_weights(hbm, weights, THEN, sems.at[W]))
+        values = primal_of(x_s[...], r_s[...], copies, weights)
+        copies["down"].wait()
+        y_s[...] = output_of(x_s, values, weights[6])
+        y_copy.start()
+
+        @pl.when(last)
+        def _():
+            keep(values, saved, saved_o, sems.at[pl.ds(14, 6)])
 
     @pl.when(even)
     def _():
-        for copy in g_copies:
-            copy.start()
-
-    x_wait()
-    values = primal_of(x_s[...], r_s[...], copies, weights)
-    copies["down"].wait()
-    outs = sems.at[OUT]
-    y_copy = pltpu.make_async_copy(y_s, sent, outs.at[0])
-
-    @pl.when(odd)
-    def _():
-        y_s[...] = output_of(x_s, values, weights[6])
-        y_copy.start()
-        x2_wait()
-        rstd, normed, share, _, low, gate_pre, up_pre = primal_of(
-            x2_s[...], r2_s[...], None, weights
+        dx, ga, gb = backward_of_saved(
+            hbm,
+            weights,
+            [((even,), saved_in)],
+            saved,
+            [((even,), arrived, None)],
+            [((even,), stash.at[plan[0, tick]], None)],
+            (x_s, g_s, b_s, e_s, ga_s, gb_s),
+            (ga_in, gb_in),
+            sems,
         )
-        kept = (jnp.broadcast_to(rstd, saved[0].shape), normed, share, low, gate_pre, up_pre)
-        moves = []
-        for i, value in enumerate(kept):
-            saved[i][...] = value
-            moves.append(pltpu.make_async_copy(saved[i], saved_o[i], outs.at[1 + i]))
-            moves[-1].start()
-        for move in moves:
-            move.wait()
-
-    @pl.when(even)
-    def _():
-        for copy in g_copies:
-            copy.wait()
-        dx, ga, gb = gradients(x_s, x2_s, values, weights)
         y_s[...] = dx
         y_copy.start()
         factor = normalizer(ga, gb, mean_scale)
@@ -346,7 +451,7 @@
     gb_in,
     *rest,
 ):
-    saved_in, rest = rest[:6], rest[6:]
+    saved_in, last_in, rest = rest[:6], rest[6:12], rest[12:]
     hbm, (sent, packed), rest = rest[:7], rest[7:9], rest[9:]
     x_s, g_s, y_s, b_s, e_s, r_s, ga_s, gb_s, packed_s, *rest = rest
     saved, weights, sems = rest[:6], rest[6:13], rest[13]
@@ -354,7 +459,7 @@
     inner = jnp.logical_and(odd, jnp.logical_not(last))
     outs = sems.at[OUT]
     y_copy = pltpu.make_async_copy(y_s, sent, outs.at[0])
-    p_copy = pltpu.make_async_copy(packed_s, packed, outs.at[1])
+    p_copy = pltpu.make_async_copy(packed_s, packed, sems.at[20])
 
     @pl.when(even)
     def _():
@@ -369,72 +474,43 @@
             r_s,
             sems.at[X1],
         )
-        copies = fetch_weights(hbm, weights, FIRST_ORDER, sems.at[W])
-        keep = pltpu.make_async_copy(packed_in, packed_s, sems.at[4])
-        keep.start()
+        copies = fetch_weights(hbm, weights, SOON, sems.at[W])
         x_wait()
+        copies.update(fetch_weights(hbm, weights, THEN, sems.at[W]))
+        hold = pltpu.make_async_copy(packed_in, packed_s, sems.at[4])
+        hold.start()
         values = primal_of(x_s[...], r_s[...], copies, weights)
         copies["down"].wait()
-        keep.wait()
+        hold.wait()
         p_copy.start()
         y_s[...] = output_of(x_s, values, weights[6])
         y_copy.start()
 
     @pl.when(odd)
     def _():
-        g_copy = pltpu.make_async_copy(arrived, g_s, sems.at[4])
-        o_copy = pltpu.make_async_copy(output, g_s, sems.at[4])
-        t_copy = pltpu.make_async_copy(examples.at[tick], e_s, sems.at[5])
-        pl.when(inner)(g_copy.start)
-
-        @pl.when(last)
-        def _():
-            o_copy.start()
-            t_copy.start()
-
-        moves = [pltpu.make_async_copy(saved_in[i], saved[i], outs.at[1 + i]) for i in range(6)]
-        for i in (2, 4, 5):
-            moves[i].start()
-        copies = fetch_weights(hbm, weights, ("down", "b", "gate", "up"), sems.at[W])
-        for i in (0, 1, 3):
-            moves[i].start()
-        x_wait = fetch(
+        dx, ga, gb = backward_of_saved(
+            hbm,
+            weights,
+            [((last,), last_in), ((inner,), saved_in)],
+            saved,
+            [((last,), output, examples.at[tick]), ((inner,), arrived, None)],
             [((last,), near, None), ((inner,), stash.at[plan[0, tick]], None)],
-            x_s,
-            b_s,
-            None,
-            sems.at[X1],
+            (x_s, g_s, b_s, e_s, ga_s, gb_s),
+            (ga_in, gb_in),
+            sems,
         )
-        copies.update(fetch_weights(hbm, weights, ("router", "a", "gain"), sems.at[W]))
-        sums = [
-            pltpu.make_async_copy(ga_in, ga_s, sems.at[2]),
-            pltpu.make_async_copy(gb_in, gb_s, sems.at[3]),
-        ]
-        for copy in sums:
-            copy.start()
-        for move in moves:
-            move.wait()
-        pl.when(inner)(g_copy.wait)
-
-        @pl.when(last)
-        def _():
-            o_copy.wait()
-            t_copy.wait()
-            g_s[...] = g_s[...] - e_s[...].astype(F32)
-
-        rstd, normed, share, low, gate_pre, up_pre = (ref[...] for ref in saved)
-        values = (rstd[:, 0:1], normed, share, share[:, 0:1], low, gate_pre, up_pre)
-        dx, ga, gb = gradients(x_s, g_s, values, weights, copies, x_wait)
         y_s[...] = dx
         y_copy.start()
         factor = normalizer(ga, gb, mean_scale)
-        for copy in sums:
-            copy.wait()
         pack(packed_s, ga_s[...] + factor * ga, gb_s[...] + factor * gb)
         p_copy.start()
 
     y_copy.wait()
     p_copy.wait()
+
+
+def sum_kernel(parts, total):
+    total[...] = jnp.sum(parts[...], axis=0).reshape(total.shape)
 
 
 def final_kernel(tall, half, pieces, parts, slow, fast, ga, gb, acts_o, grads_o, slow_s, fast_s, sems):
@@ -480,6 +556,7 @@
 
 
 def shards(
+    y_size,
     examples,
     arriving,
     returning,
@@ -496,6 +573,7 @@
     up_factors,
 ):
     replicas = lax.axis_size("dp")
+    z_size = replicas // y_size
     ticks, tokens, width = examples.shape
     mean_scale = 1.0 / (ticks * replicas)
     gain, router, gate, up, down = (
@@ -530,7 +608,7 @@
         jax.ShapeDtypeStruct((columns, width), F32),
         jax.ShapeDtypeStruct((columns, hidden_units), F32),
     )
-    packed_shape = jax.ShapeDtypeStruct((replicas, size, share_width), F32)
+    packed_shape = jax.ShapeDtypeStruct((y_size, z_size * size, share_width), F32)
     saved_shape = (
         jax.ShapeDtypeStruct((tokens, 128), F32),
         jax.ShapeDtypeStruct((tokens, width), BF16),
@@ -554,6 +632,7 @@
             in_specs=[SMEM] + [ANY] * (len(operands) - 1),
             out_specs=(ANY,) * len(outs),
             scratch_shapes=[*rooms, *scratch, semaphores],
+            compiler_params=pltpu.CompilerParams(vmem_limit_bytes=67043328),
             cost_estimate=pl.CostEstimate(
                 flops=flops, bytes_accessed=weight_bytes + 8 * tokens * width, transcendentals=0
             ),
@@ -568,15 +647,22 @@
     )
     slow_0 = lax.ppermute(slow, "section", far)
     fast_0 = lax.ppermute(fast, "section", near)
-    ahead, packed, *saved = kernel(
+    saved = kernel(
+        functools.partial(recompute_kernel, 1),
+        primal_flops,
+        saved_shape,
+        [x_scratch, b_scratch, r_scratch] + rooms(saved_shape),
+        (plan, stash, bwd_routes_t, *weights),
+    )
+    ahead, packed, *last_saved = kernel(
         functools.partial(second_kernel, 1, mean_scale),
-        2 * primal_flops + down_flops,
+        primal_flops + down_flops,
         (activation, packed_shape, *saved_shape),
         [x_scratch] * 3
         + [b_scratch] * 2
-        + [r_scratch] * 2
+        + [r_scratch]
         + rooms((*sums_shape, packed_shape, *saved_shape)),
-        (plan, fast_0, stash, fwd_routes_t, bwd_routes_t, *sums, *weights),
+        (plan, fast_0, stash, fwd_routes_t, *sums, *saved, *weights),
     )
     slow_1 = lax.ppermute(ahead, "section", far)
     sent, packed = kernel(
@@ -587,10 +673,34 @@
         + [b_scratch] * 2
         + [r_scratch]
         + rooms((*sums_shape, packed_shape, *saved_shape)),
-        (plan, slow_0, fast_0, ahead, examples, stash, fwd_routes_t, packed, *sums, *saved, *weights),
-    )
-    parts = lax.all_to_all(packed, "dp", 0, 0, tiled=True)
+        (
+            plan,
+            slow_0,
+            fast_0,
+            ahead,
+            examples,
+            stash,
+            fwd_routes_t,
+            packed,
+            *sums,
+            *saved,
+            *last_saved,
+            *weights,
+        ),
+    )
     fast_1 = lax.ppermute(sent, "section", near)
+    y_groups = [[z * y_size + y for y in range(y_size)] for z in range(z_size)]
+    z_groups = [[z * y_size + y for z in range(z_size)] for y in range(y_size)]
+    parts = lax.all_to_all(packed, "dp", 0, 0, axis_index_groups=y_groups, tiled=True)
+    parts = pl.pallas_call(
+        sum_kernel,
+        out_shape=jax.ShapeDtypeStruct((z_size, size, share_width), F32),
+        in_specs=[VMEM],
+        out_specs=VMEM,
+        compiler_params=pltpu.CompilerParams(vmem_limit_bytes=8 << 20),
+        name="sum_y",
+    )(parts)
+    parts = lax.all_to_all(parts, "dp", 0, 0, axis_index_groups=z_groups, tiled=True)
     pieces = 4
     share_a, share_b, next_acts, next_grads = pl.pallas_call(
         functools.partial(final_kernel, columns, rows_each // 2, pieces),
@@ -638,4 +748,9 @@
         P("section", None, None, "dp"),
     )
 
-    return jax.shard_map(shards, mesh=mesh, in_specs=in_specs, out_specs=out_specs, check_vma=False)
+    def body(*args):
+        return shards(4, *args)
+
+    return jax.shard_map(
+        body, mesh=mesh, in_specs=in_specs, out_specs=out_specs, check_vma=False
+    )

time: 97 us -> 83.8 us (0.86); the launches traced: 96.6 us -> 82.2 us
  waiting for transfers between devices: 46.3 us -> 15.1 us
  blocking collectives: 0 us -> 21.2 us
  starting transfers between devices: 20.4 us -> 14 us
  Pallas kernels: 27.2 us -> 31.2 us
  local copies, waits for them, and re-layouts: 1.93 us -> 0 us
    ppermute x1, waiting for transfers between devices: 28.1 us -> 0.01 us  [shards(): slow_1 = lax.ppermute(ahead, 'section', far)]
    all_to_all x0 -> x2, blocking collectives: none -> 21.2 us  [the longest x1 13.1 us: shards(): lax.all_to_all(packed, 'dp', 0, 0, axis_index_groups=y_groups, tiled=True)]
    all_to_all x1 -> x0, starting transfers between devices: 5.66 us -> none  [shards(): parts = lax.all_to_all(packed, 'dp', 0, 0, tiled=True)]
    pallas_call x3 -> x4, Pallas kernels: 25 us -> 28.9 us  [kernel(): pl.pallas_call(body, out_shape=outs, in_specs=[SMEM] + [ANY] * (len(opera...]
    ppermute x1, waiting for transfers between devices: 18.1 us -> 15.1 us  [shards(): slow_0 = lax.ppermute(slow, 'section', far)]
    unnamed x4 -> x0, local copies, waits for them, and re-layouts: 1.93 us -> none
  transfers between devices with their start and end apart: 5 -> 4, of which waited for: 2 -> 1; matrix products, arithmetic and copies ran while one was open for 0% -> 0% of each run, Pallas kernels for 7% -> 13%
where the time goes in v4:
time: 83.8 us; the launch traced here: 82.2 us
  Pallas kernels  31.2 us (37%)
  blocking collectives  21.2 us (25%)
  waiting for transfers between devices  15.1 us (18%)
  starting transfers between devices  14 us (17%)
  between operations  0.86 us (1%)
    pallas_call x4, Pallas kernels, kernel(): pl.pallas_call(body, out_shape=outs, in_specs=[SMEM] + [ANY] * (len(opera...  28.9 us
    ppermute x1, waiting for transfers between devices, shards(): slow_0 = lax.ppermute(slow, 'section', far)  15.1 us
    all_to_all x1, blocking collectives, shards(): lax.all_to_all(packed, 'dp', 0, 0, axis_index_groups=y_groups, tiled=True)  13.1 us
    all_to_all x1, blocking collectives, shards(): lax.all_to_all(parts, 'dp', 0, 0, axis_index_groups=z_groups, tiled=True)  8.03 us
    ppermute x1, starting transfers between devices, shards(): slow_0 = lax.ppermute(slow, 'section', far)  7.75 us
    ppermute x1, starting transfers between devices, shards(): slow_1 = lax.ppermute(ahead, 'section', far)  5.38 us
    pallas_call x1, Pallas kernels, shards(): pl.pallas_call(functools.partial(final_kernel, columns, rows_each // 2, p...  2.22 us
  transfers between devices with their start and end apart: 4, of which 1 were waited for; matrix products, arithmetic and copies ran while one was open for 0% of the time, Pallas kernels for 13%

profile of v4, /device:TPU:39, one launch (start us, length us, event | category | flops | bytes accessed | tf_op | source)
XLA Modules:
  0.0 82.2 jit_solution(6411707620799350711)
XLA Ops:
  0.6 10.0 %shard_map.165 = (f32[128,2048]{1,0:T(8,128)}, f32[128,2048]{1,0:T(8,128)}, f32[64,2048]{1,0:T(8,128)}, f32[64,384]{1,0:T(8,128)}) custom-call(s32[1,2]{1,0:T(1,128)} %plan.7, f32[128,2048]{1,0:T(8,128)} %bitcast.49, f32[128,2048]{1,0:T(8,128)} %bitcast.50, bf16[2,128,2048]{2,1,0:T(8,128)(2,1)} %examples.3, bf16[2,128,2048]{2,1,0:T(8,128)(2,1)} %bitcast.37, ...), custom_call_target="tpu_custom_call" | custom-call | flops 1912602624 | bytes 7659520 | tf_op jit(solution)/shard_map/pallas_call | solution.py:629
  10.6 0.8 collective-permute-start.1
  11.4 7.8 %collective-permute-start = (f32[128,2048]{1,0:T(8,128)}, f32[128,2048]{1,0:T(8,128)}, u32[]{:S(2)}, u32[]{:S(2)}) collective-permute-start(f32[128,2048]{1,0:T(8,128)} %get-tuple-element.28), channel_id=1, source_target_pairs={{16,32},{32,16},{48,64},{64,48},{80,96},{96,80},{112,128},{128,112... | collective-permute-start | bytes 3145736 | tf_op jit(solution)/shard_map/ppermute | solution.py:648
  19.1 5.1 %shard_map.166 = (f32[128,128]{1,0:T(8,128)}, bf16[128,2048]{1,0:T(8,128)(2,1)}, f32[128,128]{1,0:T(8,128)}, bf16[128,64]{1,0:T(8,128)(2,1)}, f32[128,384]{1,0:T(8,128)}, /*index=5*/f32[128,384]{1,0:T(8,128)}) custom-call(s32[1,2]{1,0:T(1,128)} %plan.7, bf16[2,128,2048]{2,1,0:T(8,128)(2,1)} %bitcast.38, s32[2,8,128]{2,1,0:T(8,128)} %bitcast.59, ...), custom_call_target="tpu_custom_call" | custom-call | flops 503316480 | bytes 7659520 | tf_op jit(solution)/shard_map/pallas_call | solution.py:629
  24.2 0.0 collective-permute-done.1.arrived.near
  24.3 5.7 %shard_map.167 = (f32[128,2048]{1,0:T(8,128)}, f32[4,320,128]{2,1,0:T(8,128)}, f32[128,128]{1,0:T(8,128)}, bf16[128,2048]{1,0:T(8,128)(2,1)}, f32[128,128]{1,0:T...) custom-call(s32[1,2]{1,0:T(1,128)} %plan.7, ...), custom_call_target="tpu_custom_call" | custom-call | flops 704643072 | bytes 7659520 | tf_op jit(solution)/shard_map/pallas_call | solution.py:629
  30.0 15.1 %collective-permute-done.arrived = f32[128,2048]{1,0:T(8,128)} collective-permute-done((f32[128,2048]{1,0:T(8,128)}, f32[128,2048]{1,0:T(8,128)}, u32[]{:S(2)}, u32[]{:S(2)}) %collective-permute-start) | collective-permute-done | bytes 1048608 | tf_op jit(solution)/shard_map/ppermute | solution.py:648
  45.0 8.1 %shard_map.168 = (f32[128,2048]{1,0:T(8,128)}, f32[4,320,128]{2,1,0:T(8,128)}) custom-call(s32[1,2]{1,0:T(1,128)} %plan.7, f32[128,2048]{1,0:T(8,128)} %collective-permute-done.arrived, f32[128,2048]{1,0:T(8,128)} %collective-permute-done.1.arrived.near, f32[128,2048]{1,0:T(8,128)} %get-tuple-element.38.output, bf16[2,128,2048]{2,1,0:T(8,128)(2,1)} %examples.3, ...), custom_call_target="tpu_custom_call" | custom-call | flops 704643072 | bytes 7659520 | tf_op jit(solution)/shard_map/pallas_call | solution.py:629
  53.2 0.1 collective-permute-start.3
  53.3 5.4 %collective-permute-start.2 = (f32[128,2048]{1,0:T(8,128)}, f32[128,2048]{1,0:T(8,128)S(1)}, u32[]{:S(2)}, u32[]{:S(2)}) collective-permute-start(f32[128,2048]{1,0:T(8,128)} %get-tuple-element.38.output), channel_id=1, source_target_pairs={{16,32},{32,16},{48,64},{64,48},{80,96},{96,80},{112,128},{128,112... | collective-permute-start | bytes 3145736 | tf_op jit(solution)/shard_map/ppermute | solution.py:667
  58.7 13.1 %all_to_all.10.parts = f32[4,320,128]{2,1,0:T(8,128)S(1)} all-to-all(f32[4,320,128]{2,1,0:T(8,128)} %get-tuple-element.46), channel_id=1, replica_groups={{0,1,2,3},{4,5,6,7},{8,9,10,11},{12,13,14,15},{16,17,18,19},{20,21,22,2..., dimensions={0} | all-to-all | bytes 1310720 | tf_op jit(solution)/shard_map/all_to_all | solution.py:694
  71.8 8.0 %all_to_all.11.parts = f32[4,80,128]{2,1,0:T(8,128)S(1)} all-to-all(f32[4,80,128]{2,1,0:T(8,128)S(1)} %sum_y.1), channel_id=1, replica_groups={{0,4,8,12},{1,5,9,13},{2,6,10,14},{3,7,11,15},{16,20,24,28},{17,21,25,2..., dimensions={0} | all-to-all | bytes 327680 | tf_op jit(solution)/shard_map/all_to_all | solution.py:703
  79.9 0.0 collective-permute-done.3.fast
  79.9 0.0 collective-permute-done.2.slow
  79.9 2.2 %sum_dp.1 = (f32[64,128]{1,0:T(8,128)}, f32[2,24,32]{2,1,0:T(8,128)}, f32[128,2048]{1,0:T(8,128)}, f32[128,2048]{1,0:T(8,128)}) custom-call(f32[4,80,128]{2,1,0:T(8,128)S(1)} %all_to_all.11.parts, f32[128,2048]{1,0:T(8,128)S(1)} %collective-permute-done.2.slow, f32[128,2048]{1,0:T(8,128)S(1)} %collective-permute-done.3.fast), custom_call_target="tpu_custom_call" | custom-call | tf_op jit(solution)/shard_map/sum_dp/pallas_call | solution.py:705
  (1 shorter events, 0.0 us)
Async XLA Ops:
  10.6 13.6 %collective-permute-start.1 = (f32[128,2048]{1,0:T(8,128)}, f32[128,2048]{1,0:T(8,128)}, u32[]{:S(2)}, u32[]{:S(2)}) collective-permute-start(f32[128,2048]{1,0:T(8,128)} %get-tuple-element.29), channel_id=1, source_target_pairs={{0,16},{16,0},{32,48},{48,32},{64,80},{80,64},{96,112},{112,96},{1... | collective-permute-start | bytes 3145736 | tf_op jit(solution)/shard_map/ppermute | solution.py:649
  11.4 33.7 %collective-permute-start = (f32[128,2048]{1,0:T(8,128)}, f32[128,2048]{1,0:T(8,128)}, u32[]{:S(2)}, u32[]{:S(2)}) collective-permute-start(f32[128,2048]{1,0:T(8,128)} %get-tuple-element.28), channel_id=1, source_target_pairs={{16,32},{32,16},{48,64},{64,48},{80,96},{96,80},{112,128},{128,112... | collective-permute-start | bytes 3145736 | tf_op jit(solution)/shard_map/ppermute | solution.py:648
  53.2 26.7 %collective-permute-start.3 = (f32[128,2048]{1,0:T(8,128)}, f32[128,2048]{1,0:T(8,128)S(1)}, u32[]{:S(2)}, u32[]{:S(2)}) collective-permute-start(f32[128,2048]{1,0:T(8,128)} %get-tuple-element.47), channel_id=1, source_target_pairs={{0,16},{16,0},{32,48},{48,32},{64,80},{80,64},{96,112},{112,96},{1... | collective-permute-start | bytes 3145736 | tf_op jit(solution)/shard_map/ppermute | solution.py:691
  53.3 26.6 %collective-permute-start.2 = (f32[128,2048]{1,0:T(8,128)}, f32[128,2048]{1,0:T(8,128)S(1)}, u32[]{:S(2)}, u32[]{:S(2)}) collective-permute-start(f32[128,2048]{1,0:T(8,128)} %get-tuple-element.38.output), channel_id=1, source_target_pairs={{16,32},{32,16},{48,64},{64,48},{80,96},{96,80},{112,128},{128,112... | collective-permute-start | bytes 3145736 | tf_op jit(solution)/shard_map/ppermute | solution.py:667

commit v5 on v3

--- a/solution.py
+++ b/solution.py
@@ -123,14 +123,18 @@
     return x_s[...] + weight * nn(hidden, down[...])
 
 
-def gradients(x_s, g_s, saved, weights, copies=None, x_wait=None):
+def gradients(x_s, g_s, saved, weights, copies=None, late=None):
     def ready(*names):
         if copies is not None:
             for name in names:
                 copies[name].wait()
 
     gain_s, router, a_t, gate, up, factors, down = weights
-    rstd, normed, share, weight, low, gate_pre, up_pre = saved
+    if late is None:
+        rstd, normed, share, weight, low, gate_pre, up_pre = saved
+    else:
+        share, gate_pre, up_pre = (saved[i][...] for i in (2, 4, 5))
+        weight = share[:, 0:1]
     sig = jax.nn.sigmoid(gate_pre)
     silu = gate_pre * sig
     hidden = (silu * up_pre).astype(BF16)
@@ -143,8 +147,8 @@
     d_gate = (d_hidden * up_pre * (sig * (1.0 + gate_pre * (1.0 - sig)))).astype(BF16)
     d_up = (d_hidden * silu).astype(BF16)
     ready("b", "gate", "up", "router", "a", "gain")
-    if x_wait is not None:
-        x_wait()
+    if late is not None:
+        rstd, normed, low = late()
     d_low_f = SCALE * jnp.concatenate([nt(d_gate, factors[0]), nt(d_up, factors[1])], axis=1)
     d_normed = (
         nt(d_gate, gate[...])
@@ -170,15 +174,21 @@
 
 def pack(packed, ga, gb):
     gb_t = gb.T
-    parts, size, width = packed.shape
-    rows = gb_t.shape[0] // parts
+    ys, _, width = packed.shape
+    zs = ga.shape[1] // (ys * width)
+    size = packed.shape[1] // zs
+    rows = gb_t.shape[0] // (ys * zs)
     tall = ga.shape[0]
     half = rows // 2
-    for p in range(parts):
-        packed[p, :tall, :] = ga[:, p * width : (p + 1) * width]
-        packed[p, tall : tall + half, :tall] = gb_t[p * rows : p * rows + half]
-        packed[p, tall : tall + half, tall:] = gb_t[p * rows + half : (p + 1) * rows]
-        packed[p, tall + half :, :] = jnp.zeros((size - tall - half, width), F32)
+    for y in range(ys):
+        for z in range(zs):
+            p = z * ys + y
+            at = z * size
+            packed[y, at : at + tall, :] = ga[:, p * width : (p + 1) * width]
+            at += tall
+            packed[y, at : at + half, :tall] = gb_t[p * rows : p * rows + half]
+            packed[y, at : at + half, tall:] = gb_t[p * rows + half : (p + 1) * rows]
+            packed[y, at + half : (z + 1) * size, :] = jnp.zeros((size - tall - half, width), F32)
 
 
 FIRST_ORDER = ("gain", "router", "a", "b", "gate", "up", "down")
@@ -265,8 +275,15 @@
         d_slow.wait()
 
 
+def fill_kernel(gain, token, gain_s, sem):
+    copy = pltpu.make_async_copy(gain, gain_s, sem)
+    copy.start()
+    copy.wait()
+    token[...] = jnp.broadcast_to(gain_s[:, :128], token.shape)
+
+
 def second_kernel(
-    tick, mean_scale, plan, arrived, stash, fwd_routes_t, bwd_routes_t, ga_in, gb_in, *rest
+    tick, mean_scale, plan, arrived, after, stash, fwd_routes_t, bwd_routes_t, ga_in, gb_in, *rest
 ):
     hbm, (sent, packed, *saved_o), rest = rest[:7], rest[7:15], rest[15:]
     x_s, x2_s, y_s, b_s, b2_s, r_s, r2_s, ga_s, gb_s, packed_s, *rest = rest
@@ -354,7 +371,7 @@
     inner = jnp.logical_and(odd, jnp.logical_not(last))
     outs = sems.at[OUT]
     y_copy = pltpu.make_async_copy(y_s, sent, outs.at[0])
-    p_copy = pltpu.make_async_copy(packed_s, packed, outs.at[1])
+    p_copy = pltpu.make_async_copy(packed_s, packed, sems.at[20])
 
     @pl.when(even)
     def _():
@@ -395,7 +412,7 @@
         moves = [pltpu.make_async_copy(saved_in[i], saved[i], outs.at[1 + i]) for i in range(6)]
         for i in (2, 4, 5):
             moves[i].start()
-        copies = fetch_weights(hbm, weights, ("down", "b", "gate", "up"), sems.at[W])
+        copies = fetch_weights(hbm, weights, ("down", "gate", "up", "b", "router", "a"), sems.at[W])
         for i in (0, 1, 3):
             moves[i].start()
         x_wait = fetch(
@@ -405,15 +422,15 @@
             None,
             sems.at[X1],
         )
-        copies.update(fetch_weights(hbm, weights, ("router", "a", "gain"), sems.at[W]))
+        copies.update(fetch_weights(hbm, weights, ("gain",), sems.at[W]))
         sums = [
             pltpu.make_async_copy(ga_in, ga_s, sems.at[2]),
             pltpu.make_async_copy(gb_in, gb_s, sems.at[3]),
         ]
         for copy in sums:
             copy.start()
-        for move in moves:
-            move.wait()
+        for i in (2, 4, 5):
+            moves[i].wait()
         pl.when(inner)(g_copy.wait)
 
         @pl.when(last)
@@ -422,9 +439,13 @@
             t_copy.wait()
             g_s[...] = g_s[...] - e_s[...].astype(F32)
 
-        rstd, normed, share, low, gate_pre, up_pre = (ref[...] for ref in saved)
-        values = (rstd[:, 0:1], normed, share, share[:, 0:1], low, gate_pre, up_pre)
-        dx, ga, gb = gradients(x_s, g_s, values, weights, copies, x_wait)
+        def late():
+            for i in (0, 1, 3):
+                moves[i].wait()
+            x_wait()
+            return saved[0][:, 0:1], saved[1][...], saved[3][...]
+
+        dx, ga, gb = gradients(x_s, g_s, saved, weights, copies, late)
         y_s[...] = dx
         y_copy.start()
         factor = normalizer(ga, gb, mean_scale)
@@ -435,6 +456,10 @@
 
     y_copy.wait()
     p_copy.wait()
+
+
+def sum_kernel(parts, total):
+    total[...] = jnp.sum(parts[...], axis=0).reshape(total.shape)
 
 
 def final_kernel(tall, half, pieces, parts, slow, fast, ga, gb, acts_o, grads_o, slow_s, fast_s, sems):
@@ -480,6 +505,7 @@
 
 
 def shards(
+    y_size,
     examples,
     arriving,
     returning,
@@ -496,6 +522,7 @@
     up_factors,
 ):
     replicas = lax.axis_size("dp")
+    z_size = replicas // y_size
     ticks, tokens, width = examples.shape
     mean_scale = 1.0 / (ticks * replicas)
     gain, router, gate, up, down = (
@@ -530,7 +557,7 @@
         jax.ShapeDtypeStruct((columns, width), F32),
         jax.ShapeDtypeStruct((columns, hidden_units), F32),
     )
-    packed_shape = jax.ShapeDtypeStruct((replicas, size, share_width), F32)
+    packed_shape = jax.ShapeDtypeStruct((y_size, z_size * size, share_width), F32)
     saved_shape = (
         jax.ShapeDtypeStruct((tokens, 128), F32),
         jax.ShapeDtypeStruct((tokens, width), BF16),
@@ -554,6 +581,7 @@
             in_specs=[SMEM] + [ANY] * (len(operands) - 1),
             out_specs=(ANY,) * len(outs),
             scratch_shapes=[*rooms, *scratch, semaphores],
+            compiler_params=pltpu.CompilerParams(vmem_limit_bytes=67043328),
             cost_estimate=pl.CostEstimate(
                 flops=flops, bytes_accessed=weight_bytes + 8 * tokens * width, transcendentals=0
             ),
@@ -568,6 +596,16 @@
     )
     slow_0 = lax.ppermute(slow, "section", far)
     fast_0 = lax.ppermute(fast, "section", near)
+    whole = pltpu.CompilerParams(vmem_limit_bytes=67043328)
+    token = pl.pallas_call(
+        fill_kernel,
+        out_shape=jax.ShapeDtypeStruct((8, 128), F32),
+        in_specs=[ANY],
+        out_specs=VMEM,
+        scratch_shapes=[pltpu.VMEM(gain.shape, F32), pltpu.SemaphoreType.DMA],
+        compiler_params=whole,
+        name="fill",
+    )(gain)
     ahead, packed, *saved = kernel(
         functools.partial(second_kernel, 1, mean_scale),
         2 * primal_flops + down_flops,
@@ -576,7 +614,7 @@
         + [b_scratch] * 2
         + [r_scratch] * 2
         + rooms((*sums_shape, packed_shape, *saved_shape)),
-        (plan, fast_0, stash, fwd_routes_t, bwd_routes_t, *sums, *weights),
+        (plan, fast_0, token, stash, fwd_routes_t, bwd_routes_t, *sums, *weights),
     )
     slow_1 = lax.ppermute(ahead, "section", far)
     sent, packed = kernel(
@@ -589,8 +627,20 @@
         + rooms((*sums_shape, packed_shape, *saved_shape)),
         (plan, slow_0, fast_0, ahead, examples, stash, fwd_routes_t, packed, *sums, *saved, *weights),
     )
-    parts = lax.all_to_all(packed, "dp", 0, 0, tiled=True)
+    y_groups = [[z * y_size + y for y in range(y_size)] for z in range(z_size)]
+    z_groups = [[z * y_size + y for z in range(z_size)] for y in range(y_size)]
+    parts = lax.all_to_all(packed, "dp", 0, 0, axis_index_groups=y_groups, tiled=True)
     fast_1 = lax.ppermute(sent, "section", near)
+    parts = pl.pallas_call(
+        sum_kernel,
+        out_shape=jax.ShapeDtypeStruct((z_size, size, share_width), F32),
+        in_specs=[VMEM],
+        out_specs=VMEM,
+        compiler_params=pltpu.CompilerParams(vmem_limit_bytes=8 << 20),
+        name="sum_y",
+    )(parts)
+    parts, slow_1 = lax.optimization_barrier((parts, slow_1))
+    parts = lax.all_to_all(parts, "dp", 0, 0, axis_index_groups=z_groups, tiled=True)
     pieces = 4
     share_a, share_b, next_acts, next_grads = pl.pallas_call(
         functools.partial(final_kernel, columns, rows_each // 2, pieces),
@@ -638,4 +688,9 @@
         P("section", None, None, "dp"),
     )
 
-    return jax.shard_map(shards, mesh=mesh, in_specs=in_specs, out_specs=out_specs, check_vma=False)
+    def body(*args):
+        return shards(4, *args)
+
+    return jax.shard_map(
+        body, mesh=mesh, in_specs=in_specs, out_specs=out_specs, check_vma=False
+    )

time: 97 us -> 93.1 us (0.960)
  the two profiles are of different devices: /device:TPU:39 before, /device:TPU:6 now
where the time goes in v5:
time: 93.1 us; the launch traced here: 92.7 us
  starting transfers between devices  39.1 us (42%)
  Pallas kernels  28.8 us (31%)
  blocking collectives  15.5 us (17%)
  waiting for transfers between devices  8.42 us (9%)
    all_to_all x1, starting transfers between devices, shards(): lax.all_to_all(parts, 'dp', 0, 0, axis_index_groups=z_groups, tiled=True)  26.1 us
    pallas_call x3, Pallas kernels, kernel(): pl.pallas_call(body, out_shape=outs, in_specs=[SMEM] + [ANY] * (len(opera...  23.8 us
    all_to_all x1, blocking collectives, shards(): lax.all_to_all(packed, 'dp', 0, 0, axis_index_groups=y_groups, tiled=True)  15.5 us
    ppermute x1, starting transfers between devices, shards(): fast_1 = lax.ppermute(sent, 'section', near)  8.12 us
    all_to_all x1, waiting for transfers between devices, shards(): lax.all_to_all(parts, 'dp', 0, 0, axis_index_groups=z_groups, tiled=True)  6 us
    pallas_call x1, Pallas kernels, shards(): pl.pallas_call(functools.partial(final_kernel, columns, rows_each // 2, p...  3.01 us
    ppermute x1, starting transfers between devices, shards(): slow_0 = lax.ppermute(slow, 'section', far)  2.81 us
    ppermute x1, waiting for transfers between devices, shards(): slow_0 = lax.ppermute(slow, 'section', far)  2.41 us
  transfers between devices with their start and end apart: 5, of which 2 were waited for; matrix products, arithmetic and copies ran while one was open for 0% of the time, Pallas kernels for 17%

profile of v5, /device:TPU:6, one launch (start us, length us, event | category | flops | bytes accessed | tf_op | source)
XLA Modules:
  0.0 92.7 jit_solution(4402615445769128777)
XLA Ops:
  0.6 10.0 %shard_map.165 = (f32[128,2048]{1,0:T(8,128)}, f32[128,2048]{1,0:T(8,128)}, f32[64,2048]{1,0:T(8,128)}, f32[64,384]{1,0:T(8,128)}) custom-call(s32[1,2]{1,0:T(1,128)} %plan.5, f32[128,2048]{1,0:T(8,128)} %bitcast.43, f32[128,2048]{1,0:T(8,128)} %bitcast.44, bf16[2,128,2048]{2,1,0:T(8,128)(2,1)} %examples.3, bf16[2,128,2048]{2,1,0:T(8,128)(2,1)} %bitcast.34, ...), custom_call_target="tpu_custom_call" | custom-call | flops 1912602624 | bytes 7659520 | tf_op jit(solution)/shard_map/pallas_call | solution.py:578
  10.6 0.1 collective-permute-start.1
  10.7 2.8 %collective-permute-start = (f32[128,2048]{1,0:T(8,128)}, f32[128,2048]{1,0:T(8,128)}, u32[]{:S(2)}, u32[]{:S(2)}) collective-permute-start(f32[128,2048]{1,0:T(8,128)} %get-tuple-element.24), channel_id=1, source_target_pairs={{16,32},{32,16},{48,64},{64,48},{80,96},{96,80},{112,128},{128,112... | collective-permute-start | bytes 3145736 | tf_op jit(solution)/shard_map/ppermute | solution.py:597
  13.5 1.3 %fill.1.after = f32[8,128]{1,0:T(8,128)} custom-call(f32[1,2048]{1,0:T(1,128)} %rest_6_.1), custom_call_target="tpu_custom_call" | custom-call | tf_op jit(solution)/shard_map/fill/pallas_call | solution.py:600
  14.8 0.0 collective-permute-done.1.arrived.near
  14.9 7.9 %shard_map.166 = (f32[128,2048]{1,0:T(8,128)}, f32[4,320,128]{2,1,0:T(8,128)}, f32[128,128]{1,0:T(8,128)}, bf16[128,2048]{1,0:T(8,128)(2,1)}, f32[128,128]{1,0:T...) custom-call(s32[1,2]{1,0:T(1,128)} %plan.5, ...), custom_call_target="tpu_custom_call" | custom-call | flops 1207959552 | bytes 7659520 | tf_op jit(solution)/shard_map/pallas_call | solution.py:578
  22.8 1.9 %collective-permute-start.2 = (f32[128,2048]{1,0:T(8,128)}, f32[128,2048]{1,0:T(8,128)}, u32[]{:S(2)}, u32[]{:S(2)}) collective-permute-start(f32[128,2048]{1,0:T(8,128)} %get-tuple-element.28.output), channel_id=1, source_target_pairs={{16,32},{32,16},{48,64},{64,48},{80,96},{96,80},{112,128},{128,112... | collective-permute-start | bytes 3145736 | tf_op jit(solution)/shard_map/ppermute | solution.py:619
  24.7 2.4 %collective-permute-done.arrived = f32[128,2048]{1,0:T(8,128)} collective-permute-done((f32[128,2048]{1,0:T(8,128)}, f32[128,2048]{1,0:T(8,128)}, u32[]{:S(2)}, u32[]{:S(2)}) %collective-permute-start) | collective-permute-done | bytes 1048608 | tf_op jit(solution)/shard_map/ppermute | solution.py:597
  27.2 5.9 %shard_map.167 = (f32[128,2048]{1,0:T(8,128)}, f32[4,320,128]{2,1,0:T(8,128)}) custom-call(s32[1,2]{1,0:T(1,128)} %plan.5, f32[128,2048]{1,0:T(8,128)} %collective-permute-done.arrived, f32[128,2048]{1,0:T(8,128)} %collective-permute-done.1.arrived.near, f32[128,2048]{1,0:T(8,128)} %get-tuple-element.28.output, bf16[2,128,2048]{2,1,0:T(8,128)(2,1)} %examples.3, ...), custom_call_target="tpu_custom_call" | custom-call | flops 704643072 | bytes 7659520 | tf_op jit(solution)/shard_map/pallas_call | solution.py:578
  33.0 8.1 %collective-permute-start.3 = (f32[128,2048]{1,0:T(8,128)}, f32[128,2048]{1,0:T(8,128)S(1)}, u32[]{:S(2)}, u32[]{:S(2)}) collective-permute-start(f32[128,2048]{1,0:T(8,128)} %get-tuple-element.39), channel_id=1, source_target_pairs={{0,16},{16,0},{32,48},{48,32},{64,80},{80,64},{96,112},{112,96},{1... | collective-permute-start | bytes 3145736 | tf_op jit(solution)/shard_map/ppermute | solution.py:633
  41.2 15.5 %all_to_all.10.parts = f32[4,320,128]{2,1,0:T(8,128)S(1)} all-to-all(f32[4,320,128]{2,1,0:T(8,128)} %get-tuple-element.36), channel_id=1, replica_groups={{0,1,2,3},{4,5,6,7},{8,9,10,11},{12,13,14,15},{16,17,18,19},{20,21,22,2..., dimensions={0} | all-to-all | bytes 1310720 | tf_op jit(solution)/shard_map/all_to_all | solution.py:632
  56.7 0.7 sum_y.1
  57.4 0.0 collective-permute-done.2.slow
  57.4 26.1 %all-to-all-start.1 = ((f32[4,80,128]{2,1,0:T(8,128)}), f32[4,80,128]{2,1,0:T(8,128)S(1)}, u32[]{:S(2)}, u32[]{:S(2)}) async-start(f32[4,80,128]{2,1,0:T(8,128)} %sum_y.1), calls=%async_computation.1 | async-start | bytes 327680 | tf_op jit(solution)/shard_map/all_to_all | solution.py:643
  83.5 0.0 collective-permute-done.3.fast
  83.5 6.0 %all-to-all-done.1.parts = f32[4,80,128]{2,1,0:T(8,128)S(1)} async-done(((f32[4,80,128]{2,1,0:T(8,128)}), f32[4,80,128]{2,1,0:T(8,128)S(1)}, u32[]{:S(2)}, u32[]{:S(2)}) %all-to-all-start.1) | async-done | bytes 163872 | tf_op jit(solution)/shard_map/all_to_all | solution.py:643
  89.5 3.0 %sum_dp.1 = (f32[64,128]{1,0:T(8,128)}, f32[2,24,32]{2,1,0:T(8,128)}, f32[128,2048]{1,0:T(8,128)}, f32[128,2048]{1,0:T(8,128)}) custom-call(f32[4,80,128]{2,1,0:T(8,128)S(1)} %all-to-all-done.1.parts, f32[128,2048]{1,0:T(8,128)} %collective-permute-done.2.slow, f32[128,2048]{1,0:T(8,128)S(1)} %collective-permute-done.3.fast), custom_call_target="tpu_custom_call" | custom-call | tf_op jit(solution)/shard_map/sum_dp/pallas_call | solution.py:645
Async XLA Ops:
  10.6 4.2 %collective-permute-start.1 = (f32[128,2048]{1,0:T(8,128)}, f32[128,2048]{1,0:T(8,128)}, u32[]{:S(2)}, u32[]{:S(2)}) collective-permute-start(f32[128,2048]{1,0:T(8,128)} %get-tuple-element.25), channel_id=1, source_target_pairs={{0,16},{16,0},{32,48},{48,32},{64,80},{80,64},{96,112},{112,96},{1... | collective-permute-start | bytes 3145736 | tf_op jit(solution)/shard_map/ppermute | solution.py:598
  10.7 16.4 %collective-permute-start = (f32[128,2048]{1,0:T(8,128)}, f32[128,2048]{1,0:T(8,128)}, u32[]{:S(2)}, u32[]{:S(2)}) collective-permute-start(f32[128,2048]{1,0:T(8,128)} %get-tuple-element.24), channel_id=1, source_target_pairs={{16,32},{32,16},{48,64},{64,48},{80,96},{96,80},{112,128},{128,112... | collective-permute-start | bytes 3145736 | tf_op jit(solution)/shard_map/ppermute | solution.py:597
  22.8 34.6 %collective-permute-start.2 = (f32[128,2048]{1,0:T(8,128)}, f32[128,2048]{1,0:T(8,128)}, u32[]{:S(2)}, u32[]{:S(2)}) collective-permute-start(f32[128,2048]{1,0:T(8,128)} %get-tuple-element.28.output), channel_id=1, source_target_pairs={{16,32},{32,16},{48,64},{64,48},{80,96},{96,80},{112,128},{128,112... | collective-permute-start | bytes 3145736 | tf_op jit(solution)/shard_map/ppermute | solution.py:619
  33.0 50.5 %collective-permute-start.3 = (f32[128,2048]{1,0:T(8,128)}, f32[128,2048]{1,0:T(8,128)S(1)}, u32[]{:S(2)}, u32[]{:S(2)}) collective-permute-start(f32[128,2048]{1,0:T(8,128)} %get-tuple-element.39), channel_id=1, source_target_pairs={{0,16},{16,0},{32,48},{48,32},{64,80},{80,64},{96,112},{112,96},{1... | collective-permute-start | bytes 3145736 | tf_op jit(solution)/shard_map/ppermute | solution.py:633
  57.4 32.1 %all-to-all-start.1 = ((f32[4,80,128]{2,1,0:T(8,128)}), f32[4,80,128]{2,1,0:T(8,128)S(1)}, u32[]{:S(2)}, u32[]{:S(2)}) async-start(f32[4,80,128]{2,1,0:T(8,128)} %sum_y.1), calls=%async_computation.1 | async-start | bytes 327680 | tf_op jit(solution)/shard_map/all_to_all | solution.py:643

commit v6 on v5

--- a/solution.py
+++ b/solution.py
@@ -71,11 +71,64 @@
     )
 
 
+class Halves:
+    def __init__(self, copies):
+        self.copies = copies
+
+    def start(self):
+        for copy in self.copies:
+            copy.start()
+
+    def wait(self):
+        for copy in self.copies:
+            copy.wait()
+
+
+def split(source, targets, sems, first, second):
+    half = source.shape[0] // 2
+    return Halves(
+        [
+            pltpu.make_async_copy(source.at[pl.ds(i * half, half)], targets[i], sems.at[k])
+            for i, k in enumerate((first, second))
+        ]
+    )
+
+
+def join(sources, target, sems, first, second):
+    half = target.shape[0] // 2
+    return Halves(
+        [
+            pltpu.make_async_copy(sources[i], target.at[pl.ds(i * half, half)], sems.at[k])
+            for i, k in enumerate((first, second))
+        ]
+    )
+
+
+class Across:
+    def __init__(self, parts, target, sems, first, second):
+        low, high, relayed = parts
+        self.plain = join((low, high), target, sems, first, second)
+        self.middle = join((low, relayed), target, sems, first, second)
+        section = lax.axis_index("section")
+        half = lax.axis_size("section") // 2
+        self.inside = jnp.logical_or(section == half - 1, section == half)
+
+    def start(self):
+        pl.when(self.inside)(self.middle.start)
+        pl.when(jnp.logical_not(self.inside))(self.plain.start)
+
+    def wait(self):
+        pl.when(self.inside)(self.middle.wait)
+        pl.when(jnp.logical_not(self.inside))(self.plain.wait)
+
+
 def fetch(cases, x_s, b_s, r_s, sems):
     moves = []
     for predicates, source, routes in cases:
-        narrow = source.dtype == BF16
-        mine = [pltpu.make_async_copy(source, b_s if narrow else x_s, sems.at[0])]
+        narrow = not isinstance(source, Across) and source.dtype == BF16
+        mine = [source]
+        if not isinstance(source, Across):
+            mine = [pltpu.make_async_copy(source, b_s if narrow else x_s, sems.at[0])]
         if routes is not None:
             mine.append(pltpu.make_async_copy(routes, r_s, sems.at[1]))
         moves.append((predicates, narrow, mine))
@@ -198,7 +251,7 @@
 def first_kernel(
     mean_scale, plan, arriving, returning, examples, stash, fwd_routes_t, bwd_routes_t, *rest
 ):
-    hbm, (slow_o, fast_o, ga_o, gb_o), rest = rest[:7], rest[7:11], rest[11:]
+    hbm, (*slow_o, fast_o, ga_o, gb_o), rest = rest[:7], rest[7:12], rest[12:]
     x_s, x2_s, g_s, y_s, d_s, b_s, b2_s, e_s, r_s, r2_s, ga_s, gb_s, *weights, sems = rest
     odd, even, first, last = position()
     slot = plan[0, 0]
@@ -233,9 +286,9 @@
     copies["down"].wait()
     y_s[...] = output_of(x_s, values, weights[6])
     outs = sems.at[OUT]
-    y_slow = pltpu.make_async_copy(y_s, slow_o, outs.at[0])
+    y_slow = split(y_s, slow_o, outs, 0, 4)
     y_fast = pltpu.make_async_copy(y_s, fast_o, outs.at[0])
-    d_slow = pltpu.make_async_copy(d_s, slow_o, outs.at[1])
+    d_slow = split(d_s, slow_o, outs, 1, 5)
     d_fast = pltpu.make_async_copy(d_s, fast_o, outs.at[1])
     pl.when(odd)(y_slow.start)
     pl.when(even)(y_fast.start)
@@ -285,7 +338,7 @@
 def second_kernel(
     tick, mean_scale, plan, arrived, after, stash, fwd_routes_t, bwd_routes_t, ga_in, gb_in, *rest
 ):
-    hbm, (sent, packed, *saved_o), rest = rest[:7], rest[7:15], rest[15:]
+    hbm, (*sent, packed), saved_o, rest = rest[:7], rest[7:10], rest[10:16], rest[16:]
     x_s, x2_s, y_s, b_s, b2_s, r_s, r2_s, ga_s, gb_s, packed_s, *rest = rest
     saved, weights, sems = rest[:6], rest[6:13], rest[13]
     odd, even, _, last = position()
@@ -313,7 +366,7 @@
     values = primal_of(x_s[...], r_s[...], copies, weights)
     copies["down"].wait()
     outs = sems.at[OUT]
-    y_copy = pltpu.make_async_copy(y_s, sent, outs.at[0])
+    y_copy = split(y_s, sent, sems, 13, 21)
 
     @pl.when(odd)
     def _():
@@ -352,9 +405,12 @@
     tick,
     mean_scale,
     plan,
-    arrived,
+    low,
+    high,
+    relayed,
     near,
-    output,
+    output_low,
+    output_high,
     examples,
     stash,
     fwd_routes_t,
@@ -370,6 +426,7 @@
     odd, even, first, last = position()
     inner = jnp.logical_and(odd, jnp.logical_not(last))
     outs = sems.at[OUT]
+    parts = (low, high, relayed)
     y_copy = pltpu.make_async_copy(y_s, sent, outs.at[0])
     p_copy = pltpu.make_async_copy(packed_s, packed, sems.at[20])
 
@@ -379,7 +436,7 @@
         x_wait = fetch(
             [
                 ((first,), examples.at[tick], mine),
-                ((jnp.logical_not(first),), arrived, mine),
+                ((jnp.logical_not(first),), Across(parts, x_s, sems, 0, 21), mine),
             ],
             x_s,
             b_s,
@@ -399,8 +456,8 @@
 
     @pl.when(odd)
     def _():
-        g_copy = pltpu.make_async_copy(arrived, g_s, sems.at[4])
-        o_copy = pltpu.make_async_copy(output, g_s, sems.at[4])
+        g_copy = Across(parts, g_s, sems, 4, 21)
+        o_copy = join((output_low, output_high), g_s, sems, 4, 21)
         t_copy = pltpu.make_async_copy(examples.at[tick], e_s, sems.at[5])
         pl.when(inner)(g_copy.start)
 
@@ -462,20 +519,43 @@
     total[...] = jnp.sum(parts[...], axis=0).reshape(total.shape)
 
 
-def final_kernel(tall, half, pieces, parts, slow, fast, ga, gb, acts_o, grads_o, slow_s, fast_s, sems):
+class Choice:
+    def __init__(self, refs, rows, target, sem):
+        self.copies = [pltpu.make_async_copy(ref.at[rows], target, sem) for ref in refs]
+        section = lax.axis_index("section")
+        count = lax.axis_size("section")
+        middle = jnp.logical_or(section == count // 2 - 1, section == count // 2)
+        ends = jnp.logical_or(section == 0, section == count - 1)
+        self.inside = jnp.logical_or(middle, ends)
+
+    def start(self):
+        pl.when(self.inside)(self.copies[1].start)
+        pl.when(jnp.logical_not(self.inside))(self.copies[0].start)
+
+    def wait(self):
+        pl.when(self.inside)(self.copies[1].wait)
+        pl.when(jnp.logical_not(self.inside))(self.copies[0].wait)
+
+
+def final_kernel(tall, half, pieces, parts, low, high, relayed, fast, ga, gb, acts_o, grads_o, slow_s, fast_s, sems):
     odd, even, _, _ = position()
-    rows = slow.shape[0] // pieces
+    rows = fast.shape[0] // pieces
     moves = []
-    for source, stage, low, high in (
-        (slow, slow_s, acts_o, grads_o),
+    for source, stage, even_o, odd_o in (
+        (None, slow_s, acts_o, grads_o),
         (fast, fast_s, grads_o, acts_o),
     ):
         for i in range(pieces):
             at = pl.ds(i * rows, rows)
             k = 2 * len(moves)
-            move_in = pltpu.make_async_copy(source.at[at], stage.at[at], sems.at[k])
-            move_even = pltpu.make_async_copy(stage.at[at], low.at[at], sems.at[k + 1])
-            move_odd = pltpu.make_async_copy(stage.at[at], high.at[at], sems.at[k + 1])
+            if source is None:
+                within = pl.ds((i % (pieces // 2)) * rows, rows)
+                refs = (low, low) if i < pieces // 2 else (high, relayed)
+                move_in = Choice(refs, within, stage.at[at], sems.at[k])
+            else:
+                move_in = pltpu.make_async_copy(source.at[at], stage.at[at], sems.at[k])
+            move_even = pltpu.make_async_copy(stage.at[at], even_o.at[at], sems.at[k + 1])
+            move_odd = pltpu.make_async_copy(stage.at[at], odd_o.at[at], sems.at[k + 1])
             moves.append((move_in, move_even, move_odd))
     for move_in, _, _ in moves:
         move_in.start()
@@ -545,14 +625,26 @@
     x_scratch = pltpu.VMEM((tokens, width), F32)
     b_scratch = pltpu.VMEM((tokens, width), BF16)
     r_scratch = pltpu.VMEM((topk, tokens), jnp.int32)
-    semaphores = pltpu.SemaphoreType.DMA((21,))
+    semaphores = pltpu.SemaphoreType.DMA((22,))
     sections = lax.axis_size("section")
     near = swaps(0, sections)
     far = swaps(1, sections)
+    mid = sections // 2 - 1
+    around = [p for p in far if p not in ((mid, mid + 1), (mid + 1, mid))]
+    around += [(mid, 0), (mid + 1, sections - 1)]
+    relays = [(0, mid + 1), (sections - 1, mid)]
+
+    def far_swap(low, high):
+        high = lax.ppermute(high, "section", around)
+        low = lax.ppermute(low, "section", far)
+        relayed = lax.ppermute(high, "section", relays)
+        return low, high, relayed
+
     rows_each = hidden_units // replicas
     size = columns + -(-(rows_each // 2) // 8) * 8
     share_width = width // replicas
     activation = jax.ShapeDtypeStruct((tokens, width), F32)
+    half_activation = jax.ShapeDtypeStruct((tokens // 2, width), F32)
     sums_shape = (
         jax.ShapeDtypeStruct((columns, width), F32),
         jax.ShapeDtypeStruct((columns, hidden_units), F32),
@@ -587,14 +679,14 @@
             ),
         )(*operands)
 
-    slow, fast, *sums = kernel(
+    low, high, fast, *sums = kernel(
         functools.partial(first_kernel, mean_scale),
         3 * primal_flops + 2 * down_flops,
-        (activation, activation, *sums_shape),
+        (half_activation, half_activation, activation, *sums_shape),
         [x_scratch] * 5 + [b_scratch] * 3 + [r_scratch] * 2 + rooms(sums_shape),
         (plan, arriving[0], returning[0], examples, stash, fwd_routes_t, bwd_routes_t, *weights),
     )
-    slow_0 = lax.ppermute(slow, "section", far)
+    slow_0 = far_swap(low, high)
     fast_0 = lax.ppermute(fast, "section", near)
     whole = pltpu.CompilerParams(vmem_limit_bytes=67043328)
     token = pl.pallas_call(
@@ -606,17 +698,18 @@
         compiler_params=whole,
         name="fill",
     )(gain)
-    ahead, packed, *saved = kernel(
+    *ahead, packed, s0, s1, s2, s3, s4, s5 = kernel(
         functools.partial(second_kernel, 1, mean_scale),
         2 * primal_flops + down_flops,
-        (activation, packed_shape, *saved_shape),
+        (half_activation, half_activation, packed_shape, *saved_shape),
         [x_scratch] * 3
         + [b_scratch] * 2
         + [r_scratch] * 2
         + rooms((*sums_shape, packed_shape, *saved_shape)),
         (plan, fast_0, token, stash, fwd_routes_t, bwd_routes_t, *sums, *weights),
     )
-    slow_1 = lax.ppermute(ahead, "section", far)
+    saved = (s0, s1, s2, s3, s4, s5)
+    slow_1 = far_swap(*ahead)
     sent, packed = kernel(
         functools.partial(third_kernel, 1, mean_scale),
         primal_flops + down_flops,
@@ -625,7 +718,7 @@
         + [b_scratch] * 2
         + [r_scratch]
         + rooms((*sums_shape, packed_shape, *saved_shape)),
-        (plan, slow_0, fast_0, ahead, examples, stash, fwd_routes_t, packed, *sums, *saved, *weights),
+        (plan, *slow_0, fast_0, *ahead, examples, stash, fwd_routes_t, packed, *sums, *saved, *weights),
     )
     y_groups = [[z * y_size + y for y in range(y_size)] for z in range(z_size)]
     z_groups = [[z * y_size + y for z in range(z_size)] for y in range(y_size)]
@@ -650,12 +743,12 @@
             activation,
             activation,
         ),
-        in_specs=[VMEM, ANY, ANY],
+        in_specs=[VMEM, ANY, ANY, ANY, ANY],
         out_specs=(VMEM, VMEM, ANY, ANY),
         scratch_shapes=[x_scratch, x_scratch, pltpu.SemaphoreType.DMA((4 * pieces,))],
         compiler_params=pltpu.CompilerParams(vmem_limit_bytes=8 << 20),
         name="sum_dp",
-    )(parts, slow_1, fast_1)
+    )(parts, *slow_1, fast_1)
     return (
         next_acts[None],
         next_grads[None],

time: 93.1 us -> 89.7 us (0.963)
  the two profiles are of different devices: /device:TPU:6 before, /device:TPU:32 now
where the time goes in v6:
time: 89.7 us; the launch traced here: 89.2 us
  starting transfers between devices  28.6 us (32%)
  Pallas kernels  27.6 us (31%)
  waiting for transfers between devices  18.9 us (21%)
  blocking collectives  13.3 us (15%)
    pallas_call x3, Pallas kernels, kernel(): pl.pallas_call(body, out_shape=outs, in_specs=[SMEM] + [ANY] * (len(opera...  23.4 us
    ppermute x2, starting transfers between devices, far_swap(): relayed = lax.ppermute(high, 'section', relays)  19.2 us
    all_to_all x1, blocking collectives, shards(): lax.all_to_all(packed, 'dp', 0, 0, axis_index_groups=y_groups, tiled=True)  13.3 us
    ppermute x2, waiting for transfers between devices, far_swap(): high = lax.ppermute(high, 'section', around)  12.4 us
    all_to_all x1, waiting for transfers between devices, shards(): lax.all_to_all(parts, 'dp', 0, 0, axis_index_groups=z_groups, tiled=True)  5.43 us
    all_to_all x1, starting transfers between devices, shards(): lax.all_to_all(parts, 'dp', 0, 0, axis_index_groups=z_groups, tiled=True)  4.33 us
    ppermute x2, starting transfers between devices, far_swap(): high = lax.ppermute(high, 'section', around)  2.76 us
    pallas_call x1, Pallas kernels, shards(): pl.pallas_call(functools.partial(final_kernel, columns, rows_each // 2, p...  2.21 us
  transfers between devices with their start and end apart: 9, of which 4 were waited for; matrix products, arithmetic and copies ran while one was open for 0% of the time, Pallas kernels for 17%

profile of v6, /device:TPU:32, one launch (start us, length us, event | category | flops | bytes accessed | tf_op | source)
XLA Modules:
  0.0 89.2 jit_solution(17891725268744994945)
XLA Ops:
  0.6 9.8 %shard_map.165 = (f32[64,2048]{1,0:T(8,128)}, f32[64,2048]{1,0:T(8,128)}, f32[128,2048]{1,0:T(8,128)}, f32[64,2048]{1,0:T(8,128)}, f32[64,384]{1,0:T(8,128)}) custom-call(s32[1,2]{1,0:T(1,128)} %plan.5, f32[128,2048]{1,0:T(8,128)} %bitcast.43, f32[128,2048]{1,0:T(8,128)} %bitcast.44, bf16[2,128,2048]{2,1,0:T(8,128)(2,1)} %examples.3, ...), custom_call_target="tpu_custom_call" | custom-call | flops 1912602624 | bytes 7659520 | tf_op jit(solution)/shard_map/pallas_call | solution.py:670
  10.5 0.1 collective-permute-start.3
  10.6 1.3 %collective-permute-start.1 = (f32[64,2048]{1,0:T(8,128)}, f32[64,2048]{1,0:T(8,128)}, u32[]{:S(2)}, u32[]{:S(2)}) collective-permute-start(f32[64,2048]{1,0:T(8,128)} %get-tuple-element.29), channel_id=1, source_target_pairs={{16,32},{32,16},{48,64},{64,48},{80,96},{96,80},{144,160},{160,144... | collective-permute-start | bytes 1572872 | tf_op jit(solution)/shard_map/ppermute | solution.py:638
  11.9 1.5 %collective-permute-start = (f32[64,2048]{1,0:T(8,128)}, f32[64,2048]{1,0:T(8,128)}, u32[]{:S(2)}, u32[]{:S(2)}) collective-permute-start(f32[64,2048]{1,0:T(8,128)} %get-tuple-element.28), channel_id=1, source_target_pairs={{16,32},{32,16},{48,64},{64,48},{80,96},{96,80},{112,128},{128,112... | collective-permute-start | bytes 1572872 | tf_op jit(solution)/shard_map/ppermute | solution.py:639
  13.3 9.3 %collective-permute-done.1.high = f32[64,2048]{1,0:T(8,128)} collective-permute-done((f32[64,2048]{1,0:T(8,128)}, f32[64,2048]{1,0:T(8,128)}, u32[]{:S(2)}, u32[]{:S(2)}) %collective-permute-start.1) | collective-permute-done | bytes 524320 | tf_op jit(solution)/shard_map/ppermute | solution.py:638
  22.6 8.8 %collective-permute-start.2 = (f32[64,2048]{1,0:T(8,128)}, f32[64,2048]{1,0:T(8,128)}, u32[]{:S(2)}, u32[]{:S(2)}) collective-permute-start(f32[64,2048]{1,0:T(8,128)} %collective-permute-done.1.high), channel_id=1, source_target_pairs={{0,128},{240,112},{1,129},{241,113},{2,130},{242,114},{3,131},{243... | collective-permute-start | bytes 1572872 | tf_op jit(solution)/shard_map/ppermute | solution.py:640
  31.4 1.3 %fill.1.after = f32[8,128]{1,0:T(8,128)} custom-call(f32[1,2048]{1,0:T(1,128)} %rest_6_.1), custom_call_target="tpu_custom_call" | custom-call | tf_op jit(solution)/shard_map/fill/pallas_call | solution.py:692
  32.8 0.0 collective-permute-done.3.arrived.near
  32.8 8.0 %shard_map.166 = (f32[64,2048]{1,0:T(8,128)}, f32[64,2048]{1,0:T(8,128)}, f32[4,320,128]{2,1,0:T(8,128)}, f32[128,128]{1,0:T(8,128)}, bf16[128,2048]{1,0:T(8,128...) custom-call(s32[1,2]{1,0:T(1,128)} %plan.5, ...), custom_call_target="tpu_custom_call" | custom-call | flops 1207959552 | bytes 7659520 | tf_op jit(solution)/shard_map/pallas_call | solution.py:670
  40.7 1.5 %collective-permute-start.5 = (f32[64,2048]{1,0:T(8,128)}, f32[64,2048]{1,0:T(8,128)}, u32[]{:S(2)}, u32[]{:S(2)}) collective-permute-start(f32[64,2048]{1,0:T(8,128)} %get-tuple-element.34.output_high), channel_id=1, source_target_pairs={{16,32},{32,16},{48,64},{64,48},{80,96},{96,80},{144,160},{160,144... | collective-permute-start | bytes 1572872 | tf_op jit(solution)/shard_map/ppermute | solution.py:638
  42.2 0.0 collective-permute-done.low
  42.2 1.0 %collective-permute-done.2.relayed = f32[64,2048]{1,0:T(8,128)} collective-permute-done((f32[64,2048]{1,0:T(8,128)}, f32[64,2048]{1,0:T(8,128)}, u32[]{:S(2)}, u32[]{:S(2)}) %collective-permute-start.2) | collective-permute-done | bytes 524320 | tf_op jit(solution)/shard_map/ppermute | solution.py:640
  43.3 5.6 %shard_map.167 = (f32[128,2048]{1,0:T(8,128)}, f32[4,320,128]{2,1,0:T(8,128)}) custom-call(s32[1,2]{1,0:T(1,128)} %plan.5, f32[64,2048]{1,0:T(8,128)} %collective-permute-done.low, f32[64,2048]{1,0:T(8,128)} %collective-permute-done.1.high, f32[64,2048]{1,0:T(8,128)} %collective-permute-done.2.relayed, f32[128,2048]{1,0:T(8,128)} %collective-permute-done.3.arrived.near, ...), custom_call_target="tpu_custom_call" | custom-call | flops 704643072 | bytes 7659520 | tf_op jit(solution)/shard_map/pallas_call | solution.py:670
  48.8 0.1 collective-permute-start.7
  48.9 0.7 collective-permute-start.4
  49.7 3.1 %collective-permute-done.5.high = f32[64,2048]{1,0:T(8,128)} collective-permute-done((f32[64,2048]{1,0:T(8,128)}, f32[64,2048]{1,0:T(8,128)}, u32[]{:S(2)}, u32[]{:S(2)}) %collective-permute-start.5) | collective-permute-done | bytes 524320 | tf_op jit(solution)/shard_map/ppermute | solution.py:638
  52.8 10.3 %collective-permute-start.6 = (f32[64,2048]{1,0:T(8,128)}, f32[64,2048]{1,0:T(8,128)S(1)}, u32[]{:S(2)}, u32[]{:S(2)}) collective-permute-start(f32[64,2048]{1,0:T(8,128)} %collective-permute-done.5.high), channel_id=1, source_target_pairs={{0,128},{240,112},{1,129},{241,113},{2,130},{242,114},{3,131},{243... | collective-permute-start | bytes 1572872 | tf_op jit(solution)/shard_map/ppermute | solution.py:640
  63.1 13.3 %all_to_all.10.parts = f32[4,320,128]{2,1,0:T(8,128)S(1)} all-to-all(f32[4,320,128]{2,1,0:T(8,128)} %get-tuple-element.42), channel_id=1, replica_groups={{0,1,2,3},{4,5,6,7},{8,9,10,11},{12,13,14,15},{16,17,18,19},{20,21,22,2..., dimensions={0} | all-to-all | bytes 1310720 | tf_op jit(solution)/shard_map/all_to_all | solution.py:725
  76.4 0.7 sum_y.1
  77.1 0.0 collective-permute-done.4.low
  77.1 0.0 collective-permute-done.6.relayed
  77.1 4.3 %all-to-all-start.1 = ((f32[4,80,128]{2,1,0:T(8,128)}), f32[4,80,128]{2,1,0:T(8,128)S(1)}, u32[]{:S(2)}, u32[]{:S(2)}) async-start(f32[4,80,128]{2,1,0:T(8,128)} %sum_y.1), calls=%async_computation.1 | async-start | bytes 327680 | tf_op jit(solution)/shard_map/all_to_all | solution.py:736
  81.4 0.0 collective-permute-done.7.fast
  81.4 5.4 %all-to-all-done.1.parts = f32[4,80,128]{2,1,0:T(8,128)S(1)} async-done(((f32[4,80,128]{2,1,0:T(8,128)}), f32[4,80,128]{2,1,0:T(8,128)S(1)}, u32[]{:S(2)}, u32[]{:S(2)}) %all-to-all-start.1) | async-done | bytes 163872 | tf_op jit(solution)/shard_map/all_to_all | solution.py:736
  86.8 2.2 %sum_dp.1 = (f32[64,128]{1,0:T(8,128)}, f32[2,24,32]{2,1,0:T(8,128)}, f32[128,2048]{1,0:T(8,128)}, f32[128,2048]{1,0:T(8,128)}) custom-call(f32[4,80,128]{2,1,0:T(8,128)S(1)} %all-to-all-done.1.parts, f32[64,2048]{1,0:T(8,128)S(1)} %collective-permute-done.4.low, f32[64,2048]{1,0:T(8,128)} %collective-permute-done.5.high, ...), custom_call_target="tpu_custom_call" | custom-call | tf_op jit(solution)/shard_map/sum_dp/pallas_call | solution.py:738
Async XLA Ops:
  10.5 22.3 %collective-permute-start.3 = (f32[128,2048]{1,0:T(8,128)}, f32[128,2048]{1,0:T(8,128)}, u32[]{:S(2)}, u32[]{:S(2)}) collective-permute-start(f32[128,2048]{1,0:T(8,128)} %get-tuple-element.30), channel_id=1, source_target_pairs={{0,16},{16,0},{32,48},{48,32},{64,80},{80,64},{96,112},{112,96},{1... | collective-permute-start | bytes 3145736 | tf_op jit(solution)/shard_map/ppermute | solution.py:690
  10.6 12.0 %collective-permute-start.1 = (f32[64,2048]{1,0:T(8,128)}, f32[64,2048]{1,0:T(8,128)}, u32[]{:S(2)}, u32[]{:S(2)}) collective-permute-start(f32[64,2048]{1,0:T(8,128)} %get-tuple-element.29), channel_id=1, source_target_pairs={{16,32},{32,16},{48,64},{64,48},{80,96},{96,80},{144,160},{160,144... | collective-permute-start | bytes 1572872 | tf_op jit(solution)/shard_map/ppermute | solution.py:638
  11.9 30.4 %collective-permute-start = (f32[64,2048]{1,0:T(8,128)}, f32[64,2048]{1,0:T(8,128)}, u32[]{:S(2)}, u32[]{:S(2)}) collective-permute-start(f32[64,2048]{1,0:T(8,128)} %get-tuple-element.28), channel_id=1, source_target_pairs={{16,32},{32,16},{48,64},{64,48},{80,96},{96,80},{112,128},{128,112... | collective-permute-start | bytes 1572872 | tf_op jit(solution)/shard_map/ppermute | solution.py:639
  22.6 20.7 %collective-permute-start.2 = (f32[64,2048]{1,0:T(8,128)}, f32[64,2048]{1,0:T(8,128)}, u32[]{:S(2)}, u32[]{:S(2)}) collective-permute-start(f32[64,2048]{1,0:T(8,128)} %collective-permute-done.1.high), channel_id=1, source_target_pairs={{0,128},{240,112},{1,129},{241,113},{2,130},{242,114},{3,131},{243... | collective-permute-start | bytes 1572872 | tf_op jit(solution)/shard_map/ppermute | solution.py:640
  40.7 12.0 %collective-permute-start.5 = (f32[64,2048]{1,0:T(8,128)}, f32[64,2048]{1,0:T(8,128)}, u32[]{:S(2)}, u32[]{:S(2)}) collective-permute-start(f32[64,2048]{1,0:T(8,128)} %get-tuple-element.34.output_high), channel_id=1, source_target_pairs={{16,32},{32,16},{48,64},{64,48},{80,96},{96,80},{144,160},{160,144... | collective-permute-start | bytes 1572872 | tf_op jit(solution)/shard_map/ppermute | solution.py:638
  48.8 32.6 %collective-permute-start.7 = (f32[128,2048]{1,0:T(8,128)}, f32[128,2048]{1,0:T(8,128)S(1)}, u32[]{:S(2)}, u32[]{:S(2)}) collective-permute-start(f32[128,2048]{1,0:T(8,128)} %get-tuple-element.47), channel_id=1, source_target_pairs={{0,16},{16,0},{32,48},{48,32},{64,80},{80,64},{96,112},{112,96},{1... | collective-permute-start | bytes 3145736 | tf_op jit(solution)/shard_map/ppermute | solution.py:726
  48.9 28.1 %collective-permute-start.4 = (f32[64,2048]{1,0:T(8,128)}, f32[64,2048]{1,0:T(8,128)S(1)}, u32[]{:S(2)}, u32[]{:S(2)}) collective-permute-start(f32[64,2048]{1,0:T(8,128)} %get-tuple-element.33.output_low), channel_id=1, source_target_pairs={{16,32},{32,16},{48,64},{64,48},{80,96},{96,80},{112,128},{128,112... | collective-permute-start | bytes 1572872 | tf_op jit(solution)/shard_map/ppermute | solution.py:639
  52.8 24.3 %collective-permute-start.6 = (f32[64,2048]{1,0:T(8,128)}, f32[64,2048]{1,0:T(8,128)S(1)}, u32[]{:S(2)}, u32[]{:S(2)}) collective-permute-start(f32[64,2048]{1,0:T(8,128)} %collective-permute-done.5.high), channel_id=1, source_target_pairs={{0,128},{240,112},{1,129},{241,113},{2,130},{242,114},{3,131},{243... | collective-permute-start | bytes 1572872 | tf_op jit(solution)/shard_map/ppermute | solution.py:640
  77.1 9.8 %all-to-all-start.1 = ((f32[4,80,128]{2,1,0:T(8,128)}), f32[4,80,128]{2,1,0:T(8,128)S(1)}, u32[]{:S(2)}, u32[]{:S(2)}) async-start(f32[4,80,128]{2,1,0:T(8,128)} %sum_y.1), calls=%async_computation.1 | async-start | bytes 327680 | tf_op jit(solution)/shard_map/all_to_all | solution.py:736
